TPU v7x, 512 devices: a whole 4x4x16 slice. The times are simulated.
512 devices in a mesh: conv: 8 (over y, core), seq: 8 (over z_lo), tensor: 8 (over z_hi, x).
Axes of the slice: x: 4, y: 4, z: 16 (z_hi: 2, z_lo: 8; z = z_hi * 8 + z_lo), core: 2. Of those that a mesh axis runs over, the one named last changes fastest.
Arguments:
- queries: bfloat16 [8, 1024, 4096], P('conv', 'seq', 'tensor'), may hold values from -6 to 6
- keys: bfloat16 [16, 1664, 1024], P('conv', ('seq', 'tensor')), may hold values from -6 to 6
- values: bfloat16 [16, 1664, 1024], P('conv', ('seq', 'tensor')), may hold values from -18 to 18
- q_gain: float32 [128], replicated, may hold values from 0.9 to 2.2
- k_gain: float32 [128], replicated, may hold values from 0.9 to 2.2
- gate: float32 [1], replicated, may hold values from 0.4 to 1.6
- tile_count: int32 [8], replicated, may hold values from 1 to 2, as said below
- tile_owner: int32 [8, 2], replicated, may hold values from -1 to 7, as said below
- visible: int32 [8, 1024], replicated, may hold values from 0 to 2, as said below
- d_out: bfloat16 [8, 1024, 4096], P('conv', 'seq', 'tensor'), may hold values from -12 to 12
Outputs:
- attended: bfloat16 [8, 1024, 4096], P('conv', 'seq', 'tensor')
- d_queries: bfloat16 [8, 1024, 4096], P('conv', 'seq', 'tensor')
- d_keys: bfloat16 [16, 1664, 1024], P('conv', ('seq', 'tensor'))
- d_values: bfloat16 [16, 1664, 1024], P('conv', ('seq', 'tensor'))
Inputs may be any that keep to these rules, and one draw needn't show every extreme that they name: `tile_count`: some conversation has 2 tiles. `tile_owner`: entries with t at or past the conversation's count are -1. The tiles of one conversation have different owners, no two tiles share a slot, and some conv index holds 2 tiles. `visible`: never falls along a conversation's text; it is 0 at the first token and 2 at the last.
All inputs are finite; a program needn't handle non-finite values.
Results may differ from a plain program's by a relative error of at most 0.02.
Values may be sent and summed in bfloat16 or wider, within the bound.
No kernel may reach another device: no remote copies, remote signals or barrier semaphores. Data moves between devices by JAX's collectives and lax.ppermute only.
A program may use at most 64 MiB of HBM per device.

v0:
```python
from functools import partial
import math

import jax
import jax.numpy as jnp
from jax import lax
from jax.sharding import PartitionSpec as P

TILE = 1601


EPSILON = 1e-05


def cut_along(value, dim, length):
    before, after = (value.shape[:dim], value.shape[dim + 1 :])
    return jnp.moveaxis(value.reshape(*before, length, -1, *after), dim, 0)


def laid_out(tiles, dim):
    tiles = jnp.moveaxis(tiles, 0, dim)
    lengths = tiles.shape
    return tiles.reshape(*lengths[:dim], lengths[dim] * lengths[dim + 1], *lengths[dim + 2 :])


def one_exchange(value, axis, axes, splits, concats):
    sizes = [lax.axis_size(a) for a in axes]
    tiles = cut_along(value, splits[0], sizes[0])
    tiles = jnp.moveaxis(cut_along(tiles, splits[1] + 1, sizes[1]), 0, 1)
    inside = tiles.shape[2:]
    tiles = tiles.reshape(-1, *inside)
    tiles = lax.all_to_all(tiles, axis, split_axis=0, concat_axis=0, tiled=True)
    tiles = laid_out(tiles.reshape(*sizes, *inside), concats[0] + 1)
    return laid_out(tiles, concats[1])


def sent_to_all(value, axis):
    copies = jnp.broadcast_to(value, (lax.axis_size(axis), *value.shape))
    return lax.all_to_all(copies, axis, split_axis=0, concat_axis=0, tiled=True)


def gathered_copies(value, axis, dim):
    return laid_out(sent_to_all(value, axis), dim)


def in_one_piece(arrays, axis, dim, along):
    ends, at = ([], 0)
    for a in arrays[:-1]:
        at += a.shape[along]
        ends.append(at)
    both = jnp.concatenate(arrays, axis=along)
    return tuple(jnp.split(gathered_copies(both, axis, dim), ends, axis=along))


def sum_at_owner(value, axis, dim):
    tiles = cut_along(value, dim, lax.axis_size(axis))
    arrived = lax.all_to_all(tiles, axis, split_axis=0, concat_axis=0, tiled=True)
    return arrived.astype(jnp.float32).sum(axis=0)


def sent_together(arrays, axis, dim, along):
    both = jnp.concatenate(arrays, axis=along)
    filled, at, finished = (sum_at_owner(both, axis, dim), 0, [])
    for a in arrays:
        finished.append(lax.slice_in_dim(filled, at, at + a.shape[along], axis=along))
        at += a.shape[along]
    return tuple(finished)


def head_norm(inputs, norm_gain):
    mean_square = jnp.mean(inputs * inputs, axis=-1, keepdims=True)
    return inputs * lax.rsqrt(mean_square + EPSILON) * norm_gain


def key_mask(seen_tiles, tile_index, row_start, row_count):
    row_ids = row_start + jnp.arange(row_count, dtype=jnp.int32)
    return (seen_tiles > tile_index)[:, None] & (row_ids < TILE)[None, :]


def tile_weights(query_bf, key_tile, visible_keys, score_scale):
    scores = (
        jnp.einsum("pkgd,rkd->kgpr", query_bf, key_tile, preferred_element_type=jnp.float32)
        * score_scale
    )
    return jnp.where(visible_keys[None, None], jnp.exp(scores), 0.0)


def tile_forward(query_bf, key_tile, value_tile, visible_keys, score_scale):
    weights = tile_weights(query_bf, key_tile, visible_keys, score_scale)
    weighted = jnp.einsum(
        "kgpr,rkd->pkgd",
        weights.astype(jnp.bfloat16),
        value_tile,
        preferred_element_type=jnp.float32,
    )
    return (jnp.sum(weights, axis=-1), weighted)


def tile_gradients(
    query_bf,
    grad_bf,
    key_tile,
    value_tile,
    visible_keys,
    safe_sum,
    row_delta,
    score_scale,
    block_count,
):
    weights = tile_weights(query_bf, key_tile, visible_keys, score_scale)
    probability = weights / safe_sum[..., None]
    grad_prob = jnp.einsum(
        "pkgd,rkd->kgpr", grad_bf, value_tile, preferred_element_type=jnp.float32
    )
    grad_score = (probability * (grad_prob - row_delta[..., None])).astype(jnp.bfloat16)
    prob_bf = probability.astype(jnp.bfloat16)
    grad_query = (
        jnp.einsum("kgpr,rkd->pkgd", grad_score, key_tile, preferred_element_type=jnp.float32)
        * score_scale
    )
    kv_local, group_size, token_count, row_count = grad_score.shape
    head_size = query_bf.shape[-1]
    block_tokens = token_count // block_count
    score_blocks = grad_score.reshape(kv_local, group_size, block_count, block_tokens, row_count)
    prob_blocks = prob_bf.reshape(kv_local, group_size, block_count, block_tokens, row_count)
    query_blocks = query_bf.reshape(block_count, block_tokens, kv_local, group_size, head_size)
    grad_blocks = grad_bf.reshape(block_count, block_tokens, kv_local, group_size, head_size)
    key_part = (
        jnp.einsum(
            "kgbpr,bpkgd->brkd", score_blocks, query_blocks, preferred_element_type=jnp.float32
        )
        * score_scale
    )
    value_part = jnp.einsum(
        "kgbpr,bpkgd->brkd", prob_blocks, grad_blocks, preferred_element_type=jnp.float32
    )
    key_part = key_part[0]
    value_part = value_part[0]
    return (
        grad_query,
        key_part.reshape(row_count, kv_local * head_size),
        value_part.reshape(row_count, kv_local * head_size),
    )


def attend_forward(query_bf, tile_keys, tile_values, seen_tiles, row_start, score_scale):
    row_count, slot_count, features = tile_keys.shape
    token_count, kv_local, group_size, head_size = query_bf.shape
    weight_sum = jnp.zeros((kv_local, group_size, token_count), jnp.float32)
    weighted = jnp.zeros(query_bf.shape, jnp.float32)
    for tile_index in range(slot_count):
        key_tile = tile_keys[:, tile_index].reshape(row_count, kv_local, head_size)
        value_tile = tile_values[:, tile_index].reshape(row_count, kv_local, head_size)
        visible_keys = key_mask(seen_tiles, tile_index, row_start, row_count)
        work = partial(tile_forward, query_bf, key_tile, value_tile, visible_keys, score_scale)
        part_sum, part_weighted = lax.cond(
            jnp.any(visible_keys),
            work,
            lambda: (jnp.zeros_like(weight_sum), jnp.zeros_like(weighted)),
        )
        weight_sum = weight_sum + part_sum
        weighted = weighted + part_weighted
    return (weight_sum, weighted)


def attend_backward(
    query_bf,
    grad_bf,
    tile_keys,
    tile_values,
    seen_tiles,
    row_start,
    safe_sum,
    row_delta,
    score_scale,
    block_tokens,
):
    row_count, slot_count, features = tile_keys.shape
    token_count, kv_local, group_size, head_size = query_bf.shape
    block_count = token_count // block_tokens
    grad_query = jnp.zeros(query_bf.shape, jnp.float32)
    key_parts = []
    value_parts = []
    for tile_index in range(slot_count):
        key_tile = tile_keys[:, tile_index].reshape(row_count, kv_local, head_size)
        value_tile = tile_values[:, tile_index].reshape(row_count, kv_local, head_size)
        visible_keys = key_mask(seen_tiles, tile_index, row_start, row_count)
        work = partial(
            tile_gradients,
            query_bf,
            grad_bf,
            key_tile,
            value_tile,
            visible_keys,
            safe_sum,
            row_delta,
            score_scale,
            block_count,
        )
        zero_parts = (
            jnp.zeros(query_bf.shape, jnp.float32),
            jnp.zeros((row_count, features), jnp.float32),
            jnp.zeros((row_count, features), jnp.float32),
        )
        part_query, key_part, value_part = lax.cond(jnp.any(visible_keys), work, lambda: zero_parts)
        grad_query = grad_query + part_query
        key_parts.append(key_part)
        value_parts.append(value_part)
    return (grad_query, jnp.stack(key_parts, axis=1), jnp.stack(value_parts, axis=1))


def shards(queries, keys, values, q_gain, k_gain, gate, tile_count, tile_owner, visible, d_out):
    conv_count = lax.axis_size("conv")
    tensor_count = lax.axis_size("tensor")
    conv_index = lax.axis_index("conv")
    sequence_index = lax.axis_index("seq")
    slot_count, row_local, features = keys.shape
    head_size = q_gain.shape[0]
    kv_heads = features // head_size
    kv_local = kv_heads // tensor_count
    token_count = queries.shape[1]
    query_heads = queries.shape[2] // head_size
    group_size = query_heads // kv_local
    score_scale = 1.0 / math.sqrt(head_size)
    gate_value = jnp.tanh(gate[0])
    conv_ids = jnp.arange(conv_count, dtype=jnp.int32)
    transfers = (tile_owner == conv_index).astype(jnp.bfloat16)
    own_owners = lax.dynamic_index_in_dim(tile_owner, conv_index, 0, keepdims=False)
    takes = (own_owners[:, None] == conv_ids[None, :]).astype(jnp.bfloat16)
    own_count = lax.dynamic_index_in_dim(tile_count, conv_index, 0, keepdims=False)
    seen_all = jnp.minimum(
        lax.dynamic_index_in_dim(visible, conv_index, 0, keepdims=False), own_count
    )
    key_raw = keys.astype(jnp.float32).reshape(slot_count, row_local, kv_heads, head_size)
    key_normed, key_back = jax.vjp(lambda inputs: head_norm(inputs, k_gain), key_raw)
    key_halfprec = key_normed.astype(jnp.bfloat16).reshape(slot_count, row_local, features)
    outgoing_keys = jnp.einsum(
        "wn,nki->wki", transfers, key_halfprec, preferred_element_type=jnp.float32
    ).astype(jnp.bfloat16)
    send_values = jnp.einsum(
        "wn,nki->wki", transfers, values, preferred_element_type=jnp.float32
    ).astype(jnp.bfloat16)
    got_keys, got_values = (
        one_exchange(outgoing_keys, ("conv", "tensor"), ("conv", "tensor"), (0, 2), (0, 1)),
        one_exchange(send_values, ("conv", "tensor"), ("conv", "tensor"), (0, 2), (0, 1)),
    )
    tile_keys = jnp.einsum(
        "to,orf->rtf", takes, got_keys, preferred_element_type=jnp.float32
    ).astype(jnp.bfloat16)
    tile_values = jnp.einsum(
        "to,orf->rtf", takes, got_values, preferred_element_type=jnp.float32
    ).astype(jnp.bfloat16)
    query_raw = queries[0].astype(jnp.float32).reshape(token_count, query_heads, head_size)
    query_normed, query_back = jax.vjp(lambda inputs: head_norm(inputs, q_gain), query_raw)
    query_bf = query_normed.astype(jnp.bfloat16).reshape(
        token_count, kv_local, group_size, head_size
    )
    grad_bf = (
        (gate_value * d_out[0].astype(jnp.float32))
        .astype(jnp.bfloat16)
        .reshape(token_count, kv_local, group_size, head_size)
    )
    own_start = sequence_index * token_count
    full_keys, full_values = in_one_piece((tile_keys, tile_values), "seq", 0, 1)
    seen_own = lax.dynamic_slice_in_dim(seen_all, own_start, token_count)
    weight_sum, weighted = attend_forward(
        query_bf, full_keys, full_values, seen_own, 0, score_scale
    )
    safe_sum = jnp.where(weight_sum > 0, weight_sum, 1.0)
    context = weighted / jnp.transpose(safe_sum, (2, 0, 1))[..., None]
    row_delta = jnp.transpose(jnp.sum(grad_bf.astype(jnp.float32) * context, axis=-1), (1, 2, 0))
    grad_query, key_parts, value_parts = attend_backward(
        query_bf,
        grad_bf,
        full_keys,
        full_values,
        seen_own,
        0,
        safe_sum,
        row_delta,
        score_scale,
        token_count,
    )
    key_sums, value_sums = sent_together(
        (key_parts.astype(jnp.bfloat16), value_parts.astype(jnp.bfloat16)), "seq", 0, 1
    )
    attended = (
        (gate_value * context).astype(jnp.bfloat16).reshape(1, token_count, query_heads * head_size)
    )
    key_round = key_sums.astype(jnp.bfloat16)
    value_round = value_sums.astype(jnp.bfloat16)
    back_keys = jnp.einsum(
        "to,rtf->orf", takes, key_round, preferred_element_type=jnp.float32
    ).astype(jnp.bfloat16)
    back_values = jnp.einsum(
        "to,rtf->orf", takes, value_round, preferred_element_type=jnp.float32
    ).astype(jnp.bfloat16)
    returned_keys, returned_values = (
        one_exchange(back_keys, ("conv", "tensor"), ("conv", "tensor"), (0, 1), (0, 2)),
        one_exchange(back_values, ("conv", "tensor"), ("conv", "tensor"), (0, 1), (0, 2)),
    )
    positioned_keys = jnp.einsum(
        "ew,eig->wig", transfers, returned_keys, preferred_element_type=jnp.float32
    )
    d_values = jnp.einsum(
        "ew,eig->wig", transfers, returned_values, preferred_element_type=jnp.float32
    ).astype(jnp.bfloat16)
    d_keys = key_back(positioned_keys.reshape(slot_count, row_local, kv_heads, head_size))[0]
    d_keys = d_keys.astype(jnp.bfloat16).reshape(slot_count, row_local, features)
    d_queries = query_back(grad_query.reshape(token_count, query_heads, head_size))[0]
    d_queries = d_queries.astype(jnp.bfloat16).reshape(1, token_count, query_heads * head_size)
    return (attended, d_queries, d_keys, d_values)


def solution(mesh):
    in_specs = (
        P("conv", "seq", "tensor"),
        P("conv", ("seq", "tensor"), None),
        P("conv", ("seq", "tensor"), None),
        P(),
        P(),
        P(),
        P(),
        P(),
        P(),
        P("conv", "seq", "tensor"),
    )
    out_specs = (
        P("conv", "seq", "tensor"),
        P("conv", "seq", "tensor"),
        P("conv", ("seq", "tensor"), None),
        P("conv", ("seq", "tensor"), None),
    )
    return jax.shard_map(shards, mesh=mesh, in_specs=in_specs, out_specs=out_specs, check_vma=False)
```

profile of v0, /device:TPU:1, one launch (start us, length us, event | category | flops | bytes accessed | tf_op | source)
XLA Modules:
  0.0 354.8 jit_solution(10101725041499599781)
XLA Ops:
  1.3 1.2 multiply_reduce_fusion.3
  3.5 1.5 fusion.48
  5.1 1.1 copy.250
  6.2 22.2 %all-to-all-start = ((bf16[64,1,26,128]{3,2,1,0:T(8,128)(2,1)}), bf16[64,1,26,128]{3,2,1,0:T(8,128)(2,1)S(1)}, u32[]{:S(2)}, u32[]{:S(2)}) async-start(bf16[64,1,26,128]{3,2,1,0:T(8,128)(2,1)} %copy.250), calls=%async_computation | async-start | bytes 1048576 | tf_op jit(solution)/shard_map/all_to_all | solution.py:32
  28.8 1.1 copy.254
  29.9 20.2 %all-to-all-done = bf16[64,1,26,128]{3,2,1,0:T(8,128)(2,1)S(1)} async-done(((bf16[64,1,26,128]{3,2,1,0:T(8,128)(2,1)}), bf16[64,1,26,128]{3,2,1,0:T(8,128)(2,1)S(1)}, u32[]{:S(2)}, u32[]{:S(2)}) %all-to-all-start) | async-done | bytes 426016 | tf_op jit(solution)/shard_map/all_to_all | solution.py:32
  50.1 4.6 %all-to-all-start.1 = ((bf16[64,1,26,128]{3,2,1,0:T(8,128)(2,1)}), bf16[64,1,26,128]{3,2,1,0:T(8,128)(2,1)S(1)}, u32[]{:S(2)}, u32[]{:S(2)}) async-start(bf16[64,1,26,128]{3,2,1,0:T(8,128)(2,1)} %copy.254), calls=%async_computation.1 | async-start | bytes 1048576 | tf_op jit(solution)/shard_map/all_to_all | solution.py:32
  55.2 20.7 %all-to-all-done.1 = bf16[64,1,26,128]{3,2,1,0:T(8,128)(2,1)S(1)} async-done(((bf16[64,1,26,128]{3,2,1,0:T(8,128)(2,1)}), bf16[64,1,26,128]{3,2,1,0:T(8,128)(2,1)S(1)}, u32[]{:S(2)}, u32[]{:S(2)}) %all-to-all-start.1) | async-done | bytes 426016 | tf_op jit(solution)/shard_map/all_to_all | solution.py:32
  77.1 1.4 broadcast_in_dim.74
  78.6 27.6 %all-to-all-start.2 = ((bf16[8,208,4,128]{3,1,2,0:T(8,128)(2,1)}), bf16[8,208,4,128]{3,1,2,0:T(8,128)(2,1)S(1)}, u32[]{:S(2)}, u32[]{:S(2)}) async-start(bf16[8,208,4,128]{3,1,2,0:T(8,128)(2,1)} %broadcast_in_dim.74), calls=%async_computation.2 | async-start | bytes 3407872 | tf_op jit(solution)/shard_map/all_to_all | solution.py:39
  108.1 1.4 compare_bitcast_fusion.1
  109.5 1.6 fusion.82
  112.7 0.8 fusion.57
  113.5 71.2 %all-to-all-done.2 = bf16[8,208,4,128]{3,1,2,0:T(8,128)(2,1)S(1)} async-done(((bf16[8,208,4,128]{3,1,2,0:T(8,128)(2,1)}), bf16[8,208,4,128]{3,1,2,0:T(8,128)(2,1)S(1)}, u32[]{:S(2)}, u32[]{:S(2)}) %all-to-all-start.2) | async-done | bytes 1703968 | tf_op jit(solution)/shard_map/all_to_all | solution.py:39
  187.7 97.5 %all_to_all.30 = bf16[8,208,4,128]{3,1,2,0:T(8,128)(2,1)S(1)} all-to-all(bf16[8,208,4,128]{3,1,2,0:T(8,128)(2,1)S(1)} %pad_maximum_fusion), channel_id=1, replica_groups=mesh['conv'=8,'seq'=8,'tensor'=8] {'seq'}, dimensions={0} | all-to-all | bytes 3407872 | tf_op jit(solution)/shard_map/all_to_all | solution.py:57
  286.0 0.9 reshape_transpose_transpose_reshape_reshape.7
  286.9 6.2 %all-to-all-start.5 = ((bf16[64,1,26,128]{3,2,1,0:T(8,128)(2,1)}), bf16[64,1,26,128]{3,2,1,0:T(8,128)(2,1)S(1)}, u32[]{:S(2)}, u32[]{:S(2)}) async-start(bf16[64,1,26,128]{3,2,1,0:T(8,128)(2,1)} %bitcast.134), calls=%async_computation.5 | async-start | bytes 1048576 | tf_op jit(solution)/shard_map/all_to_all | solution.py:32
  293.6 0.9 reshape_transpose_transpose_reshape_reshape.6
  294.5 26.7 %all-to-all-done.5 = bf16[64,1,26,128]{3,2,1,0:T(8,128)(2,1)S(1)} async-done(((bf16[64,1,26,128]{3,2,1,0:T(8,128)(2,1)}), bf16[64,1,26,128]{3,2,1,0:T(8,128)(2,1)S(1)}, u32[]{:S(2)}, u32[]{:S(2)}) %all-to-all-start.5) | async-done | bytes 426016 | tf_op jit(solution)/shard_map/all_to_all | solution.py:32
  321.3 4.6 %all-to-all-start.4 = ((bf16[64,1,26,128]{3,2,1,0:T(8,128)(2,1)}), bf16[64,1,26,128]{3,2,1,0:T(8,128)(2,1)S(1)}, u32[]{:S(2)}, u32[]{:S(2)}) async-start(bf16[64,1,26,128]{3,2,1,0:T(8,128)(2,1)} %bitcast.126), calls=%async_computation.4 | async-start | bytes 1048576 | tf_op jit(solution)/shard_map/all_to_all | solution.py:32
  326.3 0.8 copy.288
  329.2 0.9 convolution_convert_fusion.4
  330.1 22.4 %all-to-all-done.4 = bf16[64,1,26,128]{3,2,1,0:T(8,128)(2,1)S(1)} async-done(((bf16[64,1,26,128]{3,2,1,0:T(8,128)(2,1)}), bf16[64,1,26,128]{3,2,1,0:T(8,128)(2,1)S(1)}, u32[]{:S(2)}, u32[]{:S(2)}) %all-to-all-start.4) | async-done | bytes 426016 | tf_op jit(solution)/shard_map/all_to_all | solution.py:32
  353.6 1.2 fusion.66
  (122 shorter events, 13.1 us)
Async XLA Ops:
  0.6 27.8 %copy-start = (bf16[2,26,1024]{2,0,1:T(2,128)(2,1)S(1)}, bf16[2,26,1024]{2,0,1:T(2,128)(2,1)}, u32[]{:S(2)}) copy-start(bf16[2,26,1024]{2,0,1:T(2,128)(2,1)} %param.20) | copy-start | bytes 319492
  2.7 27.2 %copy-start.10 = (f32[2,26,8]{1,2,0:T(8,128)}, f32[2,26,8]{1,2,0:T(8,128)S(1)}, u32[]{:S(2)}) copy-start(f32[2,26,8]{1,2,0:T(8,128)S(1)} %copy.247) | copy-start | bytes 4996
  3.5 46.6 %copy-start.22 = (pred[8,2]{0,1:T(4,128)(4,1)}, pred[8,2]{0,1:T(4,128)(4,1)S(1)}, u32[]{:S(2)}) copy-start(pred[8,2]{0,1:T(4,128)(4,1)S(1)} %broadcast_compare_fusion) | copy-start | bytes 52
  5.0 49.7 %copy-start.24 = (s32[8,2]{0,1:T(2,128)S(1)}, s32[8,2]{0,1:T(2,128)}, u32[]{:S(2)}) copy-start(s32[8,2]{0,1:T(2,128)} %param.25) | copy-start | bytes 196
  6.2 43.9 %all-to-all-start = ((bf16[64,1,26,128]{3,2,1,0:T(8,128)(2,1)}), bf16[64,1,26,128]{3,2,1,0:T(8,128)(2,1)S(1)}, u32[]{:S(2)}, u32[]{:S(2)}) async-start(bf16[64,1,26,128]{3,2,1,0:T(8,128)(2,1)} %copy.250), calls=%async_computation | async-start | bytes 1048576 | tf_op jit(solution)/shard_map/all_to_all | solution.py:32
  50.1 25.8 %all-to-all-start.1 = ((bf16[64,1,26,128]{3,2,1,0:T(8,128)(2,1)}), bf16[64,1,26,128]{3,2,1,0:T(8,128)(2,1)S(1)}, u32[]{:S(2)}, u32[]{:S(2)}) async-start(bf16[64,1,26,128]{3,2,1,0:T(8,128)(2,1)} %copy.254), calls=%async_computation.1 | async-start | bytes 1048576 | tf_op jit(solution)/shard_map/all_to_all | solution.py:32
  76.5 29.7 %copy-start.1 = (bf16[1,128,512]{2,1,0:T(8,128)(2,1)S(1)}, bf16[1,128,512]{2,1,0:T(8,128)(2,1)}, u32[]{:S(2)}) copy-start(bf16[1,128,512]{2,1,0:T(8,128)(2,1)} %param.18) | copy-start | bytes 393220
  76.8 30.2 %copy-start.26 = (s32[8]{0:T(128)S(1)}, s32[8]{0:T(128)}, u32[]{:S(2)}) copy-start(s32[8]{0:T(128)} %param.24) | copy-start | bytes 100
  76.9 30.8 %copy-start.9 = (bf16[1,128,512]{2,1,0:T(8,128)(2,1)S(1)}, bf16[1,128,512]{2,1,0:T(8,128)(2,1)}, u32[]{:S(2)}) copy-start(bf16[1,128,512]{2,1,0:T(8,128)(2,1)} %param.27) | copy-start | bytes 393220
  78.6 34.0 %copy-start.20 = (f32[128]{0:T(128)S(1)}, f32[128]{0:T(128)}, u32[]{:S(2)}) copy-start(f32[128]{0:T(128)} %param.21) | copy-start | bytes 1540
  78.6 106.1 %all-to-all-start.2 = ((bf16[8,208,4,128]{3,1,2,0:T(8,128)(2,1)}), bf16[8,208,4,128]{3,1,2,0:T(8,128)(2,1)S(1)}, u32[]{:S(2)}, u32[]{:S(2)}) async-start(bf16[8,208,4,128]{3,1,2,0:T(8,128)(2,1)} %broadcast_in_dim.74), calls=%async_computation.2 | async-start | bytes 3407872 | tf_op jit(solution)/shard_map/all_to_all | solution.py:39
  111.1 73.9 %copy-start.8 = (pred[128,1664]{0,1:T(8,128)(4,1)}, pred[128,1664]{0,1:T(8,128)(4,1)S(1)}, u32[]{:S(2)}) copy-start(pred[128,1664]{0,1:T(8,128)(4,1)S(1)} %get-tuple-element.262) | copy-start | bytes 638980
  112.5 72.5 %copy-start.12 = (f32[128,4]{0,1:T(4,128)}, f32[128,4]{0,1:T(4,128)S(1)}, u32[]{:S(2)}) copy-start(f32[128,4]{0,1:T(4,128)S(1)} %fusion.76) | copy-start | bytes 6148
  187.7 97.8 %copy-start.19 = (s32[2]{0:T(128)S(1)}, s32[2]{0:T(128)}, u32[]{:S(2)}) copy-start(s32[2]{0:T(128)} %copy-done.18) | copy-start | bytes 28
  285.5 40.4 %copy-start.13 = (f32[128,4]{0,1:T(4,128)S(1)}, f32[128,4]{0,1:T(4,128)}, u32[]{:S(2)}) copy-start(f32[128,4]{0,1:T(4,128)} %copy-done.12) | copy-start | bytes 6148
  285.9 40.4 %copy-start.21 = (f32[128]{0:T(128)S(1)}, f32[128]{0:T(128)}, u32[]{:S(2)}) copy-start(f32[128]{0:T(128)} %param.21) | copy-start | bytes 1540
  285.9 40.4 %copy-start.6 = (bf16[128,1,4,128]{0,3,2,1:T(8,128)(2,1)S(1)}, bf16[128,1,4,128]{0,3,2,1:T(8,128)(2,1)}, u32[]{:S(2)}) copy-start(bf16[128,1,4,128]{0,3,2,1:T(8,128)(2,1)} %get-tuple-element.259) | copy-start | bytes 393220
  286.0 41.1 %copy-start.3 = (f32[128,1,4,128]{3,0,2,1:T(8,128)S(1)}, f32[128,1,4,128]{3,0,2,1:T(8,128)}, u32[]{:S(2)}) copy-start(f32[128,1,4,128]{3,0,2,1:T(8,128)} %copy-done.2) | copy-start | bytes 786436
  286.0 41.1 %copy-start.5 = (f32[128,1,4,128]{3,0,2,1:T(8,128)S(1)}, f32[128,1,4,128]{3,0,2,1:T(8,128)}, u32[]{:S(2)}) copy-start(f32[128,1,4,128]{3,0,2,1:T(8,128)} %copy-done.4) | copy-start | bytes 786436
  286.9 40.4 %copy-start.17 = (f32[128,4]{0,1:T(4,128)S(1)}, f32[128,4]{0,1:T(4,128)}, u32[]{:S(2)}) copy-start(f32[128,4]{0,1:T(4,128)} %copy-done.16) | copy-start | bytes 6148
  286.9 34.3 %all-to-all-start.5 = ((bf16[64,1,26,128]{3,2,1,0:T(8,128)(2,1)}), bf16[64,1,26,128]{3,2,1,0:T(8,128)(2,1)S(1)}, u32[]{:S(2)}, u32[]{:S(2)}) async-start(bf16[64,1,26,128]{3,2,1,0:T(8,128)(2,1)} %bitcast.134), calls=%async_computation.5 | async-start | bytes 1048576 | tf_op jit(solution)/shard_map/all_to_all | solution.py:32
  321.3 31.2 %all-to-all-start.4 = ((bf16[64,1,26,128]{3,2,1,0:T(8,128)(2,1)}), bf16[64,1,26,128]{3,2,1,0:T(8,128)(2,1)S(1)}, u32[]{:S(2)}, u32[]{:S(2)}) async-start(bf16[64,1,26,128]{3,2,1,0:T(8,128)(2,1)} %bitcast.126), calls=%async_computation.4 | async-start | bytes 1048576 | tf_op jit(solution)/shard_map/all_to_all | solution.py:32
  327.6 25.2 %copy-start.7 = (bf16[2,26,1024]{2,0,1:T(2,128)(2,1)S(1)}, bf16[2,26,1024]{2,0,1:T(2,128)(2,1)}, u32[]{:S(2)}) copy-start(bf16[2,26,1024]{2,0,1:T(2,128)(2,1)} %param.19) | copy-start | bytes 319492
  327.9 25.5 %copy-start.11 = (f32[2,26,8]{1,2,0:T(8,128)S(1)}, f32[2,26,8]{1,2,0:T(8,128)}, u32[]{:S(2)}) copy-start(f32[2,26,8]{1,2,0:T(8,128)} %copy-done.10) | copy-start | bytes 4996
  (6 other events, 57.7 us)
where the time goes:
time: 361 us; the launch traced here: 355 us
  waiting for transfers between devices  161 us (45%)
  blocking collectives  97.5 us (27%)
  starting transfers between devices  65.2 us (18%)
  local copies, waits for them, and re-layouts  13.1 us (4%)
  other arithmetic  9.69 us (3%)
  matrix products  4.52 us (1%)
    all_to_all x1, blocking collectives, sum_at_owner(): lax.all_to_all(tiles, axis, split_axis=0, concat_axis=0, tiled=True)  97.5 us
    all_to_all x4, waiting for transfers between devices, one_exchange(): tiles = lax.all_to_all(tiles, axis, split_axis=0, concat_axis=0, tiled=True)  90 us
    all_to_all x1, waiting for transfers between devices, sent_to_all(): return lax.all_to_all(copies, axis, split_axis=0, concat_axis=0, tiled=True)  71.2 us
    all_to_all x4, starting transfers between devices, one_exchange(): tiles = lax.all_to_all(tiles, axis, split_axis=0, concat_axis=0, tiled=True)  37.7 us
    all_to_all x1, starting transfers between devices, sent_to_all(): return lax.all_to_all(copies, axis, split_axis=0, concat_axis=0, tiled=True)  27.6 us
  transfers between devices with their start and end apart: 5, of which 5 were waited for; matrix products, arithmetic and copies ran while one was open for 4% of the time, Pallas kernels for 0%

commit v1 on v0

v1 whole, which is shorter than its diff:
```python
import math

import jax
import jax.numpy as jnp
from jax import lax
from jax.experimental import pallas as pl
from jax.experimental.pallas import tpu as pltpu
from jax.sharding import Mesh, PartitionSpec as P

HD = 128
TILE = 1601
ROWS = 26
HALF = 16
EPSILON = 1e-05
SCALE = 1.0 / math.sqrt(HD)
SCALE_LOG2 = SCALE / math.log(2.0)
F32 = jnp.float32
BF16 = jnp.bfloat16

Y, CORE, Z, N_O, N_C = 4, 2, 8, 8, 8
CHUNK = 256
MID = 1024


def dot(a, b):
    return jnp.dot(a, b, preferred_element_type=F32)


def call(kernel, outs, *args, smem=0, scratch=(), flops=0, limit=None):
    specs = [pl.BlockSpec(memory_space=pltpu.SMEM)] * smem
    specs += [pl.BlockSpec(memory_space=pltpu.VMEM)] * (len(args) - smem)
    size = sum(a.size * a.dtype.itemsize for a in args) + sum(o.size * o.dtype.itemsize for o in outs)
    return pl.pallas_call(
        kernel,
        out_shape=outs,
        in_specs=specs,
        out_specs=[pl.BlockSpec(memory_space=pltpu.VMEM)] * len(outs),
        scratch_shapes=list(scratch),
        cost_estimate=pl.CostEstimate(flops=flops, bytes_accessed=size, transcendentals=0),
        compiler_params=pltpu.CompilerParams(vmem_limit_bytes=limit),
    )(*args)


def shape(dims, dtype):
    return jax.ShapeDtypeStruct(dims, dtype)


def pack_queries(gate_ref, queries_ref, d_out_ref, gain_ref, out_ref):
    gain = gain_ref[...]
    gate = gate_ref[0]
    for g in range(4):
        lanes = slice(g * HD, (g + 1) * HD)
        x = queries_ref[0, :, lanes].astype(F32)
        mean_square = jnp.mean(x * x, axis=-1, keepdims=True)
        out_ref[0:128, lanes] = (x * lax.rsqrt(mean_square + EPSILON) * gain).astype(BF16)
    out_ref[128:256, :] = (gate * d_out_ref[0].astype(F32)).astype(BF16)


def pack_keys(keys_ref, values_ref, gain_ref, out_ref):
    gain = gain_ref[...]
    for n in range(2):
        for head in range(8):
            hhi, hx = divmod(head, 4)
            lanes = slice(head * HD, (head + 1) * HD)
            x = keys_ref[n, :, lanes].astype(F32)
            mean_square = jnp.mean(x * x, axis=-1, keepdims=True)
            normed = (x * lax.rsqrt(mean_square + EPSILON) * gain).astype(BF16)
            pad = jnp.zeros((2 * HALF - ROWS, HD), BF16)
            for kv, rows in ((0, normed), (1, values_ref[n, :, lanes])):
                for half in range(2):
                    at = (n * 2 + half) * 2 + kv
                    if half == 0:
                        out_ref[at, hx, hhi * HALF : (hhi + 1) * HALF, :] = rows[:HALF]
                    else:
                        out_ref[at, hx, hhi * HALF : (hhi + 1) * HALF, :] = jnp.concatenate([rows[HALF:], pad], axis=0)


def choose_tiles(owner_ref, got_ref, out_ref):
    for c in range(N_C):
        o = jnp.maximum(owner_ref[c], 0)
        chunk = got_ref[o]
        for hhi in range(2):
            out_ref[hhi, c] = chunk[:, hhi * HALF : (hhi + 1) * HALF, :].reshape(4 * HALF, HD)


def return_tiles(owner_ref, got_ref, out_ref):
    for o in range(N_O):
        found = jnp.int32(-1)
        for c in range(N_C):
            found = jnp.where(owner_ref[c] == o, c, found)
        at = jnp.maximum(found, 0)
        for hhi in range(2):
            chunk = jnp.where(found >= 0, got_ref[hhi, at].astype(F32), 0.0).astype(BF16)
            out_ref[o, :, hhi * HALF : (hhi + 1) * HALF, :] = chunk.reshape(4, HALF, HD)


def row_mask(half):
    position = lax.broadcasted_iota(jnp.int32, (MID, HD), 0)
    thi, s, tx, i = position >> 9, (position >> 6) & 7, (position >> 4) & 3, position & 15
    inside = half * HALF + i
    row = s * (8 * ROWS) + (thi * 4 + tx) * ROWS + inside
    return jnp.where((inside < ROWS) & (row < TILE), 1.0, 0.0).astype(F32)


def columns(rows):
    return jnp.concatenate([rows[:, g * HD : (g + 1) * HD].astype(F32).T for g in range(4)], axis=1)


def stacked(rows):
    return jnp.concatenate([rows[:, g * HD : (g + 1) * HD] for g in range(4)], axis=0)


def seen_row(ids_ref, count_ref, visible_ref, j):
    y, core, z = ids_ref[0], ids_ref[1], ids_ref[2]
    block = (((y - j) & 3) * 2 + core) ^ z
    seen = jnp.minimum(visible_ref[pl.ds(z * 8 + block, 1), :], count_ref[z])
    seen = jnp.where(seen > (y >> 1), 1.0, 0.0).astype(F32)
    return jnp.concatenate([seen] * 4, axis=1)


def masked_weights(keys_s, ok_s, q_t, rows):
    scores = dot(keys_s[rows, :], q_t)
    ok = ok_s[rows, :]
    return jnp.exp2(scores * SCALE_LOG2) * jnp.concatenate([ok] * 4, axis=1)


def load_pair(ids_ref, mine_ref, other_ref, keys_s, values_s, ok_s):
    core = ids_ref[1]

    @pl.when(core == 0)
    def _():
        keys_s[...] = mine_ref[...]
        values_s[...] = other_ref[...]

    @pl.when(core != 0)
    def _():
        keys_s[...] = other_ref[...]
        values_s[...] = mine_ref[...]

    ok_s[...] = row_mask(ids_ref[0] & 1)


def forward(ids_ref, count_ref, visible_ref, mine_ref, other_ref, q0, q1, q2, q3, acc_ref, sums_ref, keys_s, values_s, ok_s, turned_s, q_s):
    load_pair(ids_ref, mine_ref, other_ref, keys_s, values_s, ok_s)
    turned_s[...] = values_s[...].astype(F32).T.astype(BF16)
    for j, q in enumerate((q0, q1, q2, q3)):
        q_s[j] = q[...]

    def block(j, carry):
        q_t = columns(q_s[j, 0:128, :]).astype(BF16)
        o_t = columns(q_s[j, 128:256, :])
        total = jnp.zeros((1, 512), F32)
        acc = jnp.zeros((HD, 512), F32)
        for r in range(MID // CHUNK):
            rows = slice(r * CHUNK, (r + 1) * CHUNK)
            weights = masked_weights(keys_s, ok_s, q_t, rows)
            total = total + jnp.sum(weights, axis=0, keepdims=True)
            acc = acc + dot(turned_s[:, rows], weights.astype(BF16))
        seen = seen_row(ids_ref, count_ref, visible_ref, j)
        acc = acc * seen
        sums_ref[j] = jnp.concatenate([total * seen, jnp.sum(acc * o_t, axis=0, keepdims=True)], axis=0)
        acc_ref[j] = acc.astype(BF16)
        return carry

    lax.fori_loop(0, Y, block, 0)


def all_sums(s0, s1, s2, s3, j):
    both = s0[j] + s1[(j - 1) & 3] + s2[(j - 2) & 3] + s3[(j - 3) & 3]
    total = both[0:1]
    safe = jnp.where(total > 0, total, 1.0)
    return 1.0 / safe, both[1:2] / safe


def backward(
    ids_ref, count_ref, visible_ref, mine_ref, other_ref, q0, q1, q2, q3, s0, s1, s2, s3,
    dq_ref, keep_ref, send_ref, keys_s, values_s, ok_s, turned_s, q_s, dk_s, dv_s,
):
    load_pair(ids_ref, mine_ref, other_ref, keys_s, values_s, ok_s)
    turned_s[...] = keys_s[...].astype(F32).T.astype(BF16)
    dk_s[...] = jnp.zeros((MID, HD), F32)
    dv_s[...] = jnp.zeros((MID, HD), F32)
    for j, q in enumerate((q0, q1, q2, q3)):
        q_s[j] = q[...]

    def block(j, carry):
        q_t = columns(q_s[j, 0:128, :]).astype(BF16)
        o_t = columns(q_s[j, 128:256, :]).astype(BF16)
        q_rows = stacked(q_s[j, 0:128, :])
        o_rows = stacked(q_s[j, 128:256, :])
        inverse, delta = all_sums(s0, s1, s2, s3, j)
        inverse = inverse * seen_row(ids_ref, count_ref, visible_ref, j)
        dq = jnp.zeros((HD, 512), F32)
        for r in range(MID // CHUNK):
            rows = slice(r * CHUNK, (r + 1) * CHUNK)
            prob = masked_weights(keys_s, ok_s, q_t, rows) * inverse
            d_prob = dot(values_s[rows, :], o_t)
            d_score = (prob * (d_prob - delta)).astype(BF16)
            dk_s[rows, :] += dot(d_score, q_rows)
            dv_s[rows, :] += dot(prob.astype(BF16), o_rows)
            dq = dq + dot(turned_s[:, rows], d_score)
        dq_ref[j] = (dq * SCALE).astype(BF16)
        return carry

    lax.fori_loop(0, Y, block, 0)
    core = ids_ref[1]

    @pl.when(core == 0)
    def _():
        keep_ref[...] = dk_s[...] * SCALE
        send_ref[...] = dv_s[...].astype(BF16)

    @pl.when(core != 0)
    def _():
        keep_ref[...] = dv_s[...]
        send_ref[...] = (dk_s[...] * SCALE).astype(BF16)


def finish_attended(gate_ref, a0, a1, a2, a3, s0, s1, s2, s3, out_ref):
    inverse, _ = all_sums(s0, s1, s2, s3, 0)
    acc = a0[0].astype(F32) + a1[...].astype(F32) + a2[...].astype(F32) + a3[...].astype(F32)
    acc = acc * (inverse * gate_ref[0])
    for g in range(4):
        lanes = slice(g * HD, (g + 1) * HD)
        out_ref[:, lanes] = acc[:, lanes].T.astype(BF16)


def sum_queries(d0, d1, d2, d3, out_ref):
    dq = d0[0].astype(F32) + d1[...].astype(F32) + d2[...].astype(F32) + d3[...].astype(F32)
    for g in range(4):
        lanes = slice(g * HD, (g + 1) * HD)
        out_ref[:, lanes] = dq[:, lanes].T.astype(BF16)


def norm_back(x, d_normed, gain):
    mean_square = jnp.mean(x * x, axis=-1, keepdims=True)
    inverse = lax.rsqrt(mean_square + EPSILON)
    scaled = d_normed * gain
    dots = jnp.mean(x * scaled, axis=-1, keepdims=True)
    return inverse * scaled - x * (inverse * inverse * inverse * dots)


def finish_queries(queries_ref, dq_ref, gain_ref, out_ref):
    gain = gain_ref[...]
    for g in range(4):
        lanes = slice(g * HD, (g + 1) * HD)
        x = queries_ref[0, :, lanes].astype(F32)
        out_ref[0, :, lanes] = norm_back(x, dq_ref[:, lanes].astype(F32), gain).astype(BF16)


def finish_keys(keys_ref, got_ref, gain_ref, dk_ref, dv_ref):
    gain = gain_ref[...]
    for n in range(2):
        for head in range(8):
            hhi, hx = divmod(head, 4)
            lanes = slice(head * HD, (head + 1) * HD)
            for half, count in ((0, HALF), (1, ROWS - HALF)):
                at = (n * 2 + half) * 2
                rows = slice(half * HALF, half * HALF + count)
                piece = slice(hhi * HALF, hhi * HALF + count)
                dv_ref[n, rows, lanes] = got_ref[at + 1, hx, piece, :]
                x = keys_ref[n, rows, lanes].astype(F32)
                d_normed = got_ref[at, hx, piece, :].astype(F32)
                dk_ref[n, rows, lanes] = norm_back(x, d_normed, gain).astype(BF16)


def exchange(value, axes):
    return lax.all_to_all(value, axes, split_axis=0, concat_axis=0, tiled=True)


def rotated(value, k):
    return lax.ppermute(value, "y", [(i, (i + k) % Y) for i in range(Y)])


def swapped(value):
    return lax.ppermute(value, "core", [(0, 1), (1, 0)])


TO_PLANE = [(c * 8 + s, (s ^ c) * 8 + c) for c in range(8) for s in range(8)]
FROM_PLANE = [(b, a) for a, b in TO_PLANE]
PLANES = ("y", "core", "seq")


def shards(queries, keys, values, q_gain, k_gain, gate, tile_count, tile_owner, visible, d_out):
    y, core, z = lax.axis_index("y"), lax.axis_index("core"), lax.axis_index("seq")
    ids = jnp.stack([y, core, z]).astype(jnp.int32)
    gate_value = jnp.tanh(gate)
    q_gain = q_gain.reshape(1, HD)
    k_gain = k_gain.reshape(1, HD)
    owner = lax.dynamic_index_in_dim(tile_owner, y // 2, 1, keepdims=False)
    seen = visible.reshape(64, 128)

    (packed,) = call(pack_queries, [shape((256, 512), BF16)], gate_value, queries, d_out, q_gain, smem=1)
    q0 = lax.ppermute(packed, PLANES, TO_PLANE)
    (packed_kv,) = call(pack_keys, [shape((8, 4, 32, HD), BF16)], keys, values, k_gain)
    got = exchange(packed_kv.reshape(32, 32, HD), ("y", "core", "x"))
    (chosen,) = call(choose_tiles, [shape((2, 8, 64, HD), BF16)], owner, got.reshape(8, 4, 32, HD), smem=1)
    mine = exchange(chosen.reshape(16, 64, HD), ("zhi", "seq")).reshape(MID, HD)
    q1, q2, q3 = rotated(q0, 1), rotated(q0, 2), rotated(q0, 3)
    other = swapped(mine)

    common = [pltpu.VMEM((MID, HD), BF16), pltpu.VMEM((MID, HD), BF16), pltpu.VMEM((MID, HD), F32)]
    common += [pltpu.VMEM((HD, MID), BF16), pltpu.VMEM((Y, 256, 512), BF16)]
    acc, sums = call(
        forward,
        [shape((Y, HD, 512), BF16), shape((Y, 2, 512), F32)],
        ids, tile_count, seen, mine, other, q0, q1, q2, q3,
        smem=2, scratch=common, flops=2 * 2 * 2048 * MID * HD, limit=32 << 20,
    )
    s1, s2, s3 = rotated(sums, 1), rotated(sums, 2), rotated(sums, 3)
    a1, a2, a3 = rotated(acc[1], 3), rotated(acc[2], 2), rotated(acc[3], 1)
    dq, keep, send = call(
        backward,
        [shape((Y, HD, 512), BF16), shape((MID, HD), F32), shape((MID, HD), BF16)],
        ids, tile_count, seen, mine, other, q0, q1, q2, q3, sums, s1, s2, s3,
        smem=2, scratch=common + [pltpu.VMEM((MID, HD), F32)] * 2, flops=5 * 2 * 2048 * MID * HD, limit=32 << 20,
    )
    (attended,) = call(finish_attended, [shape((128, 512), BF16)], gate_value, acc, a1, a2, a3, sums, s1, s2, s3, smem=1)
    attended = lax.ppermute(attended, PLANES, FROM_PLANE)

    grads = (keep + swapped(send).astype(F32)).astype(BF16)
    back = exchange(grads.reshape(16, 64, HD), ("zhi", "seq"))
    d1, d2, d3 = rotated(dq[1], 3), rotated(dq[2], 2), rotated(dq[3], 1)
    (d_normed,) = call(sum_queries, [shape((128, 512), BF16)], dq, d1, d2, d3)
    d_normed = lax.ppermute(d_normed, PLANES, FROM_PLANE)
    (placed,) = call(return_tiles, [shape((8, 4, 32, HD), BF16)], owner, back.reshape(2, 8, 64, HD), smem=1)
    home = exchange(placed.reshape(32, 32, HD), ("y", "core", "x")).reshape(8, 4, 32, HD)
    d_keys, d_values = call(finish_keys, [shape(keys.shape, BF16), shape(values.shape, BF16)], keys, home, k_gain)
    (d_queries,) = call(finish_queries, [shape(queries.shape, BF16)], queries, d_normed, q_gain)
    return (attended[None], d_queries, d_keys, d_values)


def solution(mesh):
    parts = Mesh(mesh.devices.reshape(Y, CORE, Z, 2, 4), ("y", "core", "seq", "zhi", "x"))
    conv, tensor = ("y", "core"), ("zhi", "x")
    tokens = P(conv, "seq", tensor)
    rows = P(conv, ("seq", "zhi", "x"), None)
    in_specs = (tokens, rows, rows, P(), P(), P(), P(), P(), P(), tokens)
    out_specs = (tokens, tokens, rows, rows)
    return jax.shard_map(shards, mesh=parts, in_specs=in_specs, out_specs=out_specs, check_vma=False)
```

time: 361 us -> 217 us (0.60)
  the two profiles are of different devices: /device:TPU:1 before, /device:TPU:16 now
where the time goes in v1:
time: 217 us; the launch traced here: 216 us
  starting transfers between devices  110 us (51%)
  waiting for transfers between devices  62.6 us (29%)
  Pallas kernels  29 us (13%)
  local copies, waits for them, and re-layouts  11.4 us (5%)
    ppermute x12, starting transfers between devices, rotated(): return lax.ppermute(value, 'y', [(i, (i + k) % Y) for i in range(Y)])  45.4 us
    all_to_all x4, starting transfers between devices, exchange(): return lax.all_to_all(value, axes, split_axis=0, concat_axis=0, tiled=True)  40.3 us
    ppermute x1, waiting for transfers between devices, shards(): q0 = lax.ppermute(packed, PLANES, TO_PLANE)  31.6 us
    pallas_call x10, Pallas kernels, call(): pl.pallas_call(kernel, out_shape=outs, in_specs=specs, out_specs=[pl.Bloc...  29 us
    ppermute x1, waiting for transfers between devices, shards(): attended = lax.ppermute(attended, PLANES, FROM_PLANE)  13.3 us
    unnamed x47, local copies, waits for them, and re-layouts  10.8 us
    ppermute x1, starting transfers between devices, shards(): q0 = lax.ppermute(packed, PLANES, TO_PLANE)  7.73 us
    ppermute x1, starting transfers between devices, shards(): attended = lax.ppermute(attended, PLANES, FROM_PLANE)  7.39 us
  transfers between devices with their start and end apart: 21, of which 9 were waited for; matrix products, arithmetic and copies ran while one was open for 0% of the time, Pallas kernels for 4%

profile of v1, /device:TPU:16, one launch (start us, length us, event | category | flops | bytes accessed | tf_op | source)
XLA Modules:
  0.0 215.6 jit_solution(17323936823491313596)
XLA Ops:
  4.8 9.3 %all-to-all-start = ((bf16[32,32,128]{2,1,0:T(8,128)(2,1)}), bf16[32,32,128]{2,1,0:T(8,128)(2,1)S(1)}, u32[]{:S(2)}, u32[]{:S(2)}) async-start(bf16[32,32,128]{2,1,0:T(8,128)(2,1)} %bitcast.33), calls=%async_computation | async-start | bytes 524288 | tf_op jit(solution)/shard_map/all_to_all | solution.py:268
  14.7 6.5 %all-to-all-done = bf16[32,32,128]{2,1,0:T(8,128)(2,1)S(1)} async-done(((bf16[32,32,128]{2,1,0:T(8,128)(2,1)}), bf16[32,32,128]{2,1,0:T(8,128)(2,1)S(1)}, u32[]{:S(2)}, u32[]{:S(2)}) %all-to-all-start) | async-done | bytes 262176 | tf_op jit(solution)/shard_map/all_to_all | solution.py:268
  23.5 13.3 %all-to-all-start.1 = ((bf16[16,64,128]{2,1,0:T(8,128)(2,1)}), bf16[16,64,128]{2,1,0:T(8,128)(2,1)S(1)}, u32[]{:S(2)}, u32[]{:S(2)}) async-start(bf16[16,64,128]{2,1,0:T(8,128)(2,1)} %bitcast.35), calls=%async_computation.1 | async-start | bytes 524288 | tf_op jit(solution)/shard_map/all_to_all | solution.py:268
  39.4 7.7 %collective-permute-start.1 = (bf16[256,512]{1,0:T(8,128)(2,1)}, bf16[256,512]{1,0:T(8,128)(2,1)S(1)}, u32[]{:S(2)}, u32[]{:S(2)}) collective-permute-start(bf16[256,512]{1,0:T(8,128)(2,1)} %shard_map.131), channel_id=1, source_target_pairs={{0,0},{8,64},{16,128},{24,192},{32,256},{40,320},{48,384},{56,448}... | collective-permute-start | bytes 786440 | tf_op jit(solution)/shard_map/ppermute | solution.py:294
  47.1 31.6 %collective-permute-done.1.q0 = bf16[256,512]{1,0:T(8,128)(2,1)S(1)} collective-permute-done((bf16[256,512]{1,0:T(8,128)(2,1)}, bf16[256,512]{1,0:T(8,128)(2,1)S(1)}, u32[]{:S(2)}, u32[]{:S(2)}) %collective-permute-start.1) | collective-permute-done | bytes 262176 | tf_op jit(solution)/shard_map/ppermute | solution.py:294
  80.6 12.3 %collective-permute-start.3 = (bf16[256,512]{1,0:T(8,128)(2,1)S(1)}, bf16[256,512]{1,0:T(8,128)(2,1)S(1)}, u32[]{:S(2)}, u32[]{:S(2)}) collective-permute-start(bf16[256,512]{1,0:T(8,128)(2,1)S(1)} %collective-permute-done.1.q0), channel_id=1, source_target_pairs={{0,256},{128,384},{256,0},{384,128},{1,257},{129,385},{257,1},{385... | collective-permute-start | bytes 786440 | tf_op jit(solution)/shard_map/ppermute | solution.py:272
  98.2 2.9 %collective-permute-done.4.q3 = bf16[256,512]{1,0:T(8,128)(2,1)S(1)} collective-permute-done((bf16[256,512]{1,0:T(8,128)(2,1)S(1)}, bf16[256,512]{1,0:T(8,128)(2,1)S(1)}, u32[]{:S(2)}, u32[]{:S(2)}) %collective-permute-start.4) | collective-permute-done | bytes 262176 | tf_op jit(solution)/shard_map/ppermute | solution.py:272
  101.1 5.7 %shard_map.132 = (bf16[4,128,512]{2,1,0:T(8,128)(2,1)S(1)}, f32[4,2,512]{2,1,0:T(2,128)S(1)}) custom-call(s32[3]{0:T(128)S(1)} %pad_add_fusion.ids_ref, s32[8]{0:T(128)S(1)} %copy-done.7, s32[64,128]{1,0:T(8,128)S(1)} %reshape.41.visible_ref, bf16[1024,128]{1,0:T(8,128)(2,1)S(1)} %bitcast.29, bf16[1024,128]{1,0:T(8,128)(2,1)S(1)} %collective-permute-done.other_ref, ...), custom_call_target="tpu_custom_call" | custom-call | flops 1073741824 | bytes 2146348 | tf_op jit(solution)/shard_map/pallas_call | solution.py:33
  106.8 3.7 %collective-permute-start.8 = (f32[4,2,512]{2,1,0:T(2,128)S(1)}, f32[4,2,512]{2,1,0:T(2,128)S(1)}, u32[]{:S(2)}, u32[]{:S(2)}) collective-permute-start(f32[4,2,512]{2,1,0:T(2,128)S(1)} %get-tuple-element.12.s0), channel_id=1, source_target_pairs={{0,128},{128,256},{256,384},{384,0},{1,129},{129,257},{257,385},{3... | collective-permute-start | bytes 49160 | tf_op jit(solution)/shard_map/ppermute | solution.py:272
  110.6 2.5 %collective-permute-start.9 = (f32[4,2,512]{2,1,0:T(2,128)S(1)}, f32[4,2,512]{2,1,0:T(2,128)S(1)}, u32[]{:S(2)}, u32[]{:S(2)}) collective-permute-start(f32[4,2,512]{2,1,0:T(2,128)S(1)} %get-tuple-element.12.s0), channel_id=1, source_target_pairs={{0,256},{128,384},{256,0},{384,128},{1,257},{129,385},{257,1},{385... | collective-permute-start | bytes 49160 | tf_op jit(solution)/shard_map/ppermute | solution.py:272
  113.1 2.8 %collective-permute-start.10 = (f32[4,2,512]{2,1,0:T(2,128)S(1)}, f32[4,2,512]{2,1,0:T(2,128)S(1)}, u32[]{:S(2)}, u32[]{:S(2)}) collective-permute-start(f32[4,2,512]{2,1,0:T(2,128)S(1)} %get-tuple-element.12.s0), channel_id=1, source_target_pairs={{0,384},{128,0},{256,128},{384,256},{1,385},{129,1},{257,129},{385... | collective-permute-start | bytes 49160 | tf_op jit(solution)/shard_map/ppermute | solution.py:272
  118.7 8.6 %shard_map.134 = (bf16[4,128,512]{2,1,0:T(8,128)(2,1)S(1)}, f32[1024,128]{1,0:T(8,128)S(1)}, bf16[1024,128]{1,0:T(8,128)(2,1)S(1)}) custom-call(s32[3]{0:T(128)S(1)} %pad_add_fusion.ids_ref, s32[8]{0:T(128)S(1)} %copy-done.7, s32[64,128]{1,0:T(8,128)S(1)} %reshape.41.visible_ref, bf16[1024,128]{1,0:T(8,128)(2,1)S(1)} %bitcast.30, ...), custom_call_target="tpu_custom_call" | custom-call | flops 2684354560 | bytes 2981932 | tf_op jit(solution)/shard_map/pallas_call | solution.py:33
  131.6 11.0 %all-to-all-start.2 = ((bf16[16,64,128]{2,1,0:T(8,128)(2,1)}), bf16[16,64,128]{2,1,0:T(8,128)(2,1)S(1)}, u32[]{:S(2)}, u32[]{:S(2)}) async-start(bf16[16,64,128]{2,1,0:T(8,128)(2,1)} %bitcast.17), calls=%async_computation.2 | async-start | bytes 524288 | tf_op jit(solution)/shard_map/all_to_all | solution.py:268
  142.6 4.0 %collective-permute-start.5 = (bf16[128,512]{1,0:T(8,128)(2,1)S(1)}, bf16[128,512]{1,0:T(8,128)(2,1)S(1)}, u32[]{:S(2)}, u32[]{:S(2)}) collective-permute-start(bf16[128,512]{1,0:T(8,128)(2,1)S(1)} %get-tuple-element.27), channel_id=1, source_target_pairs={{0,384},{128,0},{256,128},{384,256},{1,385},{129,1},{257,129},{385... | collective-permute-start | bytes 393224 | tf_op jit(solution)/shard_map/ppermute | solution.py:272
  146.5 4.6 %collective-permute-start.6 = (bf16[128,512]{1,0:T(8,128)(2,1)S(1)}, bf16[128,512]{1,0:T(8,128)(2,1)S(1)}, u32[]{:S(2)}, u32[]{:S(2)}) collective-permute-start(bf16[128,512]{1,0:T(8,128)(2,1)S(1)} %get-tuple-element.26), channel_id=1, source_target_pairs={{0,256},{128,384},{256,0},{384,128},{1,257},{129,385},{257,1},{385... | collective-permute-start | bytes 393224 | tf_op jit(solution)/shard_map/ppermute | solution.py:272
  151.1 3.3 %collective-permute-start.7 = (bf16[128,512]{1,0:T(8,128)(2,1)S(1)}, bf16[128,512]{1,0:T(8,128)(2,1)S(1)}, u32[]{:S(2)}, u32[]{:S(2)}) collective-permute-start(bf16[128,512]{1,0:T(8,128)(2,1)S(1)} %get-tuple-element.25), channel_id=1, source_target_pairs={{0,128},{128,256},{256,384},{384,0},{1,129},{129,257},{257,385},{3... | collective-permute-start | bytes 393224 | tf_op jit(solution)/shard_map/ppermute | solution.py:272
  154.5 2.5 %collective-permute-start.12 = (bf16[128,512]{1,0:T(8,128)(2,1)S(1)}, bf16[128,512]{1,0:T(8,128)(2,1)S(1)}, u32[]{:S(2)}, u32[]{:S(2)}) collective-permute-start(bf16[128,512]{1,0:T(8,128)(2,1)S(1)} %get-tuple-element.24), channel_id=1, source_target_pairs={{0,384},{128,0},{256,128},{384,256},{1,385},{129,1},{257,129},{385... | collective-permute-start | bytes 393224 | tf_op jit(solution)/shard_map/ppermute | solution.py:272
  157.0 4.0 %collective-permute-start.13 = (bf16[128,512]{1,0:T(8,128)(2,1)S(1)}, bf16[128,512]{1,0:T(8,128)(2,1)S(1)}, u32[]{:S(2)}, u32[]{:S(2)}) collective-permute-start(bf16[128,512]{1,0:T(8,128)(2,1)S(1)} %get-tuple-element.23), channel_id=1, source_target_pairs={{0,256},{128,384},{256,0},{384,128},{1,257},{129,385},{257,1},{385... | collective-permute-start | bytes 393224 | tf_op jit(solution)/shard_map/ppermute | solution.py:272
  165.4 6.7 %all-to-all-start.3 = ((bf16[32,32,128]{2,1,0:T(8,128)(2,1)}), bf16[32,32,128]{2,1,0:T(8,128)(2,1)S(1)}, u32[]{:S(2)}, u32[]{:S(2)}) async-start(bf16[32,32,128]{2,1,0:T(8,128)(2,1)} %bitcast.31), calls=%async_computation.3 | async-start | bytes 524288 | tf_op jit(solution)/shard_map/all_to_all | solution.py:268
  173.5 2.0 shard_map.133
  175.5 7.4 %collective-permute-start.11 = (bf16[128,512]{1,0:T(8,128)(2,1)}, bf16[128,512]{1,0:T(8,128)(2,1)S(1)}, u32[]{:S(2)}, u32[]{:S(2)}) collective-permute-start(bf16[128,512]{1,0:T(8,128)(2,1)} %shard_map.133), channel_id=1, source_target_pairs={{0,0},{64,8},{128,16},{192,24},{256,32},{320,40},{384,48},{448,56}... | collective-permute-start | bytes 393224 | tf_op jit(solution)/shard_map/ppermute | solution.py:319
  186.2 5.2 %collective-permute-start.15 = (bf16[128,512]{1,0:T(8,128)(2,1)}, bf16[128,512]{1,0:T(8,128)(2,1)S(1)}, u32[]{:S(2)}, u32[]{:S(2)}) collective-permute-start(bf16[128,512]{1,0:T(8,128)(2,1)} %shard_map.135), channel_id=1, source_target_pairs={{0,0},{64,8},{128,16},{192,24},{256,32},{320,40},{384,48},{448,56}... | collective-permute-start | bytes 393224 | tf_op jit(solution)/shard_map/ppermute | solution.py:325
  191.4 13.3 %collective-permute-done.11 = bf16[128,512]{1,0:T(8,128)(2,1)S(1)} collective-permute-done((bf16[128,512]{1,0:T(8,128)(2,1)}, bf16[128,512]{1,0:T(8,128)(2,1)S(1)}, u32[]{:S(2)}, u32[]{:S(2)}) %collective-permute-start.11) | collective-permute-done | bytes 131104 | tf_op jit(solution)/shard_map/ppermute | solution.py:319
  204.7 2.7 %collective-permute-done.15.dq_ref = bf16[128,512]{1,0:T(8,128)(2,1)S(1)} collective-permute-done((bf16[128,512]{1,0:T(8,128)(2,1)}, bf16[128,512]{1,0:T(8,128)(2,1)S(1)}, u32[]{:S(2)}, u32[]{:S(2)}) %collective-permute-start.15) | collective-permute-done | bytes 131104 | tf_op jit(solution)/shard_map/ppermute | solution.py:325
  (81 shorter events, 40.3 us)
Async XLA Ops:
  4.8 16.4 %all-to-all-start = ((bf16[32,32,128]{2,1,0:T(8,128)(2,1)}), bf16[32,32,128]{2,1,0:T(8,128)(2,1)S(1)}, u32[]{:S(2)}, u32[]{:S(2)}) async-start(bf16[32,32,128]{2,1,0:T(8,128)(2,1)} %bitcast.33), calls=%async_computation | async-start | bytes 524288 | tf_op jit(solution)/shard_map/all_to_all | solution.py:268
  23.5 71.3 %all-to-all-start.1 = ((bf16[16,64,128]{2,1,0:T(8,128)(2,1)}), bf16[16,64,128]{2,1,0:T(8,128)(2,1)S(1)}, u32[]{:S(2)}, u32[]{:S(2)}) async-start(bf16[16,64,128]{2,1,0:T(8,128)(2,1)} %bitcast.35), calls=%async_computation.1 | async-start | bytes 524288 | tf_op jit(solution)/shard_map/all_to_all | solution.py:268
  37.5 59.3 %copy-start.20 = (s32[8,1024]{1,0:T(8,128)S(1)}, s32[8,1024]{1,0:T(8,128)}, u32[]{:S(2)}) copy-start(s32[8,1024]{1,0:T(8,128)} %param.18) | copy-start | bytes 98308
  39.4 39.3 %collective-permute-start.1 = (bf16[256,512]{1,0:T(8,128)(2,1)}, bf16[256,512]{1,0:T(8,128)(2,1)S(1)}, u32[]{:S(2)}, u32[]{:S(2)}) collective-permute-start(bf16[256,512]{1,0:T(8,128)(2,1)} %shard_map.131), channel_id=1, source_target_pairs={{0,0},{8,64},{16,128},{24,192},{32,256},{40,320},{48,384},{56,448}... | collective-permute-start | bytes 786440 | tf_op jit(solution)/shard_map/ppermute | solution.py:294
  78.7 18.2 %collective-permute-start.2 = (bf16[256,512]{1,0:T(8,128)(2,1)S(1)}, bf16[256,512]{1,0:T(8,128)(2,1)S(1)}, u32[]{:S(2)}, u32[]{:S(2)}) collective-permute-start(bf16[256,512]{1,0:T(8,128)(2,1)S(1)} %collective-permute-done.1.q0), channel_id=1, source_target_pairs={{0,128},{128,256},{256,384},{384,0},{1,129},{129,257},{257,385},{3... | collective-permute-start | bytes 786440 | tf_op jit(solution)/shard_map/ppermute | solution.py:272
  80.6 17.6 %collective-permute-start.3 = (bf16[256,512]{1,0:T(8,128)(2,1)S(1)}, bf16[256,512]{1,0:T(8,128)(2,1)S(1)}, u32[]{:S(2)}, u32[]{:S(2)}) collective-permute-start(bf16[256,512]{1,0:T(8,128)(2,1)S(1)} %collective-permute-done.1.q0), channel_id=1, source_target_pairs={{0,256},{128,384},{256,0},{384,128},{1,257},{129,385},{257,1},{385... | collective-permute-start | bytes 786440 | tf_op jit(solution)/shard_map/ppermute | solution.py:272
  92.9 8.3 %collective-permute-start.4 = (bf16[256,512]{1,0:T(8,128)(2,1)S(1)}, bf16[256,512]{1,0:T(8,128)(2,1)S(1)}, u32[]{:S(2)}, u32[]{:S(2)}) collective-permute-start(bf16[256,512]{1,0:T(8,128)(2,1)S(1)} %collective-permute-done.1.q0), channel_id=1, source_target_pairs={{0,384},{128,0},{256,128},{384,256},{1,385},{129,1},{257,129},{385... | collective-permute-start | bytes 786440 | tf_op jit(solution)/shard_map/ppermute | solution.py:272
  94.8 6.3 %collective-permute-start = (bf16[1024,128]{1,0:T(8,128)(2,1)S(1)}, bf16[1024,128]{1,0:T(8,128)(2,1)S(1)}, u32[]{:S(2)}, u32[]{:S(2)}) collective-permute-start(bf16[1024,128]{1,0:T(8,128)(2,1)S(1)} %bitcast.28), channel_id=1, source_target_pairs={{0,64},{64,0},{1,65},{65,1},{2,66},{66,2},{3,67},{67,3},{4,68},{68... | collective-permute-start | bytes 786440 | tf_op jit(solution)/shard_map/ppermute | solution.py:276
  106.8 35.7 %copy-start.1 = (bf16[4,128,512]{2,1,0:T(8,128)(2,1)}, bf16[4,128,512]{2,1,0:T(8,128)(2,1)S(1)}, u32[]{:S(2)}) copy-start(bf16[4,128,512]{2,1,0:T(8,128)(2,1)S(1)} %get-tuple-element.11.a0) | copy-start | bytes 1572868
  106.8 9.1 %collective-permute-start.8 = (f32[4,2,512]{2,1,0:T(2,128)S(1)}, f32[4,2,512]{2,1,0:T(2,128)S(1)}, u32[]{:S(2)}, u32[]{:S(2)}) collective-permute-start(f32[4,2,512]{2,1,0:T(2,128)S(1)} %get-tuple-element.12.s0), channel_id=1, source_target_pairs={{0,128},{128,256},{256,384},{384,0},{1,129},{129,257},{257,385},{3... | collective-permute-start | bytes 49160 | tf_op jit(solution)/shard_map/ppermute | solution.py:272
  110.6 7.1 %collective-permute-start.9 = (f32[4,2,512]{2,1,0:T(2,128)S(1)}, f32[4,2,512]{2,1,0:T(2,128)S(1)}, u32[]{:S(2)}, u32[]{:S(2)}) collective-permute-start(f32[4,2,512]{2,1,0:T(2,128)S(1)} %get-tuple-element.12.s0), channel_id=1, source_target_pairs={{0,256},{128,384},{256,0},{384,128},{1,257},{129,385},{257,1},{385... | collective-permute-start | bytes 49160 | tf_op jit(solution)/shard_map/ppermute | solution.py:272
  113.1 5.6 %collective-permute-start.10 = (f32[4,2,512]{2,1,0:T(2,128)S(1)}, f32[4,2,512]{2,1,0:T(2,128)S(1)}, u32[]{:S(2)}, u32[]{:S(2)}) collective-permute-start(f32[4,2,512]{2,1,0:T(2,128)S(1)} %get-tuple-element.12.s0), channel_id=1, source_target_pairs={{0,384},{128,0},{256,128},{384,256},{1,385},{129,1},{257,129},{385... | collective-permute-start | bytes 49160 | tf_op jit(solution)/shard_map/ppermute | solution.py:272
  127.3 27.1 %copy-start.2 = (bf16[4,128,512]{2,1,0:T(8,128)(2,1)}, bf16[4,128,512]{2,1,0:T(8,128)(2,1)S(1)}, u32[]{:S(2)}) copy-start(bf16[4,128,512]{2,1,0:T(8,128)(2,1)S(1)} %get-tuple-element.13.d0) | copy-start | bytes 1572868
  127.4 3.4 %collective-permute-start.16 = (bf16[1024,128]{1,0:T(8,128)(2,1)S(1)}, bf16[1024,128]{1,0:T(8,128)(2,1)S(1)}, u32[]{:S(2)}, u32[]{:S(2)}) collective-permute-start(bf16[1024,128]{1,0:T(8,128)(2,1)S(1)} %get-tuple-element.15), channel_id=1, source_target_pairs={{0,64},{64,0},{1,65},{65,1},{2,66},{66,2},{3,67},{67,3},{4,68},{68... | collective-permute-start | bytes 786440 | tf_op jit(solution)/shard_map/ppermute | solution.py:276
  131.6 31.4 %all-to-all-start.2 = ((bf16[16,64,128]{2,1,0:T(8,128)(2,1)}), bf16[16,64,128]{2,1,0:T(8,128)(2,1)S(1)}, u32[]{:S(2)}, u32[]{:S(2)}) async-start(bf16[16,64,128]{2,1,0:T(8,128)(2,1)} %bitcast.17), calls=%async_computation.2 | async-start | bytes 524288 | tf_op jit(solution)/shard_map/all_to_all | solution.py:268
  142.6 18.5 %collective-permute-start.5 = (bf16[128,512]{1,0:T(8,128)(2,1)S(1)}, bf16[128,512]{1,0:T(8,128)(2,1)S(1)}, u32[]{:S(2)}, u32[]{:S(2)}) collective-permute-start(bf16[128,512]{1,0:T(8,128)(2,1)S(1)} %get-tuple-element.27), channel_id=1, source_target_pairs={{0,384},{128,0},{256,128},{384,256},{1,385},{129,1},{257,129},{385... | collective-permute-start | bytes 393224 | tf_op jit(solution)/shard_map/ppermute | solution.py:272
  146.5 25.6 %collective-permute-start.6 = (bf16[128,512]{1,0:T(8,128)(2,1)S(1)}, bf16[128,512]{1,0:T(8,128)(2,1)S(1)}, u32[]{:S(2)}, u32[]{:S(2)}) collective-permute-start(bf16[128,512]{1,0:T(8,128)(2,1)S(1)} %get-tuple-element.26), channel_id=1, source_target_pairs={{0,256},{128,384},{256,0},{384,128},{1,257},{129,385},{257,1},{385... | collective-permute-start | bytes 393224 | tf_op jit(solution)/shard_map/ppermute | solution.py:272
  151.1 21.1 %collective-permute-start.7 = (bf16[128,512]{1,0:T(8,128)(2,1)S(1)}, bf16[128,512]{1,0:T(8,128)(2,1)S(1)}, u32[]{:S(2)}, u32[]{:S(2)}) collective-permute-start(bf16[128,512]{1,0:T(8,128)(2,1)S(1)} %get-tuple-element.25), channel_id=1, source_target_pairs={{0,128},{128,256},{256,384},{384,0},{1,129},{129,257},{257,385},{3... | collective-permute-start | bytes 393224 | tf_op jit(solution)/shard_map/ppermute | solution.py:272
  154.5 28.4 %collective-permute-start.12 = (bf16[128,512]{1,0:T(8,128)(2,1)S(1)}, bf16[128,512]{1,0:T(8,128)(2,1)S(1)}, u32[]{:S(2)}, u32[]{:S(2)}) collective-permute-start(bf16[128,512]{1,0:T(8,128)(2,1)S(1)} %get-tuple-element.24), channel_id=1, source_target_pairs={{0,384},{128,0},{256,128},{384,256},{1,385},{129,1},{257,129},{385... | collective-permute-start | bytes 393224 | tf_op jit(solution)/shard_map/ppermute | solution.py:272
  157.0 25.9 %collective-permute-start.13 = (bf16[128,512]{1,0:T(8,128)(2,1)S(1)}, bf16[128,512]{1,0:T(8,128)(2,1)S(1)}, u32[]{:S(2)}, u32[]{:S(2)}) collective-permute-start(bf16[128,512]{1,0:T(8,128)(2,1)S(1)} %get-tuple-element.23), channel_id=1, source_target_pairs={{0,256},{128,384},{256,0},{384,128},{1,257},{129,385},{257,1},{385... | collective-permute-start | bytes 393224 | tf_op jit(solution)/shard_map/ppermute | solution.py:272
  161.0 21.9 %collective-permute-start.14 = (bf16[128,512]{1,0:T(8,128)(2,1)S(1)}, bf16[128,512]{1,0:T(8,128)(2,1)S(1)}, u32[]{:S(2)}, u32[]{:S(2)}) collective-permute-start(bf16[128,512]{1,0:T(8,128)(2,1)S(1)} %get-tuple-element.22), channel_id=1, source_target_pairs={{0,128},{128,256},{256,384},{384,0},{1,129},{129,257},{257,385},{3... | collective-permute-start | bytes 393224 | tf_op jit(solution)/shard_map/ppermute | solution.py:272
  165.4 44.5 %all-to-all-start.3 = ((bf16[32,32,128]{2,1,0:T(8,128)(2,1)}), bf16[32,32,128]{2,1,0:T(8,128)(2,1)S(1)}, u32[]{:S(2)}, u32[]{:S(2)}) async-start(bf16[32,32,128]{2,1,0:T(8,128)(2,1)} %bitcast.31), calls=%async_computation.3 | async-start | bytes 524288 | tf_op jit(solution)/shard_map/all_to_all | solution.py:268
  175.5 29.2 %collective-permute-start.11 = (bf16[128,512]{1,0:T(8,128)(2,1)}, bf16[128,512]{1,0:T(8,128)(2,1)S(1)}, u32[]{:S(2)}, u32[]{:S(2)}) collective-permute-start(bf16[128,512]{1,0:T(8,128)(2,1)} %shard_map.133), channel_id=1, source_target_pairs={{0,0},{64,8},{128,16},{192,24},{256,32},{320,40},{384,48},{448,56}... | collective-permute-start | bytes 393224 | tf_op jit(solution)/shard_map/ppermute | solution.py:319
  186.2 21.2 %collective-permute-start.15 = (bf16[128,512]{1,0:T(8,128)(2,1)}, bf16[128,512]{1,0:T(8,128)(2,1)S(1)}, u32[]{:S(2)}, u32[]{:S(2)}) collective-permute-start(bf16[128,512]{1,0:T(8,128)(2,1)} %shard_map.135), channel_id=1, source_target_pairs={{0,0},{64,8},{128,16},{192,24},{256,32},{320,40},{384,48},{448,56}... | collective-permute-start | bytes 393224 | tf_op jit(solution)/shard_map/ppermute | solution.py:325
  (18 other events, 81.7 us)

commit v2 on v1

--- a/solution.py
+++ b/solution.py
@@ -18,6 +18,9 @@
 BF16 = jnp.bfloat16
 
 Y, CORE, Z, N_O, N_C = 4, 2, 8, 8, 8
+PLANE_OF = (0, 7, 1, 6, 2, 5, 3, 4)
+CONV_OF = tuple(PLANE_OF.index(z) for z in range(Z))
+SHIFT = (0, 4, 1, 3, 2, 6, 5, 7)
 CHUNK = 256
 MID = 1024
 
@@ -26,7 +29,7 @@
     return jnp.dot(a, b, preferred_element_type=F32)
 
 
-def call(kernel, outs, *args, smem=0, scratch=(), flops=0, limit=None):
+def call(kernel, outs, *args, smem=0, scratch=(), flops=0, limit=8 << 20):
     specs = [pl.BlockSpec(memory_space=pltpu.SMEM)] * smem
     specs += [pl.BlockSpec(memory_space=pltpu.VMEM)] * (len(args) - smem)
     size = sum(a.size * a.dtype.itemsize for a in args) + sum(o.size * o.dtype.itemsize for o in outs)
@@ -76,18 +79,18 @@
 
 
 def choose_tiles(owner_ref, got_ref, out_ref):
-    for c in range(N_C):
-        o = jnp.maximum(owner_ref[c], 0)
+    for z in range(Z):
+        o = jnp.maximum(owner_ref[CONV_OF[z]], 0)
         chunk = got_ref[o]
         for hhi in range(2):
-            out_ref[hhi, c] = chunk[:, hhi * HALF : (hhi + 1) * HALF, :].reshape(4 * HALF, HD)
+            out_ref[hhi, z] = chunk[:, hhi * HALF : (hhi + 1) * HALF, :].reshape(4 * HALF, HD)
 
 
 def return_tiles(owner_ref, got_ref, out_ref):
     for o in range(N_O):
         found = jnp.int32(-1)
         for c in range(N_C):
-            found = jnp.where(owner_ref[c] == o, c, found)
+            found = jnp.where(owner_ref[c] == o, PLANE_OF[c], found)
         at = jnp.maximum(found, 0)
         for hhi in range(2):
             chunk = jnp.where(found >= 0, got_ref[hhi, at].astype(F32), 0.0).astype(BF16)
@@ -112,8 +115,13 @@
 
 def seen_row(ids_ref, count_ref, visible_ref, j):
     y, core, z = ids_ref[0], ids_ref[1], ids_ref[2]
-    block = (((y - j) & 3) * 2 + core) ^ z
-    seen = jnp.minimum(visible_ref[pl.ds(z * 8 + block, 1), :], count_ref[z])
+    conv = jnp.where(z < 4, 2 * z, 15 - 2 * z)
+    source = ((y - j) & 3) * 2 + core
+    shift = jnp.int32(0)
+    for i in range(1, 8):
+        shift = jnp.where(source == i, SHIFT[i], shift)
+    block = (z + shift) & 7
+    seen = jnp.minimum(visible_ref[pl.ds(conv * 8 + block, 1), :], count_ref[conv])
     seen = jnp.where(seen > (y >> 1), 1.0, 0.0).astype(F32)
     return jnp.concatenate([seen] * 4, axis=1)
 
@@ -158,23 +166,28 @@
             acc = acc + dot(turned_s[:, rows], weights.astype(BF16))
         seen = seen_row(ids_ref, count_ref, visible_ref, j)
         acc = acc * seen
-        sums_ref[j] = jnp.concatenate([total * seen, jnp.sum(acc * o_t, axis=0, keepdims=True)], axis=0)
-        acc_ref[j] = acc.astype(BF16)
+        both = jnp.concatenate([total * seen, jnp.sum(acc * o_t, axis=0, keepdims=True)], axis=0)
+        for to in range(Y):
+            sums_ref[to, j] = both
+        acc_ref[j] = acc
         return carry
 
     lax.fori_loop(0, Y, block, 0)
 
 
-def all_sums(s0, s1, s2, s3, j):
-    both = s0[j] + s1[(j - 1) & 3] + s2[(j - 2) & 3] + s3[(j - 3) & 3]
+def all_sums(ids_ref, sums_ref, j):
+    y = ids_ref[0]
+    both = sums_ref[y, j]
+    for k in range(1, Y):
+        both = both + sums_ref[(y - k) & 3, (j - k) & 3]
     total = both[0:1]
     safe = jnp.where(total > 0, total, 1.0)
     return 1.0 / safe, both[1:2] / safe
 
 
 def backward(
-    ids_ref, count_ref, visible_ref, mine_ref, other_ref, q0, q1, q2, q3, s0, s1, s2, s3,
-    dq_ref, keep_ref, send_ref, keys_s, values_s, ok_s, turned_s, q_s, dk_s, dv_s,
+    ids_ref, count_ref, visible_ref, mine_ref, other_ref, q0, q1, q2, q3, acc_ref, sums_ref,
+    r0, r1, r2, r3, keep_ref, send_ref, keys_s, values_s, ok_s, turned_s, q_s, dk_s, dv_s,
 ):
     load_pair(ids_ref, mine_ref, other_ref, keys_s, values_s, ok_s)
     turned_s[...] = keys_s[...].astype(F32).T.astype(BF16)
@@ -188,7 +201,8 @@
         o_t = columns(q_s[j, 128:256, :]).astype(BF16)
         q_rows = stacked(q_s[j, 0:128, :])
         o_rows = stacked(q_s[j, 128:256, :])
-        inverse, delta = all_sums(s0, s1, s2, s3, j)
+        inverse, delta = all_sums(ids_ref, sums_ref, j)
+        acc = (acc_ref[j] * inverse).astype(BF16)
         inverse = inverse * seen_row(ids_ref, count_ref, visible_ref, j)
         dq = jnp.zeros((HD, 512), F32)
         for r in range(MID // CHUNK):
@@ -199,10 +213,12 @@
             dk_s[rows, :] += dot(d_score, q_rows)
             dv_s[rows, :] += dot(prob.astype(BF16), o_rows)
             dq = dq + dot(turned_s[:, rows], d_score)
-        dq_ref[j] = (dq * SCALE).astype(BF16)
+        q_s[j] = jnp.concatenate([acc, (dq * SCALE).astype(BF16)], axis=0)
         return carry
 
     lax.fori_loop(0, Y, block, 0)
+    for j, r in enumerate((r0, r1, r2, r3)):
+        r[...] = q_s[j]
     core = ids_ref[1]
 
     @pl.when(core == 0)
@@ -216,20 +232,12 @@
         send_ref[...] = (dk_s[...] * SCALE).astype(BF16)
 
 
-def finish_attended(gate_ref, a0, a1, a2, a3, s0, s1, s2, s3, out_ref):
-    inverse, _ = all_sums(s0, s1, s2, s3, 0)
-    acc = a0[0].astype(F32) + a1[...].astype(F32) + a2[...].astype(F32) + a3[...].astype(F32)
-    acc = acc * (inverse * gate_ref[0])
+def sum_tokens(gate_ref, r0, r1, r2, r3, out_ref):
+    both = r0[...].astype(F32) + r1[...].astype(F32) + r2[...].astype(F32) + r3[...].astype(F32)
     for g in range(4):
         lanes = slice(g * HD, (g + 1) * HD)
-        out_ref[:, lanes] = acc[:, lanes].T.astype(BF16)
-
-
-def sum_queries(d0, d1, d2, d3, out_ref):
-    dq = d0[0].astype(F32) + d1[...].astype(F32) + d2[...].astype(F32) + d3[...].astype(F32)
-    for g in range(4):
-        lanes = slice(g * HD, (g + 1) * HD)
-        out_ref[:, lanes] = dq[:, lanes].T.astype(BF16)
+        out_ref[0:128, lanes] = (both[0:128, lanes].T * gate_ref[0]).astype(BF16)
+        out_ref[128:256, lanes] = both[128:256, lanes].T.astype(BF16)
 
 
 def norm_back(x, d_normed, gain):
@@ -240,12 +248,13 @@
     return inverse * scaled - x * (inverse * inverse * inverse * dots)
 
 
-def finish_queries(queries_ref, dq_ref, gain_ref, out_ref):
+def finish_queries(queries_ref, got_ref, gain_ref, attended_ref, out_ref):
     gain = gain_ref[...]
+    attended_ref[0] = got_ref[0:128, :]
     for g in range(4):
         lanes = slice(g * HD, (g + 1) * HD)
         x = queries_ref[0, :, lanes].astype(F32)
-        out_ref[0, :, lanes] = norm_back(x, dq_ref[:, lanes].astype(F32), gain).astype(BF16)
+        out_ref[0, :, lanes] = norm_back(x, got_ref[128:256, lanes].astype(F32), gain).astype(BF16)
 
 
 def finish_keys(keys_ref, got_ref, gain_ref, dk_ref, dv_ref):
@@ -276,7 +285,7 @@
     return lax.ppermute(value, "core", [(0, 1), (1, 0)])
 
 
-TO_PLANE = [(c * 8 + s, (s ^ c) * 8 + c) for c in range(8) for s in range(8)]
+TO_PLANE = [(c * 8 + (z + SHIFT[i]) % 8, i * 8 + z) for i in range(8) for z, c in enumerate(CONV_OF)]
 FROM_PLANE = [(b, a) for a, b in TO_PLANE]
 PLANES = ("y", "core", "seq")
 
@@ -291,9 +300,11 @@
     seen = visible.reshape(64, 128)
 
     (packed,) = call(pack_queries, [shape((256, 512), BF16)], gate_value, queries, d_out, q_gain, smem=1)
+    packed, keys, values = lax.optimization_barrier((packed, keys, values))
     q0 = lax.ppermute(packed, PLANES, TO_PLANE)
     (packed_kv,) = call(pack_keys, [shape((8, 4, 32, HD), BF16)], keys, values, k_gain)
     got = exchange(packed_kv.reshape(32, 32, HD), ("y", "core", "x"))
+    got, q0 = lax.optimization_barrier((got, q0))
     (chosen,) = call(choose_tiles, [shape((2, 8, 64, HD), BF16)], owner, got.reshape(8, 4, 32, HD), smem=1)
     mine = exchange(chosen.reshape(16, 64, HD), ("zhi", "seq")).reshape(MID, HD)
     q1, q2, q3 = rotated(q0, 1), rotated(q0, 2), rotated(q0, 3)
@@ -303,31 +314,28 @@
     common += [pltpu.VMEM((HD, MID), BF16), pltpu.VMEM((Y, 256, 512), BF16)]
     acc, sums = call(
         forward,
-        [shape((Y, HD, 512), BF16), shape((Y, 2, 512), F32)],
+        [shape((Y, HD, 512), F32), shape((Y, Y, 2, 512), F32)],
         ids, tile_count, seen, mine, other, q0, q1, q2, q3,
         smem=2, scratch=common, flops=2 * 2 * 2048 * MID * HD, limit=32 << 20,
     )
-    s1, s2, s3 = rotated(sums, 1), rotated(sums, 2), rotated(sums, 3)
-    a1, a2, a3 = rotated(acc[1], 3), rotated(acc[2], 2), rotated(acc[3], 1)
-    dq, keep, send = call(
+    sums = exchange(sums, "y")
+    r0, r1, r2, r3, keep, send = call(
         backward,
-        [shape((Y, HD, 512), BF16), shape((MID, HD), F32), shape((MID, HD), BF16)],
-        ids, tile_count, seen, mine, other, q0, q1, q2, q3, sums, s1, s2, s3,
+        [shape((256, 512), BF16)] * 4 + [shape((MID, HD), F32), shape((MID, HD), BF16)],
+        ids, tile_count, seen, mine, other, q0, q1, q2, q3, acc, sums,
         smem=2, scratch=common + [pltpu.VMEM((MID, HD), F32)] * 2, flops=5 * 2 * 2048 * MID * HD, limit=32 << 20,
     )
-    (attended,) = call(finish_attended, [shape((128, 512), BF16)], gate_value, acc, a1, a2, a3, sums, s1, s2, s3, smem=1)
-    attended = lax.ppermute(attended, PLANES, FROM_PLANE)
 
     grads = (keep + swapped(send).astype(F32)).astype(BF16)
     back = exchange(grads.reshape(16, 64, HD), ("zhi", "seq"))
-    d1, d2, d3 = rotated(dq[1], 3), rotated(dq[2], 2), rotated(dq[3], 1)
-    (d_normed,) = call(sum_queries, [shape((128, 512), BF16)], dq, d1, d2, d3)
-    d_normed = lax.ppermute(d_normed, PLANES, FROM_PLANE)
+    r1, r2, r3 = rotated(r1, 3), rotated(r2, 2), rotated(r3, 1)
+    (summed,) = call(sum_tokens, [shape((256, 512), BF16)], gate_value, r0, r1, r2, r3, smem=1)
+    summed = lax.ppermute(summed, PLANES, FROM_PLANE)
     (placed,) = call(return_tiles, [shape((8, 4, 32, HD), BF16)], owner, back.reshape(2, 8, 64, HD), smem=1)
     home = exchange(placed.reshape(32, 32, HD), ("y", "core", "x")).reshape(8, 4, 32, HD)
     d_keys, d_values = call(finish_keys, [shape(keys.shape, BF16), shape(values.shape, BF16)], keys, home, k_gain)
-    (d_queries,) = call(finish_queries, [shape(queries.shape, BF16)], queries, d_normed, q_gain)
-    return (attended[None], d_queries, d_keys, d_values)
+    attended, d_queries = call(finish_queries, [shape(queries.shape, BF16)] * 2, queries, summed, q_gain)
+    return (attended, d_queries, d_keys, d_values)
 
 
 def solution(mesh):

time: 217 us -> 155 us (0.71)
  the two profiles are of different devices: /device:TPU:16 before, /device:TPU:1 now
where the time goes in v2:
time: 155 us; the launch traced here: 154 us
  starting transfers between devices  84.9 us (55%)
  waiting for transfers between devices  34 us (22%)
  Pallas kernels  19.2 us (12%)
  blocking collectives  8.77 us (6%)
  local copies, waits for them, and re-layouts  4.71 us (3%)
  between operations  1.64 us (1%)
    all_to_all x4, starting transfers between devices, exchange(): return lax.all_to_all(value, axes, split_axis=0, concat_axis=0, tiled=True)  31.6 us
    all_to_all x4, waiting for transfers between devices, exchange(): return lax.all_to_all(value, axes, split_axis=0, concat_axis=0, tiled=True)  19.7 us
    pallas_call x9, Pallas kernels, call(): pl.pallas_call(kernel, out_shape=outs, in_specs=specs, out_specs=[pl.Bloc...  19.2 us
    ppermute x6, starting transfers between devices, rotated(): return lax.ppermute(value, 'y', [(i, (i + k) % Y) for i in range(Y)])  17.7 us
    ppermute x1, starting transfers between devices, shards(): q0 = lax.ppermute(packed, PLANES, TO_PLANE)  15.4 us
    ppermute x2, starting transfers between devices, swapped(): return lax.ppermute(value, 'core', [(0, 1), (1, 0)])  12.6 us
    ppermute x6, waiting for transfers between devices, rotated(): return lax.ppermute(value, 'y', [(i, (i + k) % Y) for i in range(Y)])  12.2 us
    all_to_all x1, blocking collectives, exchange(): return lax.all_to_all(value, axes, split_axis=0, concat_axis=0, tiled=True)  8.77 us
  transfers between devices with their start and end apart: 14, of which 8 were waited for; matrix products, arithmetic and copies ran while one was open for 0% of the time, Pallas kernels for 2%

profile of v2, /device:TPU:1, one launch (start us, length us, event | category | flops | bytes accessed | tf_op | source)
XLA Modules:
  0.0 154.1 jit_solution(1735229132210837990)
XLA Ops:
  4.0 15.4 %collective-permute-start = (bf16[256,512]{1,0:T(8,128)(2,1)S(1)}, bf16[256,512]{1,0:T(8,128)(2,1)S(1)}, u32[]{:S(2)}, u32[]{:S(2)}) collective-permute-start(bf16[256,512]{1,0:T(8,128)(2,1)S(1)} %shard_map.129), channel_id=1, source_target_pairs={{0,0},{136,8},{272,16},{408,24},{480,32},{360,40},{240,48},{120,56... | collective-permute-start | bytes 786440 | tf_op jit(solution)/shard_map/ppermute | solution.py:304
  21.0 4.6 %all-to-all-start = ((bf16[32,32,128]{2,1,0:T(8,128)(2,1)}), bf16[32,32,128]{2,1,0:T(8,128)(2,1)S(1)}, u32[]{:S(2)}, u32[]{:S(2)}) async-start(bf16[32,32,128]{2,1,0:T(8,128)(2,1)} %bitcast.6), calls=%async_computation | async-start | bytes 524288 | tf_op jit(solution)/shard_map/all_to_all | solution.py:277
  25.6 8.8 %all-to-all-done = bf16[32,32,128]{2,1,0:T(8,128)(2,1)S(1)} async-done(((bf16[32,32,128]{2,1,0:T(8,128)(2,1)}), bf16[32,32,128]{2,1,0:T(8,128)(2,1)S(1)}, u32[]{:S(2)}, u32[]{:S(2)}) %all-to-all-start) | async-done | bytes 262176 | tf_op jit(solution)/shard_map/all_to_all | solution.py:277
  34.5 1.3 shard_map.131
  35.8 9.3 %all-to-all-start.1 = ((bf16[16,64,128]{2,1,0:T(8,128)(2,1)}), bf16[16,64,128]{2,1,0:T(8,128)(2,1)S(1)}, u32[]{:S(2)}, u32[]{:S(2)}) async-start(bf16[16,64,128]{2,1,0:T(8,128)(2,1)} %bitcast.8), calls=%async_computation.1 | async-start | bytes 524288 | tf_op jit(solution)/shard_map/all_to_all | solution.py:277
  45.1 3.7 %collective-permute-start.4 = (bf16[256,512]{1,0:T(8,128)(2,1)S(1)}, bf16[256,512]{1,0:T(8,128)(2,1)S(1)}, u32[]{:S(2)}, u32[]{:S(2)}) collective-permute-start(bf16[256,512]{1,0:T(8,128)(2,1)S(1)} %collective-permute-done.q0), channel_id=1, source_target_pairs={{0,384},{128,0},{256,128},{384,256},{1,385},{129,1},{257,129},{385... | collective-permute-start | bytes 786440 | tf_op jit(solution)/shard_map/ppermute | solution.py:281
  48.8 3.7 %collective-permute-start.3 = (bf16[256,512]{1,0:T(8,128)(2,1)S(1)}, bf16[256,512]{1,0:T(8,128)(2,1)S(1)}, u32[]{:S(2)}, u32[]{:S(2)}) collective-permute-start(bf16[256,512]{1,0:T(8,128)(2,1)S(1)} %collective-permute-done.q0), channel_id=1, source_target_pairs={{0,256},{128,384},{256,0},{384,128},{1,257},{129,385},{257,1},{385... | collective-permute-start | bytes 786440 | tf_op jit(solution)/shard_map/ppermute | solution.py:281
  52.4 2.5 %collective-permute-start.2 = (bf16[256,512]{1,0:T(8,128)(2,1)S(1)}, bf16[256,512]{1,0:T(8,128)(2,1)S(1)}, u32[]{:S(2)}, u32[]{:S(2)}) collective-permute-start(bf16[256,512]{1,0:T(8,128)(2,1)S(1)} %collective-permute-done.q0), channel_id=1, source_target_pairs={{0,128},{128,256},{256,384},{384,0},{1,129},{129,257},{257,385},{3... | collective-permute-start | bytes 786440 | tf_op jit(solution)/shard_map/ppermute | solution.py:281
  55.0 2.9 %all-to-all-done.1 = bf16[16,64,128]{2,1,0:T(8,128)(2,1)S(1)} async-done(((bf16[16,64,128]{2,1,0:T(8,128)(2,1)}), bf16[16,64,128]{2,1,0:T(8,128)(2,1)S(1)}, u32[]{:S(2)}, u32[]{:S(2)}) %all-to-all-start.1) | async-done | bytes 262176 | tf_op jit(solution)/shard_map/all_to_all | solution.py:277
  57.8 8.9 %collective-permute-start.1 = (bf16[1024,128]{1,0:T(8,128)(2,1)S(1)}, bf16[1024,128]{1,0:T(8,128)(2,1)S(1)}, u32[]{:S(2)}, u32[]{:S(2)}) collective-permute-start(bf16[1024,128]{1,0:T(8,128)(2,1)S(1)} %bitcast.18), channel_id=1, source_target_pairs={{0,64},{64,0},{1,65},{65,1},{2,66},{66,2},{3,67},{67,3},{4,68},{68... | collective-permute-start | bytes 786440 | tf_op jit(solution)/shard_map/ppermute | solution.py:285
  67.9 5.7 %shard_map.132 = (f32[4,128,512]{2,1,0:T(8,128)S(1)}, f32[4,4,2,512]{3,2,1,0:T(2,128)S(1)}) custom-call(s32[3]{0:T(128)S(1)} %pad_add_fusion.ids_ref, s32[8]{0:T(128)S(1)} %copy-done.6, s32[64,128]{1,0:T(8,128)S(1)} %reshape.41.visible_ref, bf16[1024,128]{1,0:T(8,128)(2,1)S(1)} %bitcast.19, bf16[1024,128]{1,0:T(8,128)(2,1)S(1)} %collective-permute-done.1.other_ref, ...), custom_call_target="tpu_custom_call" | custom-call | flops 1073741824 | bytes 2719788 | tf_op jit(solution)/shard_map/pallas_call | solution.py:36
  73.5 8.8 %all_to_all.25.sums_ref = f32[4,4,2,512]{3,2,1,0:T(2,128)S(1)} all-to-all(f32[4,4,2,512]{3,2,1,0:T(2,128)S(1)} %get-tuple-element.27), channel_id=1, replica_groups=mesh['y'=4,'core'=2,'seq'=8,'zhi'=2,'x'=4] {'y'}, dimensions={0} | all-to-all | bytes 131072 | tf_op jit(solution)/shard_map/all_to_all | solution.py:277
  82.3 8.6 %shard_map.133 = (bf16[256,512]{1,0:T(8,128)(2,1)S(1)}, bf16[256,512]{1,0:T(8,128)(2,1)S(1)}, bf16[256,512]{1,0:T(8,128)(2,1)S(1)}, bf16[256,512]{1,0:T(8,128)(2...) custom-call(s32[3]{0:T(128)S(1)} %pad_add_fusion.ids_ref, s32[8]{0:T(128)S(1)} %copy-done.6, ...), custom_call_target="tpu_custom_call" | custom-call | flops 2684354560 | bytes 4554796 | tf_op jit(solution)/shard_map/pallas_call | solution.py:36
  90.9 3.7 %collective-permute-start.9 = (bf16[1024,128]{1,0:T(8,128)(2,1)S(1)}, bf16[1024,128]{1,0:T(8,128)(2,1)S(1)}, u32[]{:S(2)}, u32[]{:S(2)}) collective-permute-start(bf16[1024,128]{1,0:T(8,128)(2,1)S(1)} %get-tuple-element.35), channel_id=1, source_target_pairs={{0,64},{64,0},{1,65},{65,1},{2,66},{66,2},{3,67},{67,3},{4,68},{68... | collective-permute-start | bytes 786440 | tf_op jit(solution)/shard_map/ppermute | solution.py:285
  96.5 8.3 %all-to-all-start.3 = ((bf16[16,64,128]{2,1,0:T(8,128)(2,1)}), bf16[16,64,128]{2,1,0:T(8,128)(2,1)S(1)}, u32[]{:S(2)}, u32[]{:S(2)}) async-start(bf16[16,64,128]{2,1,0:T(8,128)(2,1)} %bitcast.10), calls=%async_computation.3 | async-start | bytes 524288 | tf_op jit(solution)/shard_map/all_to_all | solution.py:277
  104.8 2.8 %collective-permute-start.5 = (bf16[256,512]{1,0:T(8,128)(2,1)S(1)}, bf16[256,512]{1,0:T(8,128)(2,1)S(1)}, u32[]{:S(2)}, u32[]{:S(2)}) collective-permute-start(bf16[256,512]{1,0:T(8,128)(2,1)S(1)} %get-tuple-element.29), channel_id=1, source_target_pairs={{0,384},{128,0},{256,128},{384,256},{1,385},{129,1},{257,129},{385... | collective-permute-start | bytes 786440 | tf_op jit(solution)/shard_map/ppermute | solution.py:281
  107.6 3.1 %collective-permute-start.6 = (bf16[256,512]{1,0:T(8,128)(2,1)S(1)}, bf16[256,512]{1,0:T(8,128)(2,1)S(1)}, u32[]{:S(2)}, u32[]{:S(2)}) collective-permute-start(bf16[256,512]{1,0:T(8,128)(2,1)S(1)} %get-tuple-element.30), channel_id=1, source_target_pairs={{0,256},{128,384},{256,0},{384,128},{1,257},{129,385},{257,1},{385... | collective-permute-start | bytes 786440 | tf_op jit(solution)/shard_map/ppermute | solution.py:281
  110.7 1.9 %collective-permute-start.7 = (bf16[256,512]{1,0:T(8,128)(2,1)S(1)}, bf16[256,512]{1,0:T(8,128)(2,1)S(1)}, u32[]{:S(2)}, u32[]{:S(2)}) collective-permute-start(bf16[256,512]{1,0:T(8,128)(2,1)S(1)} %get-tuple-element.31), channel_id=1, source_target_pairs={{0,128},{128,256},{256,384},{384,0},{1,129},{129,257},{257,385},{3... | collective-permute-start | bytes 786440 | tf_op jit(solution)/shard_map/ppermute | solution.py:281
  113.9 4.0 %collective-permute-done.6.r2 = bf16[256,512]{1,0:T(8,128)(2,1)S(1)} collective-permute-done((bf16[256,512]{1,0:T(8,128)(2,1)S(1)}, bf16[256,512]{1,0:T(8,128)(2,1)S(1)}, u32[]{:S(2)}, u32[]{:S(2)}) %collective-permute-start.6) | collective-permute-done | bytes 262176 | tf_op jit(solution)/shard_map/ppermute | solution.py:281
  117.9 6.9 %collective-permute-done.7.r3 = bf16[256,512]{1,0:T(8,128)(2,1)S(1)} collective-permute-done((bf16[256,512]{1,0:T(8,128)(2,1)S(1)}, bf16[256,512]{1,0:T(8,128)(2,1)S(1)}, u32[]{:S(2)}, u32[]{:S(2)}) %collective-permute-start.7) | collective-permute-done | bytes 262176 | tf_op jit(solution)/shard_map/ppermute | solution.py:281
  125.0 7.6 %collective-permute-start.8 = (bf16[256,512]{1,0:T(8,128)(2,1)S(1)}, bf16[256,512]{1,0:T(8,128)(2,1)S(1)}, u32[]{:S(2)}, u32[]{:S(2)}) collective-permute-start(bf16[256,512]{1,0:T(8,128)(2,1)S(1)} %shard_map.134), channel_id=1, source_target_pairs={{0,0},{8,136},{16,272},{24,408},{32,480},{40,360},{48,240},{56,120... | collective-permute-start | bytes 786440 | tf_op jit(solution)/shard_map/ppermute | solution.py:333
  132.7 1.3 shard_map.136
  134.0 9.5 %all-to-all-start.4 = ((bf16[32,32,128]{2,1,0:T(8,128)(2,1)}), bf16[32,32,128]{2,1,0:T(8,128)(2,1)S(1)}, u32[]{:S(2)}, u32[]{:S(2)}) async-start(bf16[32,32,128]{2,1,0:T(8,128)(2,1)} %bitcast.12), calls=%async_computation.4 | async-start | bytes 524288 | tf_op jit(solution)/shard_map/all_to_all | solution.py:277
  144.4 8.0 %all-to-all-done.4 = bf16[32,32,128]{2,1,0:T(8,128)(2,1)S(1)} async-done(((bf16[32,32,128]{2,1,0:T(8,128)(2,1)}), bf16[32,32,128]{2,1,0:T(8,128)(2,1)S(1)}, u32[]{:S(2)}, u32[]{:S(2)}) %all-to-all-start.4) | async-done | bytes 262176 | tf_op jit(solution)/shard_map/all_to_all | solution.py:277
  (42 shorter events, 11.3 us)
Async XLA Ops:
  0.6 25.0 %copy-start = (s32[8,2]{0,1:T(2,128)S(1)}, s32[8,2]{0,1:T(2,128)}, u32[]{:S(2)}) copy-start(s32[8,2]{0,1:T(2,128)} %param.17) | copy-start | bytes 196
  1.3 0.7 copy-start.5
  2.0 0.9 copy-start.1
  2.9 0.9 copy-start.3
  3.8 15.6 %copy-start.7 = (bf16[2,26,1024]{2,0,1:T(2,128)(2,1)S(1)}, bf16[2,26,1024]{2,0,1:T(2,128)(2,1)}, u32[]{:S(2)}) copy-start(bf16[2,26,1024]{2,0,1:T(2,128)(2,1)} %param.11) | copy-start | bytes 319492
  4.0 15.5 %copy-start.8 = (bf16[2,26,1024]{2,0,1:T(2,128)(2,1)S(1)}, bf16[2,26,1024]{2,0,1:T(2,128)(2,1)}, u32[]{:S(2)}) copy-start(bf16[2,26,1024]{2,0,1:T(2,128)(2,1)} %param.12) | copy-start | bytes 319492
  4.0 30.5 %collective-permute-start = (bf16[256,512]{1,0:T(8,128)(2,1)S(1)}, bf16[256,512]{1,0:T(8,128)(2,1)S(1)}, u32[]{:S(2)}, u32[]{:S(2)}) collective-permute-start(bf16[256,512]{1,0:T(8,128)(2,1)S(1)} %shard_map.129), channel_id=1, source_target_pairs={{0,0},{136,8},{272,16},{408,24},{480,32},{360,40},{240,48},{120,56... | collective-permute-start | bytes 786440 | tf_op jit(solution)/shard_map/ppermute | solution.py:304
  19.5 0.7 copy-start.4
  21.0 13.5 %all-to-all-start = ((bf16[32,32,128]{2,1,0:T(8,128)(2,1)}), bf16[32,32,128]{2,1,0:T(8,128)(2,1)S(1)}, u32[]{:S(2)}, u32[]{:S(2)}) async-start(bf16[32,32,128]{2,1,0:T(8,128)(2,1)} %bitcast.6), calls=%async_computation | async-start | bytes 524288 | tf_op jit(solution)/shard_map/all_to_all | solution.py:277
  35.8 31.0 %copy-start.9 = (s32[8,1024]{1,0:T(8,128)S(1)}, s32[8,1024]{1,0:T(8,128)}, u32[]{:S(2)}) copy-start(s32[8,1024]{1,0:T(8,128)} %param.18) | copy-start | bytes 98308
  35.8 22.1 %all-to-all-start.1 = ((bf16[16,64,128]{2,1,0:T(8,128)(2,1)}), bf16[16,64,128]{2,1,0:T(8,128)(2,1)S(1)}, u32[]{:S(2)}, u32[]{:S(2)}) async-start(bf16[16,64,128]{2,1,0:T(8,128)(2,1)} %bitcast.8), calls=%async_computation.1 | async-start | bytes 524288 | tf_op jit(solution)/shard_map/all_to_all | solution.py:277
  45.1 21.8 %collective-permute-start.4 = (bf16[256,512]{1,0:T(8,128)(2,1)S(1)}, bf16[256,512]{1,0:T(8,128)(2,1)S(1)}, u32[]{:S(2)}, u32[]{:S(2)}) collective-permute-start(bf16[256,512]{1,0:T(8,128)(2,1)S(1)} %collective-permute-done.q0), channel_id=1, source_target_pairs={{0,384},{128,0},{256,128},{384,256},{1,385},{129,1},{257,129},{385... | collective-permute-start | bytes 786440 | tf_op jit(solution)/shard_map/ppermute | solution.py:281
  48.8 18.1 %collective-permute-start.3 = (bf16[256,512]{1,0:T(8,128)(2,1)S(1)}, bf16[256,512]{1,0:T(8,128)(2,1)S(1)}, u32[]{:S(2)}, u32[]{:S(2)}) collective-permute-start(bf16[256,512]{1,0:T(8,128)(2,1)S(1)} %collective-permute-done.q0), channel_id=1, source_target_pairs={{0,256},{128,384},{256,0},{384,128},{1,257},{129,385},{257,1},{385... | collective-permute-start | bytes 786440 | tf_op jit(solution)/shard_map/ppermute | solution.py:281
  52.4 14.4 %collective-permute-start.2 = (bf16[256,512]{1,0:T(8,128)(2,1)S(1)}, bf16[256,512]{1,0:T(8,128)(2,1)S(1)}, u32[]{:S(2)}, u32[]{:S(2)}) collective-permute-start(bf16[256,512]{1,0:T(8,128)(2,1)S(1)} %collective-permute-done.q0), channel_id=1, source_target_pairs={{0,128},{128,256},{256,384},{384,0},{1,129},{129,257},{257,385},{3... | collective-permute-start | bytes 786440 | tf_op jit(solution)/shard_map/ppermute | solution.py:281
  57.8 10.0 %collective-permute-start.1 = (bf16[1024,128]{1,0:T(8,128)(2,1)S(1)}, bf16[1024,128]{1,0:T(8,128)(2,1)S(1)}, u32[]{:S(2)}, u32[]{:S(2)}) collective-permute-start(bf16[1024,128]{1,0:T(8,128)(2,1)S(1)} %bitcast.18), channel_id=1, source_target_pairs={{0,64},{64,0},{1,65},{65,1},{2,66},{66,2},{3,67},{67,3},{4,68},{68... | collective-permute-start | bytes 786440 | tf_op jit(solution)/shard_map/ppermute | solution.py:285
  66.8 1.1 copy-start.6
  90.9 4.8 %collective-permute-start.9 = (bf16[1024,128]{1,0:T(8,128)(2,1)S(1)}, bf16[1024,128]{1,0:T(8,128)(2,1)S(1)}, u32[]{:S(2)}, u32[]{:S(2)}) collective-permute-start(bf16[1024,128]{1,0:T(8,128)(2,1)S(1)} %get-tuple-element.35), channel_id=1, source_target_pairs={{0,64},{64,0},{1,65},{65,1},{2,66},{66,2},{3,67},{67,3},{4,68},{68... | collective-permute-start | bytes 786440 | tf_op jit(solution)/shard_map/ppermute | solution.py:285
  96.5 36.1 %all-to-all-start.3 = ((bf16[16,64,128]{2,1,0:T(8,128)(2,1)}), bf16[16,64,128]{2,1,0:T(8,128)(2,1)S(1)}, u32[]{:S(2)}, u32[]{:S(2)}) async-start(bf16[16,64,128]{2,1,0:T(8,128)(2,1)} %bitcast.10), calls=%async_computation.3 | async-start | bytes 524288 | tf_op jit(solution)/shard_map/all_to_all | solution.py:277
  104.8 9.1 %collective-permute-start.5 = (bf16[256,512]{1,0:T(8,128)(2,1)S(1)}, bf16[256,512]{1,0:T(8,128)(2,1)S(1)}, u32[]{:S(2)}, u32[]{:S(2)}) collective-permute-start(bf16[256,512]{1,0:T(8,128)(2,1)S(1)} %get-tuple-element.29), channel_id=1, source_target_pairs={{0,384},{128,0},{256,128},{384,256},{1,385},{129,1},{257,129},{385... | collective-permute-start | bytes 786440 | tf_op jit(solution)/shard_map/ppermute | solution.py:281
  107.6 10.3 %collective-permute-start.6 = (bf16[256,512]{1,0:T(8,128)(2,1)S(1)}, bf16[256,512]{1,0:T(8,128)(2,1)S(1)}, u32[]{:S(2)}, u32[]{:S(2)}) collective-permute-start(bf16[256,512]{1,0:T(8,128)(2,1)S(1)} %get-tuple-element.30), channel_id=1, source_target_pairs={{0,256},{128,384},{256,0},{384,128},{1,257},{129,385},{257,1},{385... | collective-permute-start | bytes 786440 | tf_op jit(solution)/shard_map/ppermute | solution.py:281
  110.7 14.1 %collective-permute-start.7 = (bf16[256,512]{1,0:T(8,128)(2,1)S(1)}, bf16[256,512]{1,0:T(8,128)(2,1)S(1)}, u32[]{:S(2)}, u32[]{:S(2)}) collective-permute-start(bf16[256,512]{1,0:T(8,128)(2,1)S(1)} %get-tuple-element.31), channel_id=1, source_target_pairs={{0,128},{128,256},{256,384},{384,0},{1,129},{129,257},{257,385},{3... | collective-permute-start | bytes 786440 | tf_op jit(solution)/shard_map/ppermute | solution.py:281
  125.0 18.5 %collective-permute-start.8 = (bf16[256,512]{1,0:T(8,128)(2,1)S(1)}, bf16[256,512]{1,0:T(8,128)(2,1)S(1)}, u32[]{:S(2)}, u32[]{:S(2)}) collective-permute-start(bf16[256,512]{1,0:T(8,128)(2,1)S(1)} %shard_map.134), channel_id=1, source_target_pairs={{0,0},{8,136},{16,272},{24,408},{32,480},{40,360},{48,240},{56,120... | collective-permute-start | bytes 786440 | tf_op jit(solution)/shard_map/ppermute | solution.py:333
  134.0 9.5 %copy-start.2 = (bf16[1,128,512]{2,1,0:T(8,128)(2,1)S(1)}, bf16[1,128,512]{2,1,0:T(8,128)(2,1)}, u32[]{:S(2)}) copy-start(bf16[1,128,512]{2,1,0:T(8,128)(2,1)} %queries_ref.3) | copy-start | bytes 393220
  134.0 18.4 %all-to-all-start.4 = ((bf16[32,32,128]{2,1,0:T(8,128)(2,1)}), bf16[32,32,128]{2,1,0:T(8,128)(2,1)S(1)}, u32[]{:S(2)}, u32[]{:S(2)}) async-start(bf16[32,32,128]{2,1,0:T(8,128)(2,1)} %bitcast.12), calls=%async_computation.4 | async-start | bytes 524288 | tf_op jit(solution)/shard_map/all_to_all | solution.py:277

commit v3 on v2

--- a/solution.py
+++ b/solution.py
@@ -29,9 +29,10 @@
     return jnp.dot(a, b, preferred_element_type=F32)
 
 
-def call(kernel, outs, *args, smem=0, scratch=(), flops=0, limit=8 << 20):
+def call(kernel, outs, *args, smem=0, hbm=0, scratch=(), flops=0, limit=8 << 20):
     specs = [pl.BlockSpec(memory_space=pltpu.SMEM)] * smem
-    specs += [pl.BlockSpec(memory_space=pltpu.VMEM)] * (len(args) - smem)
+    specs += [pl.BlockSpec(memory_space=pltpu.HBM)] * hbm
+    specs += [pl.BlockSpec(memory_space=pltpu.VMEM)] * (len(args) - smem - hbm)
     size = sum(a.size * a.dtype.itemsize for a in args) + sum(o.size * o.dtype.itemsize for o in outs)
     return pl.pallas_call(
         kernel,
@@ -48,19 +49,33 @@
     return jax.ShapeDtypeStruct(dims, dtype)
 
 
-def pack_queries(gate_ref, queries_ref, d_out_ref, gain_ref, out_ref):
-    gain = gain_ref[...]
-    gate = gate_ref[0]
+def gate_value(gate_ref):
+    return jnp.tanh(jnp.full((1, HD), gate_ref[0], F32))
+
+
+def pack_queries(gate_ref, queries_ref, d_out_ref, q_gain_ref, k_gain_ref, out_ref, gains_ref, x_s, d_s, sems):
+    copies = [
+        pltpu.make_async_copy(source, target, sems.at[i])
+        for i, (source, target) in enumerate(
+            ((queries_ref.at[0], x_s), (d_out_ref.at[0], d_s), (q_gain_ref, gains_ref.at[0:1]), (k_gain_ref, gains_ref.at[1:2]))
+        )
+    ]
+    for copy in copies:
+        copy.start()
+    gate = gate_value(gate_ref)
+    for copy in copies:
+        copy.wait()
+    gain = gains_ref[0:1]
     for g in range(4):
         lanes = slice(g * HD, (g + 1) * HD)
-        x = queries_ref[0, :, lanes].astype(F32)
+        x = x_s[:, lanes].astype(F32)
         mean_square = jnp.mean(x * x, axis=-1, keepdims=True)
         out_ref[0:128, lanes] = (x * lax.rsqrt(mean_square + EPSILON) * gain).astype(BF16)
-    out_ref[128:256, :] = (gate * d_out_ref[0].astype(F32)).astype(BF16)
-
-
-def pack_keys(keys_ref, values_ref, gain_ref, out_ref):
-    gain = gain_ref[...]
+        out_ref[128:256, lanes] = (gate * d_s[:, lanes].astype(F32)).astype(BF16)
+
+
+def pack_keys(keys_ref, values_ref, gains_ref, out_ref):
+    gain = gains_ref[1:2]
     for n in range(2):
         for head in range(8):
             hhi, hx = divmod(head, 4)
@@ -97,8 +112,8 @@
             out_ref[o, :, hhi * HALF : (hhi + 1) * HALF, :] = chunk.reshape(4, HALF, HD)
 
 
-def row_mask(half):
-    position = lax.broadcasted_iota(jnp.int32, (MID, HD), 0)
+def row_mask(half, dims, axis):
+    position = lax.broadcasted_iota(jnp.int32, dims, axis)
     thi, s, tx, i = position >> 9, (position >> 6) & 7, (position >> 4) & 3, position & 15
     inside = half * HALF + i
     row = s * (8 * ROWS) + (thi * 4 + tx) * ROWS + inside
@@ -126,13 +141,11 @@
     return jnp.concatenate([seen] * 4, axis=1)
 
 
-def masked_weights(keys_s, ok_s, q_t, rows):
-    scores = dot(keys_s[rows, :], q_t)
-    ok = ok_s[rows, :]
-    return jnp.exp2(scores * SCALE_LOG2) * jnp.concatenate([ok] * 4, axis=1)
-
-
-def load_pair(ids_ref, mine_ref, other_ref, keys_s, values_s, ok_s):
+def weights_of(keys_s, q_t, rows):
+    return jnp.exp2(dot(keys_s[rows, :], q_t) * SCALE_LOG2)
+
+
+def load_pair(ids_ref, mine_ref, other_ref, keys_s, values_s):
     core = ids_ref[1]
 
     @pl.when(core == 0)
@@ -145,31 +158,29 @@
         keys_s[...] = other_ref[...]
         values_s[...] = mine_ref[...]
 
-    ok_s[...] = row_mask(ids_ref[0] & 1)
-
-
-def forward(ids_ref, count_ref, visible_ref, mine_ref, other_ref, q0, q1, q2, q3, acc_ref, sums_ref, keys_s, values_s, ok_s, turned_s, q_s):
-    load_pair(ids_ref, mine_ref, other_ref, keys_s, values_s, ok_s)
-    turned_s[...] = values_s[...].astype(F32).T.astype(BF16)
+    return row_mask(ids_ref[0] & 1, (MID, HD), 0)
+
+
+def forward(ids_ref, count_ref, visible_ref, mine_ref, other_ref, q0, q1, q2, q3, acc_ref, sums_ref, keys_s, values_s, turned_s, q_s):
+    ok = load_pair(ids_ref, mine_ref, other_ref, keys_s, values_s)
+    keys_s[...] = (keys_s[...].astype(F32) * ok).astype(BF16)
+    turned_s[0:HD, :] = (values_s[...].astype(F32) * ok).T.astype(BF16)
+    turned_s[HD:, :] = row_mask(ids_ref[0] & 1, (16, MID), 1).astype(BF16)
     for j, q in enumerate((q0, q1, q2, q3)):
         q_s[j] = q[...]
 
     def block(j, carry):
         q_t = columns(q_s[j, 0:128, :]).astype(BF16)
         o_t = columns(q_s[j, 128:256, :])
-        total = jnp.zeros((1, 512), F32)
-        acc = jnp.zeros((HD, 512), F32)
+        acc = jnp.zeros((HD + 16, 512), F32)
         for r in range(MID // CHUNK):
             rows = slice(r * CHUNK, (r + 1) * CHUNK)
-            weights = masked_weights(keys_s, ok_s, q_t, rows)
-            total = total + jnp.sum(weights, axis=0, keepdims=True)
-            acc = acc + dot(turned_s[:, rows], weights.astype(BF16))
-        seen = seen_row(ids_ref, count_ref, visible_ref, j)
-        acc = acc * seen
-        both = jnp.concatenate([total * seen, jnp.sum(acc * o_t, axis=0, keepdims=True)], axis=0)
+            acc = acc + dot(turned_s[:, rows], weights_of(keys_s, q_t, rows).astype(BF16))
+        acc = acc * seen_row(ids_ref, count_ref, visible_ref, j)
+        both = jnp.concatenate([acc[HD : HD + 1], jnp.sum(acc[:HD] * o_t, axis=0, keepdims=True)], axis=0)
         for to in range(Y):
             sums_ref[to, j] = both
-        acc_ref[j] = acc
+        acc_ref[j] = acc[:HD]
         return carry
 
     lax.fori_loop(0, Y, block, 0)
@@ -187,10 +198,12 @@
 
 def backward(
     ids_ref, count_ref, visible_ref, mine_ref, other_ref, q0, q1, q2, q3, acc_ref, sums_ref,
-    r0, r1, r2, r3, keep_ref, send_ref, keys_s, values_s, ok_s, turned_s, q_s, dk_s, dv_s,
+    r0, r1, r2, r3, keep_ref, send_ref, keys_s, values_s, turned_s, q_s, dk_s, dv_s,
 ):
-    load_pair(ids_ref, mine_ref, other_ref, keys_s, values_s, ok_s)
-    turned_s[...] = keys_s[...].astype(F32).T.astype(BF16)
+    ok = load_pair(ids_ref, mine_ref, other_ref, keys_s, values_s)
+    masked = keys_s[...].astype(F32) * ok
+    keys_s[...] = masked.astype(BF16)
+    turned_s[...] = masked.T.astype(BF16)
     dk_s[...] = jnp.zeros((MID, HD), F32)
     dv_s[...] = jnp.zeros((MID, HD), F32)
     for j, q in enumerate((q0, q1, q2, q3)):
@@ -207,7 +220,7 @@
         dq = jnp.zeros((HD, 512), F32)
         for r in range(MID // CHUNK):
             rows = slice(r * CHUNK, (r + 1) * CHUNK)
-            prob = masked_weights(keys_s, ok_s, q_t, rows) * inverse
+            prob = weights_of(keys_s, q_t, rows) * inverse
             d_prob = dot(values_s[rows, :], o_t)
             d_score = (prob * (d_prob - delta)).astype(BF16)
             dk_s[rows, :] += dot(d_score, q_rows)
@@ -223,20 +236,21 @@
 
     @pl.when(core == 0)
     def _():
-        keep_ref[...] = dk_s[...] * SCALE
-        send_ref[...] = dv_s[...].astype(BF16)
+        keep_ref[...] = dk_s[...] * (ok * SCALE)
+        send_ref[...] = (dv_s[...] * ok).astype(BF16)
 
     @pl.when(core != 0)
     def _():
-        keep_ref[...] = dv_s[...]
-        send_ref[...] = (dk_s[...] * SCALE).astype(BF16)
+        keep_ref[...] = dv_s[...] * ok
+        send_ref[...] = (dk_s[...] * (ok * SCALE)).astype(BF16)
 
 
 def sum_tokens(gate_ref, r0, r1, r2, r3, out_ref):
+    gate = gate_value(gate_ref)
     both = r0[...].astype(F32) + r1[...].astype(F32) + r2[...].astype(F32) + r3[...].astype(F32)
     for g in range(4):
         lanes = slice(g * HD, (g + 1) * HD)
-        out_ref[0:128, lanes] = (both[0:128, lanes].T * gate_ref[0]).astype(BF16)
+        out_ref[0:128, lanes] = (both[0:128, lanes].T * gate).astype(BF16)
         out_ref[128:256, lanes] = both[128:256, lanes].T.astype(BF16)
 
 
@@ -248,8 +262,8 @@
     return inverse * scaled - x * (inverse * inverse * inverse * dots)
 
 
-def finish_queries(queries_ref, got_ref, gain_ref, attended_ref, out_ref):
-    gain = gain_ref[...]
+def finish_queries(queries_ref, got_ref, gains_ref, attended_ref, out_ref):
+    gain = gains_ref[0:1]
     attended_ref[0] = got_ref[0:128, :]
     for g in range(4):
         lanes = slice(g * HD, (g + 1) * HD)
@@ -257,8 +271,8 @@
         out_ref[0, :, lanes] = norm_back(x, got_ref[128:256, lanes].astype(F32), gain).astype(BF16)
 
 
-def finish_keys(keys_ref, got_ref, gain_ref, dk_ref, dv_ref):
-    gain = gain_ref[...]
+def finish_keys(keys_ref, got_ref, gains_ref, dk_ref, dv_ref):
+    gain = gains_ref[1:2]
     for n in range(2):
         for head in range(8):
             hhi, hx = divmod(head, 4)
@@ -293,16 +307,20 @@
 def shards(queries, keys, values, q_gain, k_gain, gate, tile_count, tile_owner, visible, d_out):
     y, core, z = lax.axis_index("y"), lax.axis_index("core"), lax.axis_index("seq")
     ids = jnp.stack([y, core, z]).astype(jnp.int32)
-    gate_value = jnp.tanh(gate)
     q_gain = q_gain.reshape(1, HD)
     k_gain = k_gain.reshape(1, HD)
     owner = lax.dynamic_index_in_dim(tile_owner, y // 2, 1, keepdims=False)
     seen = visible.reshape(64, 128)
 
-    (packed,) = call(pack_queries, [shape((256, 512), BF16)], gate_value, queries, d_out, q_gain, smem=1)
-    packed, keys, values = lax.optimization_barrier((packed, keys, values))
+    buffers = [pltpu.VMEM((128, 512), BF16), pltpu.VMEM((128, 512), BF16), pltpu.SemaphoreType.DMA((4,))]
+    packed, gains = call(
+        pack_queries,
+        [shape((256, 512), BF16), shape((2, HD), F32)],
+        gate, queries, d_out, q_gain, k_gain,
+        smem=1, hbm=4, scratch=buffers, limit=60 << 20,
+    )
     q0 = lax.ppermute(packed, PLANES, TO_PLANE)
-    (packed_kv,) = call(pack_keys, [shape((8, 4, 32, HD), BF16)], keys, values, k_gain)
+    (packed_kv,) = call(pack_keys, [shape((8, 4, 32, HD), BF16)], keys, values, gains)
     got = exchange(packed_kv.reshape(32, 32, HD), ("y", "core", "x"))
     got, q0 = lax.optimization_barrier((got, q0))
     (chosen,) = call(choose_tiles, [shape((2, 8, 64, HD), BF16)], owner, got.reshape(8, 4, 32, HD), smem=1)
@@ -310,31 +328,33 @@
     q1, q2, q3 = rotated(q0, 1), rotated(q0, 2), rotated(q0, 3)
     other = swapped(mine)
 
-    common = [pltpu.VMEM((MID, HD), BF16), pltpu.VMEM((MID, HD), BF16), pltpu.VMEM((MID, HD), F32)]
-    common += [pltpu.VMEM((HD, MID), BF16), pltpu.VMEM((Y, 256, 512), BF16)]
+    pair = [pltpu.VMEM((MID, HD), BF16), pltpu.VMEM((MID, HD), BF16)]
+    tokens = pltpu.VMEM((Y, 256, 512), BF16)
+    gradients = [pltpu.VMEM((MID, HD), F32), pltpu.VMEM((MID, HD), F32)]
     acc, sums = call(
         forward,
         [shape((Y, HD, 512), F32), shape((Y, Y, 2, 512), F32)],
         ids, tile_count, seen, mine, other, q0, q1, q2, q3,
-        smem=2, scratch=common, flops=2 * 2 * 2048 * MID * HD, limit=32 << 20,
+        smem=2, scratch=pair + [pltpu.VMEM((HD + 16, MID), BF16), tokens], flops=2 * 2 * 2048 * MID * HD, limit=32 << 20,
     )
     sums = exchange(sums, "y")
     r0, r1, r2, r3, keep, send = call(
         backward,
         [shape((256, 512), BF16)] * 4 + [shape((MID, HD), F32), shape((MID, HD), BF16)],
         ids, tile_count, seen, mine, other, q0, q1, q2, q3, acc, sums,
-        smem=2, scratch=common + [pltpu.VMEM((MID, HD), F32)] * 2, flops=5 * 2 * 2048 * MID * HD, limit=32 << 20,
+        smem=2, scratch=pair + [pltpu.VMEM((HD, MID), BF16), tokens] + gradients, flops=5 * 2 * 2048 * MID * HD, limit=32 << 20,
     )
 
     grads = (keep + swapped(send).astype(F32)).astype(BF16)
     back = exchange(grads.reshape(16, 64, HD), ("zhi", "seq"))
     r1, r2, r3 = rotated(r1, 3), rotated(r2, 2), rotated(r3, 1)
-    (summed,) = call(sum_tokens, [shape((256, 512), BF16)], gate_value, r0, r1, r2, r3, smem=1)
-    summed = lax.ppermute(summed, PLANES, FROM_PLANE)
     (placed,) = call(return_tiles, [shape((8, 4, 32, HD), BF16)], owner, back.reshape(2, 8, 64, HD), smem=1)
     home = exchange(placed.reshape(32, 32, HD), ("y", "core", "x")).reshape(8, 4, 32, HD)
-    d_keys, d_values = call(finish_keys, [shape(keys.shape, BF16), shape(values.shape, BF16)], keys, home, k_gain)
-    attended, d_queries = call(finish_queries, [shape(queries.shape, BF16)] * 2, queries, summed, q_gain)
+    r1, r2, r3, placed = lax.optimization_barrier((r1, r2, r3, placed))
+    (summed,) = call(sum_tokens, [shape((256, 512), BF16)], gate, r0, r1, r2, r3, smem=1)
+    summed = lax.ppermute(summed, PLANES, FROM_PLANE)
+    d_keys, d_values = call(finish_keys, [shape(keys.shape, BF16), shape(values.shape, BF16)], keys, home, gains)
+    attended, d_queries = call(finish_queries, [shape(queries.shape, BF16)] * 2, queries, summed, gains)
     return (attended, d_queries, d_keys, d_values)
 
 

time: 155 us -> 154 us (level)
  blocking collectives: 8.77 us -> 26.7 us
  starting transfers between devices: 84.9 us -> 75.7 us
  waiting for transfers between devices: 34 us -> 25.4 us
  local copies, waits for them, and re-layouts: 4.71 us -> 2.42 us
    all_to_all x1 -> x2, blocking collectives: 8.77 us -> 26.7 us  [exchange(): return lax.all_to_all(value, axes, split_axis=0, concat_axis=0, tiled=True)]
    all_to_all x4 -> x3, starting transfers between devices: 31.6 us -> 22.4 us  [exchange(): return lax.all_to_all(value, axes, split_axis=0, concat_axis=0, tiled=True)]
    ppermute x6, waiting for transfers between devices: 12.2 us -> 5.34 us  [rotated(): return lax.ppermute(value, 'y', [(i, (i + k) % Y) for i in range(Y)])]
    unnamed x22 -> x18, local copies, waits for them, and re-layouts: 4.65 us -> 2.4 us
    all_to_all x4 -> x3, waiting for transfers between devices: 19.7 us -> 17.9 us  [exchange(): return lax.all_to_all(value, axes, split_axis=0, concat_axis=0, tiled=True)]
  transfers between devices with their start and end apart: 14 -> 13, of which waited for: 8 -> 6; matrix products, arithmetic and copies ran while one was open for 0% -> 1% of each run, Pallas kernels for 2% -> 1%
where the time goes in v3:
time: 154 us; the launch traced here: 153 us
  starting transfers between devices  75.7 us (49%)
  blocking collectives  26.7 us (17%)
  waiting for transfers between devices  25.4 us (16%)
  Pallas kernels  20 us (13%)
  local copies, waits for them, and re-layouts  2.42 us (2%)
  between operations  1.59 us (1%)
    all_to_all x2, blocking collectives, exchange(): return lax.all_to_all(value, axes, split_axis=0, concat_axis=0, tiled=True)  26.7 us
    all_to_all x3, starting transfers between devices, exchange(): return lax.all_to_all(value, axes, split_axis=0, concat_axis=0, tiled=True)  22.4 us
    pallas_call x9, Pallas kernels, call(): pl.pallas_call(kernel, out_shape=outs, in_specs=specs, out_specs=[pl.Bloc...  20 us
    all_to_all x3, waiting for transfers between devices, exchange(): return lax.all_to_all(value, axes, split_axis=0, concat_axis=0, tiled=True)  17.9 us
    ppermute x6, starting transfers between devices, rotated(): return lax.ppermute(value, 'y', [(i, (i + k) % Y) for i in range(Y)])  17.7 us
    ppermute x1, starting transfers between devices, shards(): q0 = lax.ppermute(packed, PLANES, TO_PLANE)  15.4 us
    ppermute x2, starting transfers between devices, swapped(): return lax.ppermute(value, 'core', [(0, 1), (1, 0)])  12.6 us
    ppermute x1, starting transfers between devices, shards(): summed = lax.ppermute(summed, PLANES, FROM_PLANE)  7.61 us
  transfers between devices with their start and end apart: 13, of which 6 were waited for; matrix products, arithmetic and copies ran while one was open for 1% of the time, Pallas kernels for 1%

profile of v3, /device:TPU:1, one launch (start us, length us, event | category | flops | bytes accessed | tf_op | source)
XLA Modules:
  0.0 152.7 jit_solution(3705089033869765132)
XLA Ops:
  1.3 1.9 %shard_map.129 = (bf16[256,512]{1,0:T(8,128)(2,1)}, f32[2,128]{1,0:T(2,128)}) custom-call(f32[1]{0:T(128)S(6)} %copy.19.gate_ref, bf16[1,128,512]{2,1,0:T(8,128)(2,1)} %queries_ref.3, bf16[1,128,512]{2,1,0:T(8,128)(2,1)} %d_out_ref.1, f32[1,128]{1,0:T(1,128)} %bitcast.22, f32[1,128]{1,0:T(1,128)} %bitcast.23), custom_call_target="tpu_custom_call" | custom-call | bytes 526340 | tf_op jit(solution)/shard_map/pallas_call | solution.py:37
  3.2 15.4 %collective-permute-start = (bf16[256,512]{1,0:T(8,128)(2,1)}, bf16[256,512]{1,0:T(8,128)(2,1)S(1)}, u32[]{:S(2)}, u32[]{:S(2)}) collective-permute-start(bf16[256,512]{1,0:T(8,128)(2,1)} %get-tuple-element.24), channel_id=1, source_target_pairs={{0,0},{136,8},{272,16},{408,24},{480,32},{360,40},{240,48},{120,56... | collective-permute-start | bytes 786440 | tf_op jit(solution)/shard_map/ppermute | solution.py:322
  20.3 4.6 %all-to-all-start = ((bf16[32,32,128]{2,1,0:T(8,128)(2,1)}), bf16[32,32,128]{2,1,0:T(8,128)(2,1)S(1)}, u32[]{:S(2)}, u32[]{:S(2)}) async-start(bf16[32,32,128]{2,1,0:T(8,128)(2,1)} %bitcast.6), calls=%async_computation | async-start | bytes 524288 | tf_op jit(solution)/shard_map/all_to_all | solution.py:291
  24.9 8.8 %all-to-all-done = bf16[32,32,128]{2,1,0:T(8,128)(2,1)S(1)} async-done(((bf16[32,32,128]{2,1,0:T(8,128)(2,1)}), bf16[32,32,128]{2,1,0:T(8,128)(2,1)S(1)}, u32[]{:S(2)}, u32[]{:S(2)}) %all-to-all-start) | async-done | bytes 262176 | tf_op jit(solution)/shard_map/all_to_all | solution.py:291
  33.8 1.3 shard_map.131
  35.0 9.5 %all-to-all-start.1 = ((bf16[16,64,128]{2,1,0:T(8,128)(2,1)}), bf16[16,64,128]{2,1,0:T(8,128)(2,1)S(1)}, u32[]{:S(2)}, u32[]{:S(2)}) async-start(bf16[16,64,128]{2,1,0:T(8,128)(2,1)} %bitcast.8), calls=%async_computation.1 | async-start | bytes 524288 | tf_op jit(solution)/shard_map/all_to_all | solution.py:291
  44.5 3.7 %collective-permute-start.4 = (bf16[256,512]{1,0:T(8,128)(2,1)S(1)}, bf16[256,512]{1,0:T(8,128)(2,1)S(1)}, u32[]{:S(2)}, u32[]{:S(2)}) collective-permute-start(bf16[256,512]{1,0:T(8,128)(2,1)S(1)} %collective-permute-done.q0), channel_id=1, source_target_pairs={{0,384},{128,0},{256,128},{384,256},{1,385},{129,1},{257,129},{385... | collective-permute-start | bytes 786440 | tf_op jit(solution)/shard_map/ppermute | solution.py:295
  48.2 3.7 %collective-permute-start.3 = (bf16[256,512]{1,0:T(8,128)(2,1)S(1)}, bf16[256,512]{1,0:T(8,128)(2,1)S(1)}, u32[]{:S(2)}, u32[]{:S(2)}) collective-permute-start(bf16[256,512]{1,0:T(8,128)(2,1)S(1)} %collective-permute-done.q0), channel_id=1, source_target_pairs={{0,256},{128,384},{256,0},{384,128},{1,257},{129,385},{257,1},{385... | collective-permute-start | bytes 786440 | tf_op jit(solution)/shard_map/ppermute | solution.py:295
  51.9 2.5 %collective-permute-start.2 = (bf16[256,512]{1,0:T(8,128)(2,1)S(1)}, bf16[256,512]{1,0:T(8,128)(2,1)S(1)}, u32[]{:S(2)}, u32[]{:S(2)}) collective-permute-start(bf16[256,512]{1,0:T(8,128)(2,1)S(1)} %collective-permute-done.q0), channel_id=1, source_target_pairs={{0,128},{128,256},{256,384},{384,0},{1,129},{129,257},{257,385},{3... | collective-permute-start | bytes 786440 | tf_op jit(solution)/shard_map/ppermute | solution.py:295
  54.4 2.9 %all-to-all-done.1 = bf16[16,64,128]{2,1,0:T(8,128)(2,1)S(1)} async-done(((bf16[16,64,128]{2,1,0:T(8,128)(2,1)}), bf16[16,64,128]{2,1,0:T(8,128)(2,1)S(1)}, u32[]{:S(2)}, u32[]{:S(2)}) %all-to-all-start.1) | async-done | bytes 262176 | tf_op jit(solution)/shard_map/all_to_all | solution.py:291
  57.3 8.9 %collective-permute-start.1 = (bf16[1024,128]{1,0:T(8,128)(2,1)S(1)}, bf16[1024,128]{1,0:T(8,128)(2,1)S(1)}, u32[]{:S(2)}, u32[]{:S(2)}) collective-permute-start(bf16[1024,128]{1,0:T(8,128)(2,1)S(1)} %bitcast.19), channel_id=1, source_target_pairs={{0,64},{64,0},{1,65},{65,1},{2,66},{66,2},{3,67},{67,3},{4,68},{68... | collective-permute-start | bytes 786440 | tf_op jit(solution)/shard_map/ppermute | solution.py:299
  67.4 5.4 %shard_map.132 = (f32[4,128,512]{2,1,0:T(8,128)S(1)}, f32[4,4,2,512]{3,2,1,0:T(2,128)S(1)}) custom-call(s32[3]{0:T(128)S(1)} %pad_add_fusion.ids_ref, s32[8]{0:T(128)S(1)} %copy-done.3, s32[64,128]{1,0:T(8,128)S(1)} %reshape.41.visible_ref, bf16[1024,128]{1,0:T(8,128)(2,1)S(1)} %bitcast.20, bf16[1024,128]{1,0:T(8,128)(2,1)S(1)} %collective-permute-done.1.other_ref, ...), custom_call_target="tpu_custom_call" | custom-call | flops 1073741824 | bytes 2719788 | tf_op jit(solution)/shard_map/pallas_call | solution.py:37
  72.8 8.7 %all_to_all.25.sums_ref = f32[4,4,2,512]{3,2,1,0:T(2,128)S(1)} all-to-all(f32[4,4,2,512]{3,2,1,0:T(2,128)S(1)} %get-tuple-element.28), channel_id=1, replica_groups=mesh['y'=4,'core'=2,'seq'=8,'zhi'=2,'x'=4] {'y'}, dimensions={0} | all-to-all | bytes 131072 | tf_op jit(solution)/shard_map/all_to_all | solution.py:291
  81.4 8.6 %shard_map.133 = (bf16[256,512]{1,0:T(8,128)(2,1)S(1)}, bf16[256,512]{1,0:T(8,128)(2,1)S(1)}, bf16[256,512]{1,0:T(8,128)(2,1)S(1)}, bf16[256,512]{1,0:T(8,128)(2...) custom-call(s32[3]{0:T(128)S(1)} %pad_add_fusion.ids_ref, s32[8]{0:T(128)S(1)} %copy-done.3, ...), custom_call_target="tpu_custom_call" | custom-call | flops 2684354560 | bytes 4554796 | tf_op jit(solution)/shard_map/pallas_call | solution.py:37
  90.1 3.7 %collective-permute-start.8 = (bf16[1024,128]{1,0:T(8,128)(2,1)S(1)}, bf16[1024,128]{1,0:T(8,128)(2,1)S(1)}, u32[]{:S(2)}, u32[]{:S(2)}) collective-permute-start(bf16[1024,128]{1,0:T(8,128)(2,1)S(1)} %get-tuple-element.34), channel_id=1, source_target_pairs={{0,64},{64,0},{1,65},{65,1},{2,66},{66,2},{3,67},{67,3},{4,68},{68... | collective-permute-start | bytes 786440 | tf_op jit(solution)/shard_map/ppermute | solution.py:299
  93.8 1.1 collective-permute-done.8
  95.7 8.3 %all-to-all-start.3 = ((bf16[16,64,128]{2,1,0:T(8,128)(2,1)}), bf16[16,64,128]{2,1,0:T(8,128)(2,1)S(1)}, u32[]{:S(2)}, u32[]{:S(2)}) async-start(bf16[16,64,128]{2,1,0:T(8,128)(2,1)} %bitcast.10), calls=%async_computation.3 | async-start | bytes 524288 | tf_op jit(solution)/shard_map/all_to_all | solution.py:291
  104.0 2.8 %collective-permute-start.5 = (bf16[256,512]{1,0:T(8,128)(2,1)S(1)}, bf16[256,512]{1,0:T(8,128)(2,1)S(1)}, u32[]{:S(2)}, u32[]{:S(2)}) collective-permute-start(bf16[256,512]{1,0:T(8,128)(2,1)S(1)} %get-tuple-element.30), channel_id=1, source_target_pairs={{0,384},{128,0},{256,128},{384,256},{1,385},{129,1},{257,129},{385... | collective-permute-start | bytes 786440 | tf_op jit(solution)/shard_map/ppermute | solution.py:295
  106.8 3.1 %collective-permute-start.6 = (bf16[256,512]{1,0:T(8,128)(2,1)S(1)}, bf16[256,512]{1,0:T(8,128)(2,1)S(1)}, u32[]{:S(2)}, u32[]{:S(2)}) collective-permute-start(bf16[256,512]{1,0:T(8,128)(2,1)S(1)} %get-tuple-element.31), channel_id=1, source_target_pairs={{0,256},{128,384},{256,0},{384,128},{1,257},{129,385},{257,1},{385... | collective-permute-start | bytes 786440 | tf_op jit(solution)/shard_map/ppermute | solution.py:295
  109.9 1.9 %collective-permute-start.7 = (bf16[256,512]{1,0:T(8,128)(2,1)S(1)}, bf16[256,512]{1,0:T(8,128)(2,1)S(1)}, u32[]{:S(2)}, u32[]{:S(2)}) collective-permute-start(bf16[256,512]{1,0:T(8,128)(2,1)S(1)} %get-tuple-element.32), channel_id=1, source_target_pairs={{0,128},{128,256},{256,384},{384,0},{1,129},{129,257},{257,385},{3... | collective-permute-start | bytes 786440 | tf_op jit(solution)/shard_map/ppermute | solution.py:295
  111.9 6.2 %all-to-all-done.3 = bf16[16,64,128]{2,1,0:T(8,128)(2,1)S(1)} async-done(((bf16[16,64,128]{2,1,0:T(8,128)(2,1)}), bf16[16,64,128]{2,1,0:T(8,128)(2,1)S(1)}, u32[]{:S(2)}, u32[]{:S(2)}) %all-to-all-start.3) | async-done | bytes 262176 | tf_op jit(solution)/shard_map/all_to_all | solution.py:291
  118.7 5.3 %collective-permute-done.7.r3 = bf16[256,512]{1,0:T(8,128)(2,1)S(1)} collective-permute-done((bf16[256,512]{1,0:T(8,128)(2,1)S(1)}, bf16[256,512]{1,0:T(8,128)(2,1)S(1)}, u32[]{:S(2)}, u32[]{:S(2)}) %collective-permute-start.7) | collective-permute-done | bytes 262176 | tf_op jit(solution)/shard_map/ppermute | solution.py:295
  124.2 7.6 %collective-permute-start.9 = (bf16[256,512]{1,0:T(8,128)(2,1)S(1)}, bf16[256,512]{1,0:T(8,128)(2,1)S(1)}, u32[]{:S(2)}, u32[]{:S(2)}) collective-permute-start(bf16[256,512]{1,0:T(8,128)(2,1)S(1)} %shard_map.135), channel_id=1, source_target_pairs={{0,0},{8,136},{16,272},{24,408},{32,480},{40,360},{48,240},{56,120... | collective-permute-start | bytes 786440 | tf_op jit(solution)/shard_map/ppermute | solution.py:355
  131.9 18.1 %all_to_all.26 = bf16[32,32,128]{2,1,0:T(8,128)(2,1)S(1)} all-to-all(bf16[32,32,128]{2,1,0:T(8,128)(2,1)S(1)} %bitcast.16), channel_id=1, replica_groups=mesh['y'=4,'core'=2,'seq'=8,'zhi'=2,'x'=4] {'y','core','x'}, dimensions={0} | all-to-all | bytes 524288 | tf_op jit(solution)/shard_map/all_to_all | solution.py:291
  (35 shorter events, 7.1 us)
Async XLA Ops:
  0.6 24.2 %copy-start = (s32[8,2]{0,1:T(2,128)S(1)}, s32[8,2]{0,1:T(2,128)}, u32[]{:S(2)}) copy-start(s32[8,2]{0,1:T(2,128)} %param.17) | copy-start | bytes 196
  1.3 17.4 %copy-start.4 = (bf16[2,26,1024]{2,0,1:T(2,128)(2,1)S(1)}, bf16[2,26,1024]{2,0,1:T(2,128)(2,1)}, u32[]{:S(2)}) copy-start(bf16[2,26,1024]{2,0,1:T(2,128)(2,1)} %param.11) | copy-start | bytes 319492
  3.2 15.5 %copy-start.5 = (bf16[2,26,1024]{2,0,1:T(2,128)(2,1)S(1)}, bf16[2,26,1024]{2,0,1:T(2,128)(2,1)}, u32[]{:S(2)}) copy-start(bf16[2,26,1024]{2,0,1:T(2,128)(2,1)} %param.12) | copy-start | bytes 319492
  3.2 30.5 %collective-permute-start = (bf16[256,512]{1,0:T(8,128)(2,1)}, bf16[256,512]{1,0:T(8,128)(2,1)S(1)}, u32[]{:S(2)}, u32[]{:S(2)}) collective-permute-start(bf16[256,512]{1,0:T(8,128)(2,1)} %get-tuple-element.24), channel_id=1, source_target_pairs={{0,0},{136,8},{272,16},{408,24},{480,32},{360,40},{240,48},{120,56... | collective-permute-start | bytes 786440 | tf_op jit(solution)/shard_map/ppermute | solution.py:322
  18.7 0.7 copy-start.2
  20.3 13.5 %all-to-all-start = ((bf16[32,32,128]{2,1,0:T(8,128)(2,1)}), bf16[32,32,128]{2,1,0:T(8,128)(2,1)S(1)}, u32[]{:S(2)}, u32[]{:S(2)}) async-start(bf16[32,32,128]{2,1,0:T(8,128)(2,1)} %bitcast.6), calls=%async_computation | async-start | bytes 524288 | tf_op jit(solution)/shard_map/all_to_all | solution.py:291
  35.0 31.2 %copy-start.6 = (s32[8,1024]{1,0:T(8,128)S(1)}, s32[8,1024]{1,0:T(8,128)}, u32[]{:S(2)}) copy-start(s32[8,1024]{1,0:T(8,128)} %param.18) | copy-start | bytes 98308
  35.0 22.3 %all-to-all-start.1 = ((bf16[16,64,128]{2,1,0:T(8,128)(2,1)}), bf16[16,64,128]{2,1,0:T(8,128)(2,1)S(1)}, u32[]{:S(2)}, u32[]{:S(2)}) async-start(bf16[16,64,128]{2,1,0:T(8,128)(2,1)} %bitcast.8), calls=%async_computation.1 | async-start | bytes 524288 | tf_op jit(solution)/shard_map/all_to_all | solution.py:291
  44.5 21.8 %collective-permute-start.4 = (bf16[256,512]{1,0:T(8,128)(2,1)S(1)}, bf16[256,512]{1,0:T(8,128)(2,1)S(1)}, u32[]{:S(2)}, u32[]{:S(2)}) collective-permute-start(bf16[256,512]{1,0:T(8,128)(2,1)S(1)} %collective-permute-done.q0), channel_id=1, source_target_pairs={{0,384},{128,0},{256,128},{384,256},{1,385},{129,1},{257,129},{385... | collective-permute-start | bytes 786440 | tf_op jit(solution)/shard_map/ppermute | solution.py:295
  48.2 18.1 %collective-permute-start.3 = (bf16[256,512]{1,0:T(8,128)(2,1)S(1)}, bf16[256,512]{1,0:T(8,128)(2,1)S(1)}, u32[]{:S(2)}, u32[]{:S(2)}) collective-permute-start(bf16[256,512]{1,0:T(8,128)(2,1)S(1)} %collective-permute-done.q0), channel_id=1, source_target_pairs={{0,256},{128,384},{256,0},{384,128},{1,257},{129,385},{257,1},{385... | collective-permute-start | bytes 786440 | tf_op jit(solution)/shard_map/ppermute | solution.py:295
  51.9 14.5 %collective-permute-start.2 = (bf16[256,512]{1,0:T(8,128)(2,1)S(1)}, bf16[256,512]{1,0:T(8,128)(2,1)S(1)}, u32[]{:S(2)}, u32[]{:S(2)}) collective-permute-start(bf16[256,512]{1,0:T(8,128)(2,1)S(1)} %collective-permute-done.q0), channel_id=1, source_target_pairs={{0,128},{128,256},{256,384},{384,0},{1,129},{129,257},{257,385},{3... | collective-permute-start | bytes 786440 | tf_op jit(solution)/shard_map/ppermute | solution.py:295
  57.3 10.1 %collective-permute-start.1 = (bf16[1024,128]{1,0:T(8,128)(2,1)S(1)}, bf16[1024,128]{1,0:T(8,128)(2,1)S(1)}, u32[]{:S(2)}, u32[]{:S(2)}) collective-permute-start(bf16[1024,128]{1,0:T(8,128)(2,1)S(1)} %bitcast.19), channel_id=1, source_target_pairs={{0,64},{64,0},{1,65},{65,1},{2,66},{66,2},{3,67},{67,3},{4,68},{68... | collective-permute-start | bytes 786440 | tf_op jit(solution)/shard_map/ppermute | solution.py:299
  66.2 1.1 copy-start.3
  90.1 4.9 %collective-permute-start.8 = (bf16[1024,128]{1,0:T(8,128)(2,1)S(1)}, bf16[1024,128]{1,0:T(8,128)(2,1)S(1)}, u32[]{:S(2)}, u32[]{:S(2)}) collective-permute-start(bf16[1024,128]{1,0:T(8,128)(2,1)S(1)} %get-tuple-element.34), channel_id=1, source_target_pairs={{0,64},{64,0},{1,65},{65,1},{2,66},{66,2},{3,67},{67,3},{4,68},{68... | collective-permute-start | bytes 786440 | tf_op jit(solution)/shard_map/ppermute | solution.py:299
  95.7 22.3 %all-to-all-start.3 = ((bf16[16,64,128]{2,1,0:T(8,128)(2,1)}), bf16[16,64,128]{2,1,0:T(8,128)(2,1)S(1)}, u32[]{:S(2)}, u32[]{:S(2)}) async-start(bf16[16,64,128]{2,1,0:T(8,128)(2,1)} %bitcast.10), calls=%async_computation.3 | async-start | bytes 524288 | tf_op jit(solution)/shard_map/all_to_all | solution.py:291
  104.0 14.6 %collective-permute-start.5 = (bf16[256,512]{1,0:T(8,128)(2,1)S(1)}, bf16[256,512]{1,0:T(8,128)(2,1)S(1)}, u32[]{:S(2)}, u32[]{:S(2)}) collective-permute-start(bf16[256,512]{1,0:T(8,128)(2,1)S(1)} %get-tuple-element.30), channel_id=1, source_target_pairs={{0,384},{128,0},{256,128},{384,256},{1,385},{129,1},{257,129},{385... | collective-permute-start | bytes 786440 | tf_op jit(solution)/shard_map/ppermute | solution.py:295
  106.8 11.9 %collective-permute-start.6 = (bf16[256,512]{1,0:T(8,128)(2,1)S(1)}, bf16[256,512]{1,0:T(8,128)(2,1)S(1)}, u32[]{:S(2)}, u32[]{:S(2)}) collective-permute-start(bf16[256,512]{1,0:T(8,128)(2,1)S(1)} %get-tuple-element.31), channel_id=1, source_target_pairs={{0,256},{128,384},{256,0},{384,128},{1,257},{129,385},{257,1},{385... | collective-permute-start | bytes 786440 | tf_op jit(solution)/shard_map/ppermute | solution.py:295
  109.9 14.1 %collective-permute-start.7 = (bf16[256,512]{1,0:T(8,128)(2,1)S(1)}, bf16[256,512]{1,0:T(8,128)(2,1)S(1)}, u32[]{:S(2)}, u32[]{:S(2)}) collective-permute-start(bf16[256,512]{1,0:T(8,128)(2,1)S(1)} %get-tuple-element.32), channel_id=1, source_target_pairs={{0,128},{128,256},{256,384},{384,0},{1,129},{129,257},{257,385},{3... | collective-permute-start | bytes 786440 | tf_op jit(solution)/shard_map/ppermute | solution.py:295
  124.2 27.4 %collective-permute-start.9 = (bf16[256,512]{1,0:T(8,128)(2,1)S(1)}, bf16[256,512]{1,0:T(8,128)(2,1)S(1)}, u32[]{:S(2)}, u32[]{:S(2)}) collective-permute-start(bf16[256,512]{1,0:T(8,128)(2,1)S(1)} %shard_map.135), channel_id=1, source_target_pairs={{0,0},{8,136},{16,272},{24,408},{32,480},{40,360},{48,240},{56,120... | collective-permute-start | bytes 786440 | tf_op jit(solution)/shard_map/ppermute | solution.py:355
  150.9 0.9 copy-start.1

commit v4 on v3

--- a/solution.py
+++ b/solution.py
@@ -10,7 +10,9 @@
 HD = 128
 TILE = 1601
 ROWS = 26
-HALF = 16
+HALF = 13
+SLOT = 16
+STEP = 14
 EPSILON = 1e-05
 SCALE = 1.0 / math.sqrt(HD)
 SCALE_LOG2 = SCALE / math.log(2.0)
@@ -21,8 +23,8 @@
 PLANE_OF = (0, 7, 1, 6, 2, 5, 3, 4)
 CONV_OF = tuple(PLANE_OF.index(z) for z in range(Z))
 SHIFT = (0, 4, 1, 3, 2, 6, 5, 7)
-CHUNK = 256
-MID = 1024
+BLOCK = 4 * STEP
+MID = 2 * Z * BLOCK
 
 
 def dot(a, b):
@@ -82,23 +84,22 @@
             lanes = slice(head * HD, (head + 1) * HD)
             x = keys_ref[n, :, lanes].astype(F32)
             mean_square = jnp.mean(x * x, axis=-1, keepdims=True)
-            normed = (x * lax.rsqrt(mean_square + EPSILON) * gain).astype(BF16)
-            pad = jnp.zeros((2 * HALF - ROWS, HD), BF16)
-            for kv, rows in ((0, normed), (1, values_ref[n, :, lanes])):
+            normed = x * lax.rsqrt(mean_square + EPSILON) * gain
+            pad = jnp.zeros((SLOT - HALF, HD), F32)
+            for kv, rows in ((0, normed), (1, values_ref[n, :, lanes].astype(F32))):
                 for half in range(2):
                     at = (n * 2 + half) * 2 + kv
-                    if half == 0:
-                        out_ref[at, hx, hhi * HALF : (hhi + 1) * HALF, :] = rows[:HALF]
-                    else:
-                        out_ref[at, hx, hhi * HALF : (hhi + 1) * HALF, :] = jnp.concatenate([rows[HALF:], pad], axis=0)
+                    piece = jnp.concatenate([rows[half * HALF : (half + 1) * HALF], pad], axis=0)
+                    out_ref[at, hx, hhi * SLOT : (hhi + 1) * SLOT, :] = piece.astype(BF16)
 
 
 def choose_tiles(owner_ref, got_ref, out_ref):
     for z in range(Z):
         o = jnp.maximum(owner_ref[CONV_OF[z]], 0)
-        chunk = got_ref[o]
+        chunk = got_ref[o].astype(F32)
         for hhi in range(2):
-            out_ref[hhi, z] = chunk[:, hhi * HALF : (hhi + 1) * HALF, :].reshape(4 * HALF, HD)
+            pieces = [chunk[tx, hhi * SLOT : hhi * SLOT + STEP, :] for tx in range(4)]
+            out_ref[hhi, z] = jnp.concatenate(pieces, axis=0).astype(BF16)
 
 
 def return_tiles(owner_ref, got_ref, out_ref):
@@ -108,16 +109,24 @@
             found = jnp.where(owner_ref[c] == o, PLANE_OF[c], found)
         at = jnp.maximum(found, 0)
         for hhi in range(2):
-            chunk = jnp.where(found >= 0, got_ref[hhi, at].astype(F32), 0.0).astype(BF16)
-            out_ref[o, :, hhi * HALF : (hhi + 1) * HALF, :] = chunk.reshape(4, HALF, HD)
+            chunk = jnp.where(found >= 0, got_ref[hhi, at].astype(F32), 0.0)
+            pad = jnp.zeros((SLOT - STEP, HD), F32)
+            for tx in range(4):
+                piece = jnp.concatenate([chunk[tx * STEP : (tx + 1) * STEP], pad], axis=0)
+                out_ref[o, tx, hhi * SLOT : (hhi + 1) * SLOT, :] = piece.astype(BF16)
 
 
 def row_mask(half, dims, axis):
-    position = lax.broadcasted_iota(jnp.int32, dims, axis)
-    thi, s, tx, i = position >> 9, (position >> 6) & 7, (position >> 4) & 3, position & 15
-    inside = half * HALF + i
-    row = s * (8 * ROWS) + (thi * 4 + tx) * ROWS + inside
-    return jnp.where((inside < ROWS) & (row < TILE), 1.0, 0.0).astype(F32)
+    def split(value, size):
+        whole = jnp.floor((value + 0.5) * (1.0 / size))
+        return whole, value - whole * size
+
+    position = lax.broadcasted_iota(jnp.int32, dims, axis).astype(F32)
+    group, inside = split(position, BLOCK)
+    thi, s = split(group, Z)
+    tx, i = split(inside, STEP)
+    row = s * (8 * ROWS) + (thi * 4 + tx) * ROWS + (i + (half * HALF).astype(F32))
+    return jnp.where((i < HALF - 0.5) & (row < TILE - 0.5), 1.0, 0.0).astype(F32)
 
 
 def columns(rows):
@@ -141,8 +150,8 @@
     return jnp.concatenate([seen] * 4, axis=1)
 
 
-def weights_of(keys_s, q_t, rows):
-    return jnp.exp2(dot(keys_s[rows, :], q_t) * SCALE_LOG2)
+def weights_of(keys_s, q_t):
+    return jnp.exp2(dot(keys_s[...], q_t) * SCALE_LOG2)
 
 
 def load_pair(ids_ref, mine_ref, other_ref, keys_s, values_s):
@@ -172,10 +181,7 @@
     def block(j, carry):
         q_t = columns(q_s[j, 0:128, :]).astype(BF16)
         o_t = columns(q_s[j, 128:256, :])
-        acc = jnp.zeros((HD + 16, 512), F32)
-        for r in range(MID // CHUNK):
-            rows = slice(r * CHUNK, (r + 1) * CHUNK)
-            acc = acc + dot(turned_s[:, rows], weights_of(keys_s, q_t, rows).astype(BF16))
+        acc = dot(turned_s[...], weights_of(keys_s, q_t).astype(BF16))
         acc = acc * seen_row(ids_ref, count_ref, visible_ref, j)
         both = jnp.concatenate([acc[HD : HD + 1], jnp.sum(acc[:HD] * o_t, axis=0, keepdims=True)], axis=0)
         for to in range(Y):
@@ -183,7 +189,7 @@
         acc_ref[j] = acc[:HD]
         return carry
 
-    lax.fori_loop(0, Y, block, 0)
+    lax.fori_loop(0, Y, block, 0, unroll=True)
 
 
 def all_sums(ids_ref, sums_ref, j):
@@ -217,19 +223,15 @@
         inverse, delta = all_sums(ids_ref, sums_ref, j)
         acc = (acc_ref[j] * inverse).astype(BF16)
         inverse = inverse * seen_row(ids_ref, count_ref, visible_ref, j)
-        dq = jnp.zeros((HD, 512), F32)
-        for r in range(MID // CHUNK):
-            rows = slice(r * CHUNK, (r + 1) * CHUNK)
-            prob = weights_of(keys_s, q_t, rows) * inverse
-            d_prob = dot(values_s[rows, :], o_t)
-            d_score = (prob * (d_prob - delta)).astype(BF16)
-            dk_s[rows, :] += dot(d_score, q_rows)
-            dv_s[rows, :] += dot(prob.astype(BF16), o_rows)
-            dq = dq + dot(turned_s[:, rows], d_score)
+        prob = weights_of(keys_s, q_t) * inverse
+        d_score = (prob * (dot(values_s[...], o_t) - delta)).astype(BF16)
+        dk_s[...] += dot(d_score, q_rows)
+        dv_s[...] += dot(prob.astype(BF16), o_rows)
+        dq = dot(turned_s[...], d_score)
         q_s[j] = jnp.concatenate([acc, (dq * SCALE).astype(BF16)], axis=0)
         return carry
 
-    lax.fori_loop(0, Y, block, 0)
+    lax.fori_loop(0, Y, block, 0, unroll=2)
     for j, r in enumerate((r0, r1, r2, r3)):
         r[...] = q_s[j]
     core = ids_ref[1]
@@ -277,14 +279,14 @@
         for head in range(8):
             hhi, hx = divmod(head, 4)
             lanes = slice(head * HD, (head + 1) * HD)
-            for half, count in ((0, HALF), (1, ROWS - HALF)):
-                at = (n * 2 + half) * 2
-                rows = slice(half * HALF, half * HALF + count)
-                piece = slice(hhi * HALF, hhi * HALF + count)
-                dv_ref[n, rows, lanes] = got_ref[at + 1, hx, piece, :]
-                x = keys_ref[n, rows, lanes].astype(F32)
-                d_normed = got_ref[at, hx, piece, :].astype(F32)
-                dk_ref[n, rows, lanes] = norm_back(x, d_normed, gain).astype(BF16)
+            x = keys_ref[n, :, lanes].astype(F32)
+
+            def rows(kv):
+                halves = [got_ref[(n * 2 + half) * 2 + kv, hx, hhi * SLOT : (hhi + 1) * SLOT, :].astype(F32) for half in range(2)]
+                return jnp.concatenate([piece[:HALF] for piece in halves], axis=0)
+
+            dk_ref[n, :, lanes] = norm_back(x, rows(0), gain).astype(BF16)
+            dv_ref[n, :, lanes] = rows(1).astype(BF16)
 
 
 def exchange(value, axes):
@@ -323,8 +325,8 @@
     (packed_kv,) = call(pack_keys, [shape((8, 4, 32, HD), BF16)], keys, values, gains)
     got = exchange(packed_kv.reshape(32, 32, HD), ("y", "core", "x"))
     got, q0 = lax.optimization_barrier((got, q0))
-    (chosen,) = call(choose_tiles, [shape((2, 8, 64, HD), BF16)], owner, got.reshape(8, 4, 32, HD), smem=1)
-    mine = exchange(chosen.reshape(16, 64, HD), ("zhi", "seq")).reshape(MID, HD)
+    (chosen,) = call(choose_tiles, [shape((2, 8, BLOCK, HD), BF16)], owner, got.reshape(8, 4, 32, HD), smem=1)
+    mine = exchange(chosen.reshape(16, BLOCK, HD), ("zhi", "seq")).reshape(MID, HD)
     q1, q2, q3 = rotated(q0, 1), rotated(q0, 2), rotated(q0, 3)
     other = swapped(mine)
 
@@ -346,14 +348,14 @@
     )
 
     grads = (keep + swapped(send).astype(F32)).astype(BF16)
-    back = exchange(grads.reshape(16, 64, HD), ("zhi", "seq"))
+    back = exchange(grads.reshape(16, BLOCK, HD), ("zhi", "seq"))
     r1, r2, r3 = rotated(r1, 3), rotated(r2, 2), rotated(r3, 1)
-    (placed,) = call(return_tiles, [shape((8, 4, 32, HD), BF16)], owner, back.reshape(2, 8, 64, HD), smem=1)
+    (placed,) = call(return_tiles, [shape((8, 4, 32, HD), BF16)], owner, back.reshape(2, 8, BLOCK, HD), smem=1)
     home = exchange(placed.reshape(32, 32, HD), ("y", "core", "x")).reshape(8, 4, 32, HD)
     r1, r2, r3, placed = lax.optimization_barrier((r1, r2, r3, placed))
     (summed,) = call(sum_tokens, [shape((256, 512), BF16)], gate, r0, r1, r2, r3, smem=1)
     summed = lax.ppermute(summed, PLANES, FROM_PLANE)
-    d_keys, d_values = call(finish_keys, [shape(keys.shape, BF16), shape(values.shape, BF16)], keys, home, gains)
+    d_keys, d_values = call(finish_keys, [shape(keys.shape, BF16), shape(values.shape, BF16)], keys, home, gains, flops=20_000_000_000)
     attended, d_queries = call(finish_queries, [shape(queries.shape, BF16)] * 2, queries, summed, gains)
     return (attended, d_queries, d_keys, d_values)
 

time: 154 us -> 146 us (0.948)
  the two profiles are of different devices: /device:TPU:1 before, /device:TPU:25 now
where the time goes in v4:
time: 146 us; the launch traced here: 145 us
  starting transfers between devices  85 us (58%)
  waiting for transfers between devices  30.6 us (21%)
  Pallas kernels  15.9 us (11%)
  blocking collectives  8.86 us (6%)
  local copies, waits for them, and re-layouts  2.28 us (2%)
  between operations  1.6 us (1%)
    all_to_all x4, starting transfers between devices, exchange(): return lax.all_to_all(value, axes, split_axis=0, concat_axis=0, tiled=True)  41.3 us
    ppermute x6, starting transfers between devices, rotated(): return lax.ppermute(value, 'y', [(i, (i + k) % Y) for i in range(Y)])  19.7 us
    pallas_call x9, Pallas kernels, call(): pl.pallas_call(kernel, out_shape=outs, in_specs=specs, out_specs=[pl.Bloc...  15.9 us
    all_to_all x4, waiting for transfers between devices, exchange(): return lax.all_to_all(value, axes, split_axis=0, concat_axis=0, tiled=True)  15.6 us
    ppermute x1, waiting for transfers between devices, shards(): summed = lax.ppermute(summed, PLANES, FROM_PLANE)  12.9 us
    ppermute x2, starting transfers between devices, swapped(): return lax.ppermute(value, 'core', [(0, 1), (1, 0)])  9.33 us
    all_to_all x1, blocking collectives, exchange(): return lax.all_to_all(value, axes, split_axis=0, concat_axis=0, tiled=True)  8.86 us
    ppermute x1, starting transfers between devices, shards(): q0 = lax.ppermute(packed, PLANES, TO_PLANE)  8.61 us
  transfers between devices with their start and end apart: 14, of which 7 were waited for; matrix products, arithmetic and copies ran while one was open for 1% of the time, Pallas kernels for 2%

profile of v4, /device:TPU:25, one launch (start us, length us, event | category | flops | bytes accessed | tf_op | source)
XLA Modules:
  0.0 145.0 jit_solution(26012385985533632)
XLA Ops:
  1.3 1.9 %shard_map.129 = (bf16[256,512]{1,0:T(8,128)(2,1)}, f32[2,128]{1,0:T(2,128)}) custom-call(f32[1]{0:T(128)S(6)} %copy.19.gate_ref, bf16[1,128,512]{2,1,0:T(8,128)(2,1)} %queries_ref.3, bf16[1,128,512]{2,1,0:T(8,128)(2,1)} %d_out_ref.1, f32[1,128]{1,0:T(1,128)} %bitcast.21, f32[1,128]{1,0:T(1,128)} %bitcast.22), custom_call_target="tpu_custom_call" | custom-call | bytes 526340 | tf_op jit(solution)/shard_map/pallas_call | solution.py:39
  3.2 8.6 %collective-permute-start = (bf16[256,512]{1,0:T(8,128)(2,1)}, bf16[256,512]{1,0:T(8,128)(2,1)S(1)}, u32[]{:S(2)}, u32[]{:S(2)}) collective-permute-start(bf16[256,512]{1,0:T(8,128)(2,1)} %get-tuple-element.24), channel_id=1, source_target_pairs={{0,0},{136,8},{272,16},{408,24},{480,32},{360,40},{240,48},{120,56... | collective-permute-start | bytes 786440 | tf_op jit(solution)/shard_map/ppermute | solution.py:324
  13.5 10.5 %all-to-all-start = ((bf16[32,32,128]{2,1,0:T(8,128)(2,1)}), bf16[32,32,128]{2,1,0:T(8,128)(2,1)S(1)}, u32[]{:S(2)}, u32[]{:S(2)}) async-start(bf16[32,32,128]{2,1,0:T(8,128)(2,1)} %bitcast.6), calls=%async_computation | async-start | bytes 524288 | tf_op jit(solution)/shard_map/all_to_all | solution.py:293
  24.0 7.1 %all-to-all-done = bf16[32,32,128]{2,1,0:T(8,128)(2,1)S(1)} async-done(((bf16[32,32,128]{2,1,0:T(8,128)(2,1)}), bf16[32,32,128]{2,1,0:T(8,128)(2,1)S(1)}, u32[]{:S(2)}, u32[]{:S(2)}) %all-to-all-start) | async-done | bytes 262176 | tf_op jit(solution)/shard_map/all_to_all | solution.py:293
  31.1 1.3 shard_map.131
  32.4 10.4 %all-to-all-start.1 = ((bf16[16,56,128]{2,1,0:T(8,128)(2,1)}), bf16[16,56,128]{2,1,0:T(8,128)(2,1)S(1)}, u32[]{:S(2)}, u32[]{:S(2)}) async-start(bf16[16,56,128]{2,1,0:T(8,128)(2,1)} %bitcast.8), calls=%async_computation.1 | async-start | bytes 458752 | tf_op jit(solution)/shard_map/all_to_all | solution.py:293
  42.8 3.6 %collective-permute-start.4 = (bf16[256,512]{1,0:T(8,128)(2,1)S(1)}, bf16[256,512]{1,0:T(8,128)(2,1)S(1)}, u32[]{:S(2)}, u32[]{:S(2)}) collective-permute-start(bf16[256,512]{1,0:T(8,128)(2,1)S(1)} %collective-permute-done.q0), channel_id=1, source_target_pairs={{0,384},{128,0},{256,128},{384,256},{1,385},{129,1},{257,129},{385... | collective-permute-start | bytes 786440 | tf_op jit(solution)/shard_map/ppermute | solution.py:297
  46.4 2.5 %collective-permute-start.3 = (bf16[256,512]{1,0:T(8,128)(2,1)S(1)}, bf16[256,512]{1,0:T(8,128)(2,1)S(1)}, u32[]{:S(2)}, u32[]{:S(2)}) collective-permute-start(bf16[256,512]{1,0:T(8,128)(2,1)S(1)} %collective-permute-done.q0), channel_id=1, source_target_pairs={{0,256},{128,384},{256,0},{384,128},{1,257},{129,385},{257,1},{385... | collective-permute-start | bytes 786440 | tf_op jit(solution)/shard_map/ppermute | solution.py:297
  49.0 4.0 %collective-permute-start.2 = (bf16[256,512]{1,0:T(8,128)(2,1)S(1)}, bf16[256,512]{1,0:T(8,128)(2,1)S(1)}, u32[]{:S(2)}, u32[]{:S(2)}) collective-permute-start(bf16[256,512]{1,0:T(8,128)(2,1)S(1)} %collective-permute-done.q0), channel_id=1, source_target_pairs={{0,128},{128,256},{256,384},{384,0},{1,129},{129,257},{257,385},{3... | collective-permute-start | bytes 786440 | tf_op jit(solution)/shard_map/ppermute | solution.py:297
  52.9 3.9 %all-to-all-done.1 = bf16[16,56,128]{2,1,0:T(8,128)(2,1)S(1)} async-done(((bf16[16,56,128]{2,1,0:T(8,128)(2,1)}), bf16[16,56,128]{2,1,0:T(8,128)(2,1)S(1)}, u32[]{:S(2)}, u32[]{:S(2)}) %all-to-all-start.1) | async-done | bytes 229408 | tf_op jit(solution)/shard_map/all_to_all | solution.py:293
  56.9 5.6 %collective-permute-start.1 = (bf16[896,128]{1,0:T(8,128)(2,1)S(1)}, bf16[896,128]{1,0:T(8,128)(2,1)S(1)}, u32[]{:S(2)}, u32[]{:S(2)}) collective-permute-start(bf16[896,128]{1,0:T(8,128)(2,1)S(1)} %bitcast.18), channel_id=1, source_target_pairs={{0,64},{64,0},{1,65},{65,1},{2,66},{66,2},{3,67},{67,3},{4,68},{68... | collective-permute-start | bytes 688136 | tf_op jit(solution)/shard_map/ppermute | solution.py:301
  63.6 3.0 %shard_map.132 = (f32[4,128,512]{2,1,0:T(8,128)S(1)}, f32[4,4,2,512]{3,2,1,0:T(2,128)S(1)}) custom-call(s32[3]{0:T(128)S(1)} %pad_add_fusion.ids_ref, s32[8]{0:T(128)S(1)} %copy-done.3, s32[64,128]{1,0:T(8,128)S(1)} %reshape.41.visible_ref, bf16[896,128]{1,0:T(8,128)(2,1)S(1)} %bitcast.19, bf16[896,128]{1,0:T(8,128)(2,1)S(1)} %collective-permute-done.1.other_ref, ...), custom_call_target="tpu_custom_call" | custom-call | flops 939524096 | bytes 2654252 | tf_op jit(solution)/shard_map/pallas_call | solution.py:39
  66.6 8.9 %all_to_all.25.sums_ref = f32[4,4,2,512]{3,2,1,0:T(2,128)S(1)} all-to-all(f32[4,4,2,512]{3,2,1,0:T(2,128)S(1)} %get-tuple-element.28), channel_id=1, replica_groups=mesh['y'=4,'core'=2,'seq'=8,'zhi'=2,'x'=4] {'y'}, dimensions={0} | all-to-all | bytes 131072 | tf_op jit(solution)/shard_map/all_to_all | solution.py:293
  75.4 6.2 %shard_map.133 = (bf16[256,512]{1,0:T(8,128)(2,1)S(1)}, bf16[256,512]{1,0:T(8,128)(2,1)S(1)}, bf16[256,512]{1,0:T(8,128)(2,1)S(1)}, bf16[256,512]{1,0:T(8,128)(2...) custom-call(s32[3]{0:T(128)S(1)} %pad_add_fusion.ids_ref, s32[8]{0:T(128)S(1)} %copy-done.3, ...), custom_call_target="tpu_custom_call" | custom-call | flops 2348810240 | bytes 4390956 | tf_op jit(solution)/shard_map/pallas_call | solution.py:39
  81.6 3.7 %collective-permute-start.8 = (bf16[896,128]{1,0:T(8,128)(2,1)S(1)}, bf16[896,128]{1,0:T(8,128)(2,1)S(1)}, u32[]{:S(2)}, u32[]{:S(2)}) collective-permute-start(bf16[896,128]{1,0:T(8,128)(2,1)S(1)} %get-tuple-element.34), channel_id=1, source_target_pairs={{0,64},{64,0},{1,65},{65,1},{2,66},{66,2},{3,67},{67,3},{4,68},{68... | collective-permute-start | bytes 688136 | tf_op jit(solution)/shard_map/ppermute | solution.py:301
  87.2 9.2 %all-to-all-start.3 = ((bf16[16,56,128]{2,1,0:T(8,128)(2,1)}), bf16[16,56,128]{2,1,0:T(8,128)(2,1)S(1)}, u32[]{:S(2)}, u32[]{:S(2)}) async-start(bf16[16,56,128]{2,1,0:T(8,128)(2,1)} %bitcast.10), calls=%async_computation.3 | async-start | bytes 458752 | tf_op jit(solution)/shard_map/all_to_all | solution.py:293
  96.4 2.0 %collective-permute-start.5 = (bf16[256,512]{1,0:T(8,128)(2,1)S(1)}, bf16[256,512]{1,0:T(8,128)(2,1)S(1)}, u32[]{:S(2)}, u32[]{:S(2)}) collective-permute-start(bf16[256,512]{1,0:T(8,128)(2,1)S(1)} %get-tuple-element.30), channel_id=1, source_target_pairs={{0,384},{128,0},{256,128},{384,256},{1,385},{129,1},{257,129},{385... | collective-permute-start | bytes 786440 | tf_op jit(solution)/shard_map/ppermute | solution.py:297
  98.4 4.8 %collective-permute-start.6 = (bf16[256,512]{1,0:T(8,128)(2,1)S(1)}, bf16[256,512]{1,0:T(8,128)(2,1)S(1)}, u32[]{:S(2)}, u32[]{:S(2)}) collective-permute-start(bf16[256,512]{1,0:T(8,128)(2,1)S(1)} %get-tuple-element.31), channel_id=1, source_target_pairs={{0,256},{128,384},{256,0},{384,128},{1,257},{129,385},{257,1},{385... | collective-permute-start | bytes 786440 | tf_op jit(solution)/shard_map/ppermute | solution.py:297
  103.2 2.8 %collective-permute-start.7 = (bf16[256,512]{1,0:T(8,128)(2,1)S(1)}, bf16[256,512]{1,0:T(8,128)(2,1)S(1)}, u32[]{:S(2)}, u32[]{:S(2)}) collective-permute-start(bf16[256,512]{1,0:T(8,128)(2,1)S(1)} %get-tuple-element.32), channel_id=1, source_target_pairs={{0,128},{128,256},{256,384},{384,0},{1,129},{129,257},{257,385},{3... | collective-permute-start | bytes 786440 | tf_op jit(solution)/shard_map/ppermute | solution.py:297
  106.0 3.8 %all-to-all-done.3 = bf16[16,56,128]{2,1,0:T(8,128)(2,1)S(1)} async-done(((bf16[16,56,128]{2,1,0:T(8,128)(2,1)}), bf16[16,56,128]{2,1,0:T(8,128)(2,1)S(1)}, u32[]{:S(2)}, u32[]{:S(2)}) %all-to-all-start.3) | async-done | bytes 229408 | tf_op jit(solution)/shard_map/all_to_all | solution.py:293
  109.8 1.3 shard_map.134
  111.1 11.2 %all-to-all-start.4 = ((bf16[32,32,128]{2,1,0:T(8,128)(2,1)}), bf16[32,32,128]{2,1,0:T(8,128)(2,1)S(1)}, u32[]{:S(2)}, u32[]{:S(2)}) async-start(bf16[32,32,128]{2,1,0:T(8,128)(2,1)} %bitcast.12), calls=%async_computation.4 | async-start | bytes 524288 | tf_op jit(solution)/shard_map/all_to_all | solution.py:293
  122.6 6.0 %collective-permute-start.9 = (bf16[256,512]{1,0:T(8,128)(2,1)S(1)}, bf16[256,512]{1,0:T(8,128)(2,1)S(1)}, u32[]{:S(2)}, u32[]{:S(2)}) collective-permute-start(bf16[256,512]{1,0:T(8,128)(2,1)S(1)} %shard_map.135), channel_id=1, source_target_pairs={{0,0},{8,136},{16,272},{24,408},{32,480},{40,360},{48,240},{56,120... | collective-permute-start | bytes 786440 | tf_op jit(solution)/shard_map/ppermute | solution.py:357
  131.2 12.9 %collective-permute-done.9.got_ref = bf16[256,512]{1,0:T(8,128)(2,1)S(1)} collective-permute-done((bf16[256,512]{1,0:T(8,128)(2,1)S(1)}, bf16[256,512]{1,0:T(8,128)(2,1)S(1)}, u32[]{:S(2)}, u32[]{:S(2)}) %collective-permute-start.9) | collective-permute-done | bytes 262176 | tf_op jit(solution)/shard_map/ppermute | solution.py:357
  (36 shorter events, 8.2 us)
Async XLA Ops:
  0.6 23.4 %copy-start = (s32[8,2]{0,1:T(2,128)S(1)}, s32[8,2]{0,1:T(2,128)}, u32[]{:S(2)}) copy-start(s32[8,2]{0,1:T(2,128)} %param.17) | copy-start | bytes 196
  1.3 10.5 %copy-start.4 = (bf16[2,26,1024]{2,0,1:T(2,128)(2,1)S(1)}, bf16[2,26,1024]{2,0,1:T(2,128)(2,1)}, u32[]{:S(2)}) copy-start(bf16[2,26,1024]{2,0,1:T(2,128)(2,1)} %param.11) | copy-start | bytes 319492
  3.2 8.7 %copy-start.5 = (bf16[2,26,1024]{2,0,1:T(2,128)(2,1)S(1)}, bf16[2,26,1024]{2,0,1:T(2,128)(2,1)}, u32[]{:S(2)}) copy-start(bf16[2,26,1024]{2,0,1:T(2,128)(2,1)} %param.12) | copy-start | bytes 319492
  3.2 27.9 %collective-permute-start = (bf16[256,512]{1,0:T(8,128)(2,1)}, bf16[256,512]{1,0:T(8,128)(2,1)S(1)}, u32[]{:S(2)}, u32[]{:S(2)}) collective-permute-start(bf16[256,512]{1,0:T(8,128)(2,1)} %get-tuple-element.24), channel_id=1, source_target_pairs={{0,0},{136,8},{272,16},{408,24},{480,32},{360,40},{240,48},{120,56... | collective-permute-start | bytes 786440 | tf_op jit(solution)/shard_map/ppermute | solution.py:324
  11.9 0.7 copy-start.2
  13.5 17.6 %all-to-all-start = ((bf16[32,32,128]{2,1,0:T(8,128)(2,1)}), bf16[32,32,128]{2,1,0:T(8,128)(2,1)S(1)}, u32[]{:S(2)}, u32[]{:S(2)}) async-start(bf16[32,32,128]{2,1,0:T(8,128)(2,1)} %bitcast.6), calls=%async_computation | async-start | bytes 524288 | tf_op jit(solution)/shard_map/all_to_all | solution.py:293
  32.4 30.1 %copy-start.6 = (s32[8,1024]{1,0:T(8,128)S(1)}, s32[8,1024]{1,0:T(8,128)}, u32[]{:S(2)}) copy-start(s32[8,1024]{1,0:T(8,128)} %param.18) | copy-start | bytes 98308
  32.4 24.5 %all-to-all-start.1 = ((bf16[16,56,128]{2,1,0:T(8,128)(2,1)}), bf16[16,56,128]{2,1,0:T(8,128)(2,1)S(1)}, u32[]{:S(2)}, u32[]{:S(2)}) async-start(bf16[16,56,128]{2,1,0:T(8,128)(2,1)} %bitcast.8), calls=%async_computation.1 | async-start | bytes 458752 | tf_op jit(solution)/shard_map/all_to_all | solution.py:293
  42.8 19.8 %collective-permute-start.4 = (bf16[256,512]{1,0:T(8,128)(2,1)S(1)}, bf16[256,512]{1,0:T(8,128)(2,1)S(1)}, u32[]{:S(2)}, u32[]{:S(2)}) collective-permute-start(bf16[256,512]{1,0:T(8,128)(2,1)S(1)} %collective-permute-done.q0), channel_id=1, source_target_pairs={{0,384},{128,0},{256,128},{384,256},{1,385},{129,1},{257,129},{385... | collective-permute-start | bytes 786440 | tf_op jit(solution)/shard_map/ppermute | solution.py:297
  46.4 16.2 %collective-permute-start.3 = (bf16[256,512]{1,0:T(8,128)(2,1)S(1)}, bf16[256,512]{1,0:T(8,128)(2,1)S(1)}, u32[]{:S(2)}, u32[]{:S(2)}) collective-permute-start(bf16[256,512]{1,0:T(8,128)(2,1)S(1)} %collective-permute-done.q0), channel_id=1, source_target_pairs={{0,256},{128,384},{256,0},{384,128},{1,257},{129,385},{257,1},{385... | collective-permute-start | bytes 786440 | tf_op jit(solution)/shard_map/ppermute | solution.py:297
  49.0 13.7 %collective-permute-start.2 = (bf16[256,512]{1,0:T(8,128)(2,1)S(1)}, bf16[256,512]{1,0:T(8,128)(2,1)S(1)}, u32[]{:S(2)}, u32[]{:S(2)}) collective-permute-start(bf16[256,512]{1,0:T(8,128)(2,1)S(1)} %collective-permute-done.q0), channel_id=1, source_target_pairs={{0,128},{128,256},{256,384},{384,0},{1,129},{129,257},{257,385},{3... | collective-permute-start | bytes 786440 | tf_op jit(solution)/shard_map/ppermute | solution.py:297
  56.9 6.7 %collective-permute-start.1 = (bf16[896,128]{1,0:T(8,128)(2,1)S(1)}, bf16[896,128]{1,0:T(8,128)(2,1)S(1)}, u32[]{:S(2)}, u32[]{:S(2)}) collective-permute-start(bf16[896,128]{1,0:T(8,128)(2,1)S(1)} %bitcast.18), channel_id=1, source_target_pairs={{0,64},{64,0},{1,65},{65,1},{2,66},{66,2},{3,67},{67,3},{4,68},{68... | collective-permute-start | bytes 688136 | tf_op jit(solution)/shard_map/ppermute | solution.py:301
  62.5 1.1 copy-start.3
  81.6 4.8 %collective-permute-start.8 = (bf16[896,128]{1,0:T(8,128)(2,1)S(1)}, bf16[896,128]{1,0:T(8,128)(2,1)S(1)}, u32[]{:S(2)}, u32[]{:S(2)}) collective-permute-start(bf16[896,128]{1,0:T(8,128)(2,1)S(1)} %get-tuple-element.34), channel_id=1, source_target_pairs={{0,64},{64,0},{1,65},{65,1},{2,66},{66,2},{3,67},{67,3},{4,68},{68... | collective-permute-start | bytes 688136 | tf_op jit(solution)/shard_map/ppermute | solution.py:301
  87.2 22.6 %all-to-all-start.3 = ((bf16[16,56,128]{2,1,0:T(8,128)(2,1)}), bf16[16,56,128]{2,1,0:T(8,128)(2,1)S(1)}, u32[]{:S(2)}, u32[]{:S(2)}) async-start(bf16[16,56,128]{2,1,0:T(8,128)(2,1)} %bitcast.10), calls=%async_computation.3 | async-start | bytes 458752 | tf_op jit(solution)/shard_map/all_to_all | solution.py:293
  96.4 25.9 %collective-permute-start.5 = (bf16[256,512]{1,0:T(8,128)(2,1)S(1)}, bf16[256,512]{1,0:T(8,128)(2,1)S(1)}, u32[]{:S(2)}, u32[]{:S(2)}) collective-permute-start(bf16[256,512]{1,0:T(8,128)(2,1)S(1)} %get-tuple-element.30), channel_id=1, source_target_pairs={{0,384},{128,0},{256,128},{384,256},{1,385},{129,1},{257,129},{385... | collective-permute-start | bytes 786440 | tf_op jit(solution)/shard_map/ppermute | solution.py:297
  98.4 23.9 %collective-permute-start.6 = (bf16[256,512]{1,0:T(8,128)(2,1)S(1)}, bf16[256,512]{1,0:T(8,128)(2,1)S(1)}, u32[]{:S(2)}, u32[]{:S(2)}) collective-permute-start(bf16[256,512]{1,0:T(8,128)(2,1)S(1)} %get-tuple-element.31), channel_id=1, source_target_pairs={{0,256},{128,384},{256,0},{384,128},{1,257},{129,385},{257,1},{385... | collective-permute-start | bytes 786440 | tf_op jit(solution)/shard_map/ppermute | solution.py:297
  103.2 19.2 %collective-permute-start.7 = (bf16[256,512]{1,0:T(8,128)(2,1)S(1)}, bf16[256,512]{1,0:T(8,128)(2,1)S(1)}, u32[]{:S(2)}, u32[]{:S(2)}) collective-permute-start(bf16[256,512]{1,0:T(8,128)(2,1)S(1)} %get-tuple-element.32), channel_id=1, source_target_pairs={{0,128},{128,256},{256,384},{384,0},{1,129},{129,257},{257,385},{3... | collective-permute-start | bytes 786440 | tf_op jit(solution)/shard_map/ppermute | solution.py:297
  111.1 18.4 %all-to-all-start.4 = ((bf16[32,32,128]{2,1,0:T(8,128)(2,1)}), bf16[32,32,128]{2,1,0:T(8,128)(2,1)S(1)}, u32[]{:S(2)}, u32[]{:S(2)}) async-start(bf16[32,32,128]{2,1,0:T(8,128)(2,1)} %bitcast.12), calls=%async_computation.4 | async-start | bytes 524288 | tf_op jit(solution)/shard_map/all_to_all | solution.py:293
  122.6 21.6 %collective-permute-start.9 = (bf16[256,512]{1,0:T(8,128)(2,1)S(1)}, bf16[256,512]{1,0:T(8,128)(2,1)S(1)}, u32[]{:S(2)}, u32[]{:S(2)}) collective-permute-start(bf16[256,512]{1,0:T(8,128)(2,1)S(1)} %shard_map.135), channel_id=1, source_target_pairs={{0,0},{8,136},{16,272},{24,408},{32,480},{40,360},{48,240},{56,120... | collective-permute-start | bytes 786440 | tf_op jit(solution)/shard_map/ppermute | solution.py:357
  130.4 13.7 %copy-start.1 = (bf16[1,128,512]{2,1,0:T(8,128)(2,1)S(1)}, bf16[1,128,512]{2,1,0:T(8,128)(2,1)}, u32[]{:S(2)}) copy-start(bf16[1,128,512]{2,1,0:T(8,128)(2,1)} %queries_ref.3) | copy-start | bytes 393220

commit v5 on v4

--- a/solution.py
+++ b/solution.py
@@ -20,9 +20,10 @@
 BF16 = jnp.bfloat16
 
 Y, CORE, Z, N_O, N_C = 4, 2, 8, 8, 8
-PLANE_OF = (0, 7, 1, 6, 2, 5, 3, 4)
+PLANE_OF = (0, 7, 1, 6, 3, 4, 2, 5)
 CONV_OF = tuple(PLANE_OF.index(z) for z in range(Z))
-SHIFT = (0, 4, 1, 3, 2, 6, 5, 7)
+SHIFT = (0, 4, 1, 3, 5, 7, 2, 6)
+MIXED = 160
 BLOCK = 4 * STEP
 MID = 2 * Z * BLOCK
 
@@ -139,7 +140,9 @@
 
 def seen_row(ids_ref, count_ref, visible_ref, j):
     y, core, z = ids_ref[0], ids_ref[1], ids_ref[2]
-    conv = jnp.where(z < 4, 2 * z, 15 - 2 * z)
+    conv = jnp.int32(CONV_OF[0])
+    for i in range(1, Z):
+        conv = jnp.where(z == i, CONV_OF[i], conv)
     source = ((y - j) & 3) * 2 + core
     shift = jnp.int32(0)
     for i in range(1, 8):
@@ -170,41 +173,49 @@
     return row_mask(ids_ref[0] & 1, (MID, HD), 0)
 
 
-def forward(ids_ref, count_ref, visible_ref, mine_ref, other_ref, q0, q1, q2, q3, acc_ref, sums_ref, keys_s, values_s, turned_s, q_s):
+def thirds(value):
+    high = value.astype(BF16).astype(F32)
+    middle = (value - high).astype(BF16).astype(F32)
+    return [high, middle, value - high - middle]
+
+
+def forward(ids_ref, count_ref, visible_ref, mine_ref, other_ref, q0, q1, q2, q3, mixed_ref, keys_s, values_s, turned_s):
+    y = ids_ref[0]
     ok = load_pair(ids_ref, mine_ref, other_ref, keys_s, values_s)
     keys_s[...] = (keys_s[...].astype(F32) * ok).astype(BF16)
     turned_s[0:HD, :] = (values_s[...].astype(F32) * ok).T.astype(BF16)
     turned_s[HD:, :] = row_mask(ids_ref[0] & 1, (16, MID), 1).astype(BF16)
+    rows = []
     for j, q in enumerate((q0, q1, q2, q3)):
-        q_s[j] = q[...]
-
-    def block(j, carry):
-        q_t = columns(q_s[j, 0:128, :]).astype(BF16)
-        o_t = columns(q_s[j, 128:256, :])
-        acc = dot(turned_s[...], weights_of(keys_s, q_t).astype(BF16))
-        acc = acc * seen_row(ids_ref, count_ref, visible_ref, j)
-        both = jnp.concatenate([acc[HD : HD + 1], jnp.sum(acc[:HD] * o_t, axis=0, keepdims=True)], axis=0)
-        for to in range(Y):
-            sums_ref[to, j] = both
-        acc_ref[j] = acc[:HD]
-        return carry
-
-    lax.fori_loop(0, Y, block, 0, unroll=True)
-
-
-def all_sums(ids_ref, sums_ref, j):
-    y = ids_ref[0]
-    both = sums_ref[y, j]
-    for k in range(1, Y):
-        both = both + sums_ref[(y - k) & 3, (j - k) & 3]
-    total = both[0:1]
-    safe = jnp.where(total > 0, total, 1.0)
-    return 1.0 / safe, both[1:2] / safe
+        q_t = columns(q[0:128, :]).astype(BF16)
+        o_t = columns(q[128:256, :])
+        acc = dot(turned_s[...], weights_of(keys_s, q_t).astype(BF16)) * seen_row(ids_ref, count_ref, visible_ref, j)
+        mixed_ref[(y - j) & 3, 0:HD, :] = acc[:HD].astype(BF16)
+        rows += thirds(acc[HD : HD + 1]) + thirds(jnp.sum(acc[:HD] * o_t, axis=0, keepdims=True))
+    rows = jnp.concatenate(rows + [jnp.zeros((MIXED - HD - 24, 512), F32)], axis=0).astype(BF16)
+    for to in range(Y):
+        mixed_ref[to, HD:, :] = rows
+
+
+def all_sums(ids_ref, mixed_ref):
+    sums = [[jnp.zeros((1, 512), F32)] * 2 for _ in range(Y)]
+    for k in range(Y):
+        rows = mixed_ref[(ids_ref[0] - k) & 3, HD:, :].astype(F32)
+        for j in range(Y):
+            at = 6 * ((j - k) & 3)
+            for i in range(2):
+                first = at + 3 * i
+                sums[j][i] = sums[j][i] + (rows[first : first + 1] + rows[first + 1 : first + 2] + rows[first + 2 : first + 3])
+    found = []
+    for total, product in sums:
+        safe = jnp.where(total > 0, total, 1.0)
+        found.append((1.0 / safe, product / safe))
+    return found
 
 
 def backward(
-    ids_ref, count_ref, visible_ref, mine_ref, other_ref, q0, q1, q2, q3, acc_ref, sums_ref,
-    r0, r1, r2, r3, keep_ref, send_ref, keys_s, values_s, turned_s, q_s, dk_s, dv_s,
+    ids_ref, count_ref, visible_ref, mine_ref, other_ref, q0, q1, q2, q3, mixed_ref,
+    r0, r1, r2, r3, keep_ref, send_ref, keys_s, values_s, turned_s, dk_s, dv_s,
 ):
     ok = load_pair(ids_ref, mine_ref, other_ref, keys_s, values_s)
     masked = keys_s[...].astype(F32) * ok
@@ -212,28 +223,17 @@
     turned_s[...] = masked.T.astype(BF16)
     dk_s[...] = jnp.zeros((MID, HD), F32)
     dv_s[...] = jnp.zeros((MID, HD), F32)
-    for j, q in enumerate((q0, q1, q2, q3)):
-        q_s[j] = q[...]
-
-    def block(j, carry):
-        q_t = columns(q_s[j, 0:128, :]).astype(BF16)
-        o_t = columns(q_s[j, 128:256, :]).astype(BF16)
-        q_rows = stacked(q_s[j, 0:128, :])
-        o_rows = stacked(q_s[j, 128:256, :])
-        inverse, delta = all_sums(ids_ref, sums_ref, j)
-        acc = (acc_ref[j] * inverse).astype(BF16)
+    found = all_sums(ids_ref, mixed_ref)
+    for j, (q, r) in enumerate(((q0, r0), (q1, r1), (q2, r2), (q3, r3))):
+        q_t = columns(q[0:128, :]).astype(BF16)
+        o_t = columns(q[128:256, :]).astype(BF16)
+        inverse, delta = found[j]
         inverse = inverse * seen_row(ids_ref, count_ref, visible_ref, j)
         prob = weights_of(keys_s, q_t) * inverse
         d_score = (prob * (dot(values_s[...], o_t) - delta)).astype(BF16)
-        dk_s[...] += dot(d_score, q_rows)
-        dv_s[...] += dot(prob.astype(BF16), o_rows)
-        dq = dot(turned_s[...], d_score)
-        q_s[j] = jnp.concatenate([acc, (dq * SCALE).astype(BF16)], axis=0)
-        return carry
-
-    lax.fori_loop(0, Y, block, 0, unroll=2)
-    for j, r in enumerate((r0, r1, r2, r3)):
-        r[...] = q_s[j]
+        dk_s[...] += dot(d_score, stacked(q[0:128, :]))
+        dv_s[...] += dot(prob.astype(BF16), stacked(q[128:256, :]))
+        r[...] = (dot(turned_s[...], d_score) * SCALE).astype(BF16)
     core = ids_ref[1]
 
     @pl.when(core == 0)
@@ -247,13 +247,22 @@
         send_ref[...] = (dk_s[...] * (ok * SCALE)).astype(BF16)
 
 
-def sum_tokens(gate_ref, r0, r1, r2, r3, out_ref):
+def finish_attended(ids_ref, gate_ref, mixed_ref, out_ref):
+    acc = mixed_ref[0, 0:HD, :].astype(F32)
+    for i in range(1, Y):
+        acc = acc + mixed_ref[i, 0:HD, :].astype(F32)
+    acc = acc * all_sums(ids_ref, mixed_ref)[0][0]
     gate = gate_value(gate_ref)
-    both = r0[...].astype(F32) + r1[...].astype(F32) + r2[...].astype(F32) + r3[...].astype(F32)
     for g in range(4):
         lanes = slice(g * HD, (g + 1) * HD)
-        out_ref[0:128, lanes] = (both[0:128, lanes].T * gate).astype(BF16)
-        out_ref[128:256, lanes] = both[128:256, lanes].T.astype(BF16)
+        out_ref[:, lanes] = (acc[:, lanes].T * gate).astype(BF16)
+
+
+def sum_queries(r0, r1, r2, r3, out_ref):
+    dq = r0[...].astype(F32) + r1[...].astype(F32) + r2[...].astype(F32) + r3[...].astype(F32)
+    for g in range(4):
+        lanes = slice(g * HD, (g + 1) * HD)
+        out_ref[:, lanes] = dq[:, lanes].T.astype(BF16)
 
 
 def norm_back(x, d_normed, gain):
@@ -264,29 +273,27 @@
     return inverse * scaled - x * (inverse * inverse * inverse * dots)
 
 
-def finish_queries(queries_ref, got_ref, gains_ref, attended_ref, out_ref):
+def finish_queries(queries_ref, got_ref, gains_ref, out_ref):
     gain = gains_ref[0:1]
-    attended_ref[0] = got_ref[0:128, :]
     for g in range(4):
         lanes = slice(g * HD, (g + 1) * HD)
         x = queries_ref[0, :, lanes].astype(F32)
-        out_ref[0, :, lanes] = norm_back(x, got_ref[128:256, lanes].astype(F32), gain).astype(BF16)
+        out_ref[0, :, lanes] = norm_back(x, got_ref[:, lanes].astype(F32), gain).astype(BF16)
 
 
 def finish_keys(keys_ref, got_ref, gains_ref, dk_ref, dv_ref):
     gain = gains_ref[1:2]
-    for n in range(2):
-        for head in range(8):
-            hhi, hx = divmod(head, 4)
-            lanes = slice(head * HD, (head + 1) * HD)
-            x = keys_ref[n, :, lanes].astype(F32)
-
-            def rows(kv):
-                halves = [got_ref[(n * 2 + half) * 2 + kv, hx, hhi * SLOT : (hhi + 1) * SLOT, :].astype(F32) for half in range(2)]
-                return jnp.concatenate([piece[:HALF] for piece in halves], axis=0)
-
-            dk_ref[n, :, lanes] = norm_back(x, rows(0), gain).astype(BF16)
-            dv_ref[n, :, lanes] = rows(1).astype(BF16)
+    for head in range(8):
+        hhi, hx = divmod(head, 4)
+        lanes = slice(head * HD, (head + 1) * HD)
+
+        def rows(n, kv):
+            halves = [got_ref[(n * 2 + half) * 2 + kv, hx, hhi * SLOT : (hhi + 1) * SLOT, :].astype(F32) for half in range(2)]
+            return jnp.concatenate([piece[:HALF] for piece in halves], axis=0)
+
+        grads = [norm_back(keys_ref[n, :, lanes].astype(F32), rows(n, 0), gain) for n in range(2)]
+        dk_ref[:, :, lanes] = jnp.stack(grads, axis=1).astype(BF16)
+        dv_ref[:, :, lanes] = jnp.stack([rows(n, 1) for n in range(2)], axis=1).astype(BF16)
 
 
 def exchange(value, axes):
@@ -331,33 +338,36 @@
     other = swapped(mine)
 
     pair = [pltpu.VMEM((MID, HD), BF16), pltpu.VMEM((MID, HD), BF16)]
-    tokens = pltpu.VMEM((Y, 256, 512), BF16)
     gradients = [pltpu.VMEM((MID, HD), F32), pltpu.VMEM((MID, HD), F32)]
-    acc, sums = call(
+    (mixed,) = call(
         forward,
-        [shape((Y, HD, 512), F32), shape((Y, Y, 2, 512), F32)],
+        [shape((Y, MIXED, 512), BF16)],
         ids, tile_count, seen, mine, other, q0, q1, q2, q3,
-        smem=2, scratch=pair + [pltpu.VMEM((HD + 16, MID), BF16), tokens], flops=2 * 2 * 2048 * MID * HD, limit=32 << 20,
+        smem=2, scratch=pair + [pltpu.VMEM((HD + 16, MID), BF16)], flops=2 * 2 * 2048 * MID * HD, limit=32 << 20,
     )
-    sums = exchange(sums, "y")
+    mixed = exchange(mixed, "y")
     r0, r1, r2, r3, keep, send = call(
         backward,
-        [shape((256, 512), BF16)] * 4 + [shape((MID, HD), F32), shape((MID, HD), BF16)],
-        ids, tile_count, seen, mine, other, q0, q1, q2, q3, acc, sums,
-        smem=2, scratch=pair + [pltpu.VMEM((HD, MID), BF16), tokens] + gradients, flops=5 * 2 * 2048 * MID * HD, limit=32 << 20,
+        [shape((HD, 512), BF16)] * 4 + [shape((MID, HD), F32), shape((MID, HD), BF16)],
+        ids, tile_count, seen, mine, other, q0, q1, q2, q3, mixed,
+        smem=2, scratch=pair + [pltpu.VMEM((HD, MID), BF16)] + gradients, flops=5 * 2 * 2048 * MID * HD, limit=32 << 20,
     )
 
     grads = (keep + swapped(send).astype(F32)).astype(BF16)
     back = exchange(grads.reshape(16, BLOCK, HD), ("zhi", "seq"))
+    (attended,) = call(finish_attended, [shape((128, 512), BF16)], ids, gate, mixed, smem=2)
+    attended = lax.ppermute(attended, PLANES, FROM_PLANE)
     r1, r2, r3 = rotated(r1, 3), rotated(r2, 2), rotated(r3, 1)
+    back, attended = lax.optimization_barrier((back, attended))
     (placed,) = call(return_tiles, [shape((8, 4, 32, HD), BF16)], owner, back.reshape(2, 8, BLOCK, HD), smem=1)
     home = exchange(placed.reshape(32, 32, HD), ("y", "core", "x")).reshape(8, 4, 32, HD)
     r1, r2, r3, placed = lax.optimization_barrier((r1, r2, r3, placed))
-    (summed,) = call(sum_tokens, [shape((256, 512), BF16)], gate, r0, r1, r2, r3, smem=1)
-    summed = lax.ppermute(summed, PLANES, FROM_PLANE)
-    d_keys, d_values = call(finish_keys, [shape(keys.shape, BF16), shape(values.shape, BF16)], keys, home, gains, flops=20_000_000_000)
-    attended, d_queries = call(finish_queries, [shape(queries.shape, BF16)] * 2, queries, summed, gains)
-    return (attended, d_queries, d_keys, d_values)
+    (d_normed,) = call(sum_queries, [shape((128, 512), BF16)], r0, r1, r2, r3)
+    d_normed = lax.ppermute(d_normed, PLANES, FROM_PLANE)
+    pairs = shape((ROWS, 2, 8 * HD), BF16)
+    d_keys, d_values = call(finish_keys, [pairs, pairs], keys, home, gains, flops=20_000_000_000)
+    (d_queries,) = call(finish_queries, [shape(queries.shape, BF16)], queries, d_normed, gains)
+    return (attended[None], d_queries, d_keys.transpose(1, 0, 2), d_values.transpose(1, 0, 2))
 
 
 def solution(mesh):

time: 146 us -> 152 us (1.041)
  the two profiles are of different devices: /device:TPU:25 before, /device:TPU:1 now
where the time goes in v5:
time: 152 us
  starting transfers between devices  89.8 us (59%)
  waiting for transfers between devices  25.7 us (17%)
  Pallas kernels  17.1 us (11%)
  blocking collectives  15.1 us (10%)
  between operations  1.61 us (1%)
    all_to_all x4, starting transfers between devices, exchange(): return lax.all_to_all(value, axes, split_axis=0, concat_axis=0, tiled=True)  30.1 us
    ppermute x6, starting transfers between devices, rotated(): return lax.ppermute(value, 'y', [(i, (i + k) % Y) for i in range(Y)])  22.8 us
    pallas_call x10, Pallas kernels, call(): pl.pallas_call(kernel, out_shape=outs, in_specs=specs, out_specs=[pl.Bloc...  17.1 us
    ppermute x1, starting transfers between devices, shards(): q0 = lax.ppermute(packed, PLANES, TO_PLANE)  15.4 us
    all_to_all x1, blocking collectives, exchange(): return lax.all_to_all(value, axes, split_axis=0, concat_axis=0, tiled=True)  15.1 us
    ppermute x1, waiting for transfers between devices, shards(): d_normed = lax.ppermute(d_normed, PLANES, FROM_PLANE)  12 us
    ppermute x2, starting transfers between devices, swapped(): return lax.ppermute(value, 'core', [(0, 1), (1, 0)])  11.4 us
    all_to_all x4, waiting for transfers between devices, exchange(): return lax.all_to_all(value, axes, split_axis=0, concat_axis=0, tiled=True)  10.6 us
  transfers between devices with their start and end apart: 15, of which 6 were waited for; matrix products, arithmetic and copies ran while one was open for 0% of the time, Pallas kernels for 3%

profile of v5, /device:TPU:1, one launch (start us, length us, event | category | flops | bytes accessed | tf_op | source)
XLA Modules:
  0.0 151.5 jit_solution(14004244136962840218)
XLA Ops:
  1.3 1.9 %shard_map.129 = (bf16[256,512]{1,0:T(8,128)(2,1)}, f32[2,128]{1,0:T(2,128)}) custom-call(f32[1]{0:T(128)S(6)} %copy.18.gate_ref, bf16[1,128,512]{2,1,0:T(8,128)(2,1)} %queries_ref.3, bf16[1,128,512]{2,1,0:T(8,128)(2,1)} %d_out_ref.1, f32[1,128]{1,0:T(1,128)} %bitcast.25, f32[1,128]{1,0:T(1,128)} %bitcast.26), custom_call_target="tpu_custom_call" | custom-call | bytes 526340 | tf_op jit(solution)/shard_map/pallas_call | solution.py:40
  3.3 15.4 %collective-permute-start = (bf16[256,512]{1,0:T(8,128)(2,1)}, bf16[256,512]{1,0:T(8,128)(2,1)S(1)}, u32[]{:S(2)}, u32[]{:S(2)}) collective-permute-start(bf16[256,512]{1,0:T(8,128)(2,1)} %get-tuple-element.22), channel_id=1, source_target_pairs={{0,0},{136,8},{400,16},{280,24},{352,32},{488,40},{240,48},{120,56... | collective-permute-start | bytes 786440 | tf_op jit(solution)/shard_map/ppermute | solution.py:331
  20.3 4.9 %all-to-all-start = ((bf16[32,32,128]{2,1,0:T(8,128)(2,1)}), bf16[32,32,128]{2,1,0:T(8,128)(2,1)S(1)}, u32[]{:S(2)}, u32[]{:S(2)}) async-start(bf16[32,32,128]{2,1,0:T(8,128)(2,1)} %bitcast.6), calls=%async_computation | async-start | bytes 524288 | tf_op jit(solution)/shard_map/all_to_all | solution.py:300
  25.3 8.8 %all-to-all-done = bf16[32,32,128]{2,1,0:T(8,128)(2,1)S(1)} async-done(((bf16[32,32,128]{2,1,0:T(8,128)(2,1)}), bf16[32,32,128]{2,1,0:T(8,128)(2,1)S(1)}, u32[]{:S(2)}, u32[]{:S(2)}) %all-to-all-start) | async-done | bytes 262176 | tf_op jit(solution)/shard_map/all_to_all | solution.py:300
  34.2 1.3 shard_map.131
  35.5 8.4 %all-to-all-start.1 = ((bf16[16,56,128]{2,1,0:T(8,128)(2,1)}), bf16[16,56,128]{2,1,0:T(8,128)(2,1)S(1)}, u32[]{:S(2)}, u32[]{:S(2)}) async-start(bf16[16,56,128]{2,1,0:T(8,128)(2,1)} %bitcast.8), calls=%async_computation.1 | async-start | bytes 458752 | tf_op jit(solution)/shard_map/all_to_all | solution.py:300
  43.9 4.5 %collective-permute-start.4 = (bf16[256,512]{1,0:T(8,128)(2,1)S(1)}, bf16[256,512]{1,0:T(8,128)(2,1)S(1)}, u32[]{:S(2)}, u32[]{:S(2)}) collective-permute-start(bf16[256,512]{1,0:T(8,128)(2,1)S(1)} %collective-permute-done.q0), channel_id=1, source_target_pairs={{0,384},{128,0},{256,128},{384,256},{1,385},{129,1},{257,129},{385... | collective-permute-start | bytes 786440 | tf_op jit(solution)/shard_map/ppermute | solution.py:304
  48.4 3.7 %collective-permute-start.3 = (bf16[256,512]{1,0:T(8,128)(2,1)S(1)}, bf16[256,512]{1,0:T(8,128)(2,1)S(1)}, u32[]{:S(2)}, u32[]{:S(2)}) collective-permute-start(bf16[256,512]{1,0:T(8,128)(2,1)S(1)} %collective-permute-done.q0), channel_id=1, source_target_pairs={{0,256},{128,384},{256,0},{384,128},{1,257},{129,385},{257,1},{385... | collective-permute-start | bytes 786440 | tf_op jit(solution)/shard_map/ppermute | solution.py:304
  52.1 2.7 %collective-permute-start.2 = (bf16[256,512]{1,0:T(8,128)(2,1)S(1)}, bf16[256,512]{1,0:T(8,128)(2,1)S(1)}, u32[]{:S(2)}, u32[]{:S(2)}) collective-permute-start(bf16[256,512]{1,0:T(8,128)(2,1)S(1)} %collective-permute-done.q0), channel_id=1, source_target_pairs={{0,128},{128,256},{256,384},{384,0},{1,129},{129,257},{257,385},{3... | collective-permute-start | bytes 786440 | tf_op jit(solution)/shard_map/ppermute | solution.py:304
  54.8 1.7 %all-to-all-done.1 = bf16[16,56,128]{2,1,0:T(8,128)(2,1)S(1)} async-done(((bf16[16,56,128]{2,1,0:T(8,128)(2,1)}), bf16[16,56,128]{2,1,0:T(8,128)(2,1)S(1)}, u32[]{:S(2)}, u32[]{:S(2)}) %all-to-all-start.1) | async-done | bytes 229408 | tf_op jit(solution)/shard_map/all_to_all | solution.py:300
  56.5 7.7 %collective-permute-start.1 = (bf16[896,128]{1,0:T(8,128)(2,1)S(1)}, bf16[896,128]{1,0:T(8,128)(2,1)S(1)}, u32[]{:S(2)}, u32[]{:S(2)}) collective-permute-start(bf16[896,128]{1,0:T(8,128)(2,1)S(1)} %bitcast.21), channel_id=1, source_target_pairs={{0,64},{64,0},{1,65},{65,1},{2,66},{66,2},{3,67},{67,3},{4,68},{68... | collective-permute-start | bytes 688136 | tf_op jit(solution)/shard_map/ppermute | solution.py:308
  65.3 3.0 %shard_map.132 = bf16[4,160,512]{2,1,0:T(8,128)(2,1)S(1)} custom-call(s32[3]{0:T(128)S(1)} %pad_add_fusion.ids_ref, s32[8]{0:T(128)S(1)} %copy-done.3, s32[64,128]{1,0:T(8,128)S(1)} %reshape.41.visible_ref, bf16[896,128]{1,0:T(8,128)(2,1)S(1)} %bitcast.22, bf16[896,128]{1,0:T(8,128)(2,1)S(1)} %collective-permute-done.1.other_ref, ...), custom_call_target="tpu_custom_call" | custom-call | flops 939524096 | bytes 2195500 | tf_op jit(solution)/shard_map/pallas_call | solution.py:40
  68.4 15.1 %all_to_all.25.mixed_ref = bf16[4,160,512]{2,1,0:T(8,128)(2,1)S(1)} all-to-all(bf16[4,160,512]{2,1,0:T(8,128)(2,1)S(1)} %shard_map.132), channel_id=1, replica_groups=mesh['y'=4,'core'=2,'seq'=8,'zhi'=2,'x'=4] {'y'}, dimensions={0} | all-to-all | bytes 1310720 | tf_op jit(solution)/shard_map/all_to_all | solution.py:300
  83.4 5.7 %shard_map.133 = (bf16[128,512]{1,0:T(8,128)(2,1)S(1)}, bf16[128,512]{1,0:T(8,128)(2,1)S(1)}, bf16[128,512]{1,0:T(8,128)(2,1)S(1)}, bf16[128,512]{1,0:T(8,128)(2...) custom-call(s32[3]{0:T(128)S(1)} %pad_add_fusion.ids_ref, s32[8]{0:T(128)S(1)} %copy-done.3, ...), custom_call_target="tpu_custom_call" | custom-call | flops 2348810240 | bytes 3407916 | tf_op jit(solution)/shard_map/pallas_call | solution.py:40
  89.2 3.7 %collective-permute-start.5 = (bf16[896,128]{1,0:T(8,128)(2,1)S(1)}, bf16[896,128]{1,0:T(8,128)(2,1)S(1)}, u32[]{:S(2)}, u32[]{:S(2)}) collective-permute-start(bf16[896,128]{1,0:T(8,128)(2,1)S(1)} %get-tuple-element.26), channel_id=1, source_target_pairs={{0,64},{64,0},{1,65},{65,1},{2,66},{66,2},{3,67},{67,3},{4,68},{68... | collective-permute-start | bytes 688136 | tf_op jit(solution)/shard_map/ppermute | solution.py:308
  94.7 7.5 %all-to-all-start.3 = ((bf16[16,56,128]{2,1,0:T(8,128)(2,1)}), bf16[16,56,128]{2,1,0:T(8,128)(2,1)S(1)}, u32[]{:S(2)}, u32[]{:S(2)}) async-start(bf16[16,56,128]{2,1,0:T(8,128)(2,1)} %bitcast.10), calls=%async_computation.3 | async-start | bytes 458752 | tf_op jit(solution)/shard_map/all_to_all | solution.py:300
  103.0 8.0 %collective-permute-start.6 = (bf16[128,512]{1,0:T(8,128)(2,1)S(1)}, bf16[128,512]{1,0:T(8,128)(2,1)S(1)}, u32[]{:S(2)}, u32[]{:S(2)}) collective-permute-start(bf16[128,512]{1,0:T(8,128)(2,1)S(1)} %shard_map.134), channel_id=1, source_target_pairs={{0,0},{8,136},{16,400},{24,280},{32,352},{40,488},{48,240},{56,120... | collective-permute-start | bytes 393224 | tf_op jit(solution)/shard_map/ppermute | solution.py:359
  111.0 6.1 %collective-permute-start.7 = (bf16[128,512]{1,0:T(8,128)(2,1)S(1)}, bf16[128,512]{1,0:T(8,128)(2,1)S(1)}, u32[]{:S(2)}, u32[]{:S(2)}) collective-permute-start(bf16[128,512]{1,0:T(8,128)(2,1)S(1)} %get-tuple-element.29), channel_id=1, source_target_pairs={{0,384},{128,0},{256,128},{384,256},{1,385},{129,1},{257,129},{385... | collective-permute-start | bytes 393224 | tf_op jit(solution)/shard_map/ppermute | solution.py:304
  117.1 3.1 %collective-permute-start.8 = (bf16[128,512]{1,0:T(8,128)(2,1)S(1)}, bf16[128,512]{1,0:T(8,128)(2,1)S(1)}, u32[]{:S(2)}, u32[]{:S(2)}) collective-permute-start(bf16[128,512]{1,0:T(8,128)(2,1)S(1)} %get-tuple-element.30), channel_id=1, source_target_pairs={{0,256},{128,384},{256,0},{384,128},{1,257},{129,385},{257,1},{385... | collective-permute-start | bytes 393224 | tf_op jit(solution)/shard_map/ppermute | solution.py:304
  120.2 2.8 %collective-permute-start.9 = (bf16[128,512]{1,0:T(8,128)(2,1)S(1)}, bf16[128,512]{1,0:T(8,128)(2,1)S(1)}, u32[]{:S(2)}, u32[]{:S(2)}) collective-permute-start(bf16[128,512]{1,0:T(8,128)(2,1)S(1)} %get-tuple-element.31), channel_id=1, source_target_pairs={{0,128},{128,256},{256,384},{384,0},{1,129},{129,257},{257,385},{3... | collective-permute-start | bytes 393224 | tf_op jit(solution)/shard_map/ppermute | solution.py:304
  124.1 1.3 shard_map.135
  125.5 9.2 %all-to-all-start.4 = ((bf16[32,32,128]{2,1,0:T(8,128)(2,1)}), bf16[32,32,128]{2,1,0:T(8,128)(2,1)S(1)}, u32[]{:S(2)}, u32[]{:S(2)}) async-start(bf16[32,32,128]{2,1,0:T(8,128)(2,1)} %bitcast.13), calls=%async_computation.4 | async-start | bytes 524288 | tf_op jit(solution)/shard_map/all_to_all | solution.py:300
  134.9 1.9 %collective-permute-start.10 = (bf16[128,512]{1,0:T(8,128)(2,1)S(1)}, bf16[128,512]{1,0:T(8,128)(2,1)S(1)}, u32[]{:S(2)}, u32[]{:S(2)}) collective-permute-start(bf16[128,512]{1,0:T(8,128)(2,1)S(1)} %shard_map.136), channel_id=1, source_target_pairs={{0,0},{8,136},{16,400},{24,280},{32,352},{40,488},{48,240},{56,120... | collective-permute-start | bytes 393224 | tf_op jit(solution)/shard_map/ppermute | solution.py:366
  136.8 12.0 %collective-permute-done.10.got_ref = bf16[128,512]{1,0:T(8,128)(2,1)S(1)} collective-permute-done((bf16[128,512]{1,0:T(8,128)(2,1)S(1)}, bf16[128,512]{1,0:T(8,128)(2,1)S(1)}, u32[]{:S(2)}, u32[]{:S(2)}) %collective-permute-start.10) | collective-permute-done | bytes 131104 | tf_op jit(solution)/shard_map/ppermute | solution.py:366
  (38 shorter events, 9.2 us)
Async XLA Ops:
  0.6 24.6 %copy-start = (s32[8,2]{0,1:T(2,128)S(1)}, s32[8,2]{0,1:T(2,128)}, u32[]{:S(2)}) copy-start(s32[8,2]{0,1:T(2,128)} %param.17) | copy-start | bytes 196
  1.3 17.4 %copy-start.4 = (bf16[2,26,1024]{2,0,1:T(2,128)(2,1)S(1)}, bf16[2,26,1024]{2,0,1:T(2,128)(2,1)}, u32[]{:S(2)}) copy-start(bf16[2,26,1024]{2,0,1:T(2,128)(2,1)} %param.11) | copy-start | bytes 319492
  3.2 15.5 %copy-start.5 = (bf16[2,26,1024]{2,0,1:T(2,128)(2,1)S(1)}, bf16[2,26,1024]{2,0,1:T(2,128)(2,1)}, u32[]{:S(2)}) copy-start(bf16[2,26,1024]{2,0,1:T(2,128)(2,1)} %param.12) | copy-start | bytes 319492
  3.3 30.9 %collective-permute-start = (bf16[256,512]{1,0:T(8,128)(2,1)}, bf16[256,512]{1,0:T(8,128)(2,1)S(1)}, u32[]{:S(2)}, u32[]{:S(2)}) collective-permute-start(bf16[256,512]{1,0:T(8,128)(2,1)} %get-tuple-element.22), channel_id=1, source_target_pairs={{0,0},{136,8},{400,16},{280,24},{352,32},{488,40},{240,48},{120,56... | collective-permute-start | bytes 786440 | tf_op jit(solution)/shard_map/ppermute | solution.py:331
  18.8 0.7 copy-start.2
  20.3 13.8 %all-to-all-start = ((bf16[32,32,128]{2,1,0:T(8,128)(2,1)}), bf16[32,32,128]{2,1,0:T(8,128)(2,1)S(1)}, u32[]{:S(2)}, u32[]{:S(2)}) async-start(bf16[32,32,128]{2,1,0:T(8,128)(2,1)} %bitcast.6), calls=%async_computation | async-start | bytes 524288 | tf_op jit(solution)/shard_map/all_to_all | solution.py:300
  35.4 28.8 %copy-start.6 = (s32[8,1024]{1,0:T(8,128)S(1)}, s32[8,1024]{1,0:T(8,128)}, u32[]{:S(2)}) copy-start(s32[8,1024]{1,0:T(8,128)} %param.18) | copy-start | bytes 98308
  35.5 21.0 %all-to-all-start.1 = ((bf16[16,56,128]{2,1,0:T(8,128)(2,1)}), bf16[16,56,128]{2,1,0:T(8,128)(2,1)S(1)}, u32[]{:S(2)}, u32[]{:S(2)}) async-start(bf16[16,56,128]{2,1,0:T(8,128)(2,1)} %bitcast.8), calls=%async_computation.1 | async-start | bytes 458752 | tf_op jit(solution)/shard_map/all_to_all | solution.py:300
  43.9 20.5 %collective-permute-start.4 = (bf16[256,512]{1,0:T(8,128)(2,1)S(1)}, bf16[256,512]{1,0:T(8,128)(2,1)S(1)}, u32[]{:S(2)}, u32[]{:S(2)}) collective-permute-start(bf16[256,512]{1,0:T(8,128)(2,1)S(1)} %collective-permute-done.q0), channel_id=1, source_target_pairs={{0,384},{128,0},{256,128},{384,256},{1,385},{129,1},{257,129},{385... | collective-permute-start | bytes 786440 | tf_op jit(solution)/shard_map/ppermute | solution.py:304
  48.4 16.0 %collective-permute-start.3 = (bf16[256,512]{1,0:T(8,128)(2,1)S(1)}, bf16[256,512]{1,0:T(8,128)(2,1)S(1)}, u32[]{:S(2)}, u32[]{:S(2)}) collective-permute-start(bf16[256,512]{1,0:T(8,128)(2,1)S(1)} %collective-permute-done.q0), channel_id=1, source_target_pairs={{0,256},{128,384},{256,0},{384,128},{1,257},{129,385},{257,1},{385... | collective-permute-start | bytes 786440 | tf_op jit(solution)/shard_map/ppermute | solution.py:304
  52.1 12.3 %collective-permute-start.2 = (bf16[256,512]{1,0:T(8,128)(2,1)S(1)}, bf16[256,512]{1,0:T(8,128)(2,1)S(1)}, u32[]{:S(2)}, u32[]{:S(2)}) collective-permute-start(bf16[256,512]{1,0:T(8,128)(2,1)S(1)} %collective-permute-done.q0), channel_id=1, source_target_pairs={{0,128},{128,256},{256,384},{384,0},{1,129},{129,257},{257,385},{3... | collective-permute-start | bytes 786440 | tf_op jit(solution)/shard_map/ppermute | solution.py:304
  56.5 8.8 %collective-permute-start.1 = (bf16[896,128]{1,0:T(8,128)(2,1)S(1)}, bf16[896,128]{1,0:T(8,128)(2,1)S(1)}, u32[]{:S(2)}, u32[]{:S(2)}) collective-permute-start(bf16[896,128]{1,0:T(8,128)(2,1)S(1)} %bitcast.21), channel_id=1, source_target_pairs={{0,64},{64,0},{1,65},{65,1},{2,66},{66,2},{3,67},{67,3},{4,68},{68... | collective-permute-start | bytes 688136 | tf_op jit(solution)/shard_map/ppermute | solution.py:308
  64.3 1.1 copy-start.3
  89.2 4.8 %collective-permute-start.5 = (bf16[896,128]{1,0:T(8,128)(2,1)S(1)}, bf16[896,128]{1,0:T(8,128)(2,1)S(1)}, u32[]{:S(2)}, u32[]{:S(2)}) collective-permute-start(bf16[896,128]{1,0:T(8,128)(2,1)S(1)} %get-tuple-element.26), channel_id=1, source_target_pairs={{0,64},{64,0},{1,65},{65,1},{2,66},{66,2},{3,67},{67,3},{4,68},{68... | collective-permute-start | bytes 688136 | tf_op jit(solution)/shard_map/ppermute | solution.py:308
  94.7 29.4 %all-to-all-start.3 = ((bf16[16,56,128]{2,1,0:T(8,128)(2,1)}), bf16[16,56,128]{2,1,0:T(8,128)(2,1)S(1)}, u32[]{:S(2)}, u32[]{:S(2)}) async-start(bf16[16,56,128]{2,1,0:T(8,128)(2,1)} %bitcast.10), calls=%async_computation.3 | async-start | bytes 458752 | tf_op jit(solution)/shard_map/all_to_all | solution.py:300
  103.0 21.1 %collective-permute-start.6 = (bf16[128,512]{1,0:T(8,128)(2,1)S(1)}, bf16[128,512]{1,0:T(8,128)(2,1)S(1)}, u32[]{:S(2)}, u32[]{:S(2)}) collective-permute-start(bf16[128,512]{1,0:T(8,128)(2,1)S(1)} %shard_map.134), channel_id=1, source_target_pairs={{0,0},{8,136},{16,400},{24,280},{32,352},{40,488},{48,240},{56,120... | collective-permute-start | bytes 393224 | tf_op jit(solution)/shard_map/ppermute | solution.py:359
  111.0 23.7 %collective-permute-start.7 = (bf16[128,512]{1,0:T(8,128)(2,1)S(1)}, bf16[128,512]{1,0:T(8,128)(2,1)S(1)}, u32[]{:S(2)}, u32[]{:S(2)}) collective-permute-start(bf16[128,512]{1,0:T(8,128)(2,1)S(1)} %get-tuple-element.29), channel_id=1, source_target_pairs={{0,384},{128,0},{256,128},{384,256},{1,385},{129,1},{257,129},{385... | collective-permute-start | bytes 393224 | tf_op jit(solution)/shard_map/ppermute | solution.py:304
  117.1 17.6 %collective-permute-start.8 = (bf16[128,512]{1,0:T(8,128)(2,1)S(1)}, bf16[128,512]{1,0:T(8,128)(2,1)S(1)}, u32[]{:S(2)}, u32[]{:S(2)}) collective-permute-start(bf16[128,512]{1,0:T(8,128)(2,1)S(1)} %get-tuple-element.30), channel_id=1, source_target_pairs={{0,256},{128,384},{256,0},{384,128},{1,257},{129,385},{257,1},{385... | collective-permute-start | bytes 393224 | tf_op jit(solution)/shard_map/ppermute | solution.py:304
  120.2 14.5 %collective-permute-start.9 = (bf16[128,512]{1,0:T(8,128)(2,1)S(1)}, bf16[128,512]{1,0:T(8,128)(2,1)S(1)}, u32[]{:S(2)}, u32[]{:S(2)}) collective-permute-start(bf16[128,512]{1,0:T(8,128)(2,1)S(1)} %get-tuple-element.31), channel_id=1, source_target_pairs={{0,128},{128,256},{256,384},{384,0},{1,129},{129,257},{257,385},{3... | collective-permute-start | bytes 393224 | tf_op jit(solution)/shard_map/ppermute | solution.py:304
  125.5 24.2 %all-to-all-start.4 = ((bf16[32,32,128]{2,1,0:T(8,128)(2,1)}), bf16[32,32,128]{2,1,0:T(8,128)(2,1)S(1)}, u32[]{:S(2)}, u32[]{:S(2)}) async-start(bf16[32,32,128]{2,1,0:T(8,128)(2,1)} %bitcast.13), calls=%async_computation.4 | async-start | bytes 524288 | tf_op jit(solution)/shard_map/all_to_all | solution.py:300
  134.7 14.1 %copy-start.1 = (bf16[1,128,512]{2,1,0:T(8,128)(2,1)S(1)}, bf16[1,128,512]{2,1,0:T(8,128)(2,1)}, u32[]{:S(2)}) copy-start(bf16[1,128,512]{2,1,0:T(8,128)(2,1)} %queries_ref.3) | copy-start | bytes 393220
  134.9 13.9 %collective-permute-start.10 = (bf16[128,512]{1,0:T(8,128)(2,1)S(1)}, bf16[128,512]{1,0:T(8,128)(2,1)S(1)}, u32[]{:S(2)}, u32[]{:S(2)}) collective-permute-start(bf16[128,512]{1,0:T(8,128)(2,1)S(1)} %shard_map.136), channel_id=1, source_target_pairs={{0,0},{8,136},{16,400},{24,280},{32,352},{40,488},{48,240},{56,120... | collective-permute-start | bytes 393224 | tf_op jit(solution)/shard_map/ppermute | solution.py:366

commit v6 on v4

--- a/solution.py
+++ b/solution.py
@@ -17,6 +17,7 @@
 SCALE = 1.0 / math.sqrt(HD)
 SCALE_LOG2 = SCALE / math.log(2.0)
 F32 = jnp.float32
+HEAVY = 20_000_000_000
 BF16 = jnp.bfloat16
 
 Y, CORE, Z, N_O, N_C = 4, 2, 8, 8, 8
@@ -55,11 +56,11 @@
     return jnp.tanh(jnp.full((1, HD), gate_ref[0], F32))
 
 
-def pack_queries(gate_ref, queries_ref, d_out_ref, q_gain_ref, k_gain_ref, out_ref, gains_ref, x_s, d_s, sems):
+def pack_queries(gate_ref, queries_ref, d_out_ref, gain_ref, out_ref, x_s, d_s, gain_s, sems):
     copies = [
         pltpu.make_async_copy(source, target, sems.at[i])
         for i, (source, target) in enumerate(
-            ((queries_ref.at[0], x_s), (d_out_ref.at[0], d_s), (q_gain_ref, gains_ref.at[0:1]), (k_gain_ref, gains_ref.at[1:2]))
+            ((queries_ref.at[0], x_s), (d_out_ref.at[0], d_s), (gain_ref, gain_s))
         )
     ]
     for copy in copies:
@@ -67,7 +68,7 @@
     gate = gate_value(gate_ref)
     for copy in copies:
         copy.wait()
-    gain = gains_ref[0:1]
+    gain = gain_s[...]
     for g in range(4):
         lanes = slice(g * HD, (g + 1) * HD)
         x = x_s[:, lanes].astype(F32)
@@ -76,8 +77,15 @@
         out_ref[128:256, lanes] = (gate * d_s[:, lanes].astype(F32)).astype(BF16)
 
 
-def pack_keys(keys_ref, values_ref, gains_ref, out_ref):
-    gain = gains_ref[1:2]
+def turn(packed_ref, out_ref):
+    for g in range(4):
+        lanes = slice(g * HD, (g + 1) * HD)
+        for rows in (slice(0, 128), slice(128, 256)):
+            out_ref[rows, lanes] = packed_ref[rows, lanes].astype(F32).T.astype(BF16)
+
+
+def pack_keys(keys_ref, values_ref, gain_ref, out_ref):
+    gain = gain_ref[...]
     for n in range(2):
         for head in range(8):
             hhi, hx = divmod(head, 4)
@@ -129,12 +137,8 @@
     return jnp.where((i < HALF - 0.5) & (row < TILE - 0.5), 1.0, 0.0).astype(F32)
 
 
-def columns(rows):
-    return jnp.concatenate([rows[:, g * HD : (g + 1) * HD].astype(F32).T for g in range(4)], axis=1)
-
-
-def stacked(rows):
-    return jnp.concatenate([rows[:, g * HD : (g + 1) * HD] for g in range(4)], axis=0)
+def stacked(columns):
+    return jnp.concatenate([columns[:, g * HD : (g + 1) * HD].astype(F32).T.astype(BF16) for g in range(4)], axis=0)
 
 
 def seen_row(ids_ref, count_ref, visible_ref, j):
@@ -179,8 +183,8 @@
         q_s[j] = q[...]
 
     def block(j, carry):
-        q_t = columns(q_s[j, 0:128, :]).astype(BF16)
-        o_t = columns(q_s[j, 128:256, :])
+        q_t = q_s[j, 0:128, :]
+        o_t = q_s[j, 128:256, :].astype(F32)
         acc = dot(turned_s[...], weights_of(keys_s, q_t).astype(BF16))
         acc = acc * seen_row(ids_ref, count_ref, visible_ref, j)
         both = jnp.concatenate([acc[HD : HD + 1], jnp.sum(acc[:HD] * o_t, axis=0, keepdims=True)], axis=0)
@@ -216,10 +220,10 @@
         q_s[j] = q[...]
 
     def block(j, carry):
-        q_t = columns(q_s[j, 0:128, :]).astype(BF16)
-        o_t = columns(q_s[j, 128:256, :]).astype(BF16)
-        q_rows = stacked(q_s[j, 0:128, :])
-        o_rows = stacked(q_s[j, 128:256, :])
+        q_t = q_s[j, 0:128, :]
+        o_t = q_s[j, 128:256, :]
+        q_rows = stacked(q_t)
+        o_rows = stacked(o_t)
         inverse, delta = all_sums(ids_ref, sums_ref, j)
         acc = (acc_ref[j] * inverse).astype(BF16)
         inverse = inverse * seen_row(ids_ref, count_ref, visible_ref, j)
@@ -264,8 +268,8 @@
     return inverse * scaled - x * (inverse * inverse * inverse * dots)
 
 
-def finish_queries(queries_ref, got_ref, gains_ref, attended_ref, out_ref):
-    gain = gains_ref[0:1]
+def finish_queries(queries_ref, got_ref, gain_ref, attended_ref, out_ref):
+    gain = gain_ref[...]
     attended_ref[0] = got_ref[0:128, :]
     for g in range(4):
         lanes = slice(g * HD, (g + 1) * HD)
@@ -273,8 +277,8 @@
         out_ref[0, :, lanes] = norm_back(x, got_ref[128:256, lanes].astype(F32), gain).astype(BF16)
 
 
-def finish_keys(keys_ref, got_ref, gains_ref, dk_ref, dv_ref):
-    gain = gains_ref[1:2]
+def finish_keys(keys_ref, got_ref, gain_ref, dk_ref, dv_ref):
+    gain = gain_ref[...]
     for n in range(2):
         for head in range(8):
             hhi, hx = divmod(head, 4)
@@ -314,17 +318,17 @@
     owner = lax.dynamic_index_in_dim(tile_owner, y // 2, 1, keepdims=False)
     seen = visible.reshape(64, 128)
 
-    buffers = [pltpu.VMEM((128, 512), BF16), pltpu.VMEM((128, 512), BF16), pltpu.SemaphoreType.DMA((4,))]
-    packed, gains = call(
+    (packed_kv,) = call(pack_keys, [shape((8, 4, 32, HD), BF16)], keys, values, k_gain)
+    packed_kv, queries = lax.optimization_barrier((packed_kv, queries))
+    buffers = [pltpu.VMEM((128, 512), BF16), pltpu.VMEM((128, 512), BF16), pltpu.VMEM((1, HD), F32), pltpu.SemaphoreType.DMA((3,))]
+    (packed,) = call(
         pack_queries,
-        [shape((256, 512), BF16), shape((2, HD), F32)],
-        gate, queries, d_out, q_gain, k_gain,
-        smem=1, hbm=4, scratch=buffers, limit=60 << 20,
+        [shape((256, 512), BF16)],
+        gate, queries, d_out, q_gain,
+        smem=1, hbm=3, scratch=buffers, limit=60 << 20,
     )
-    q0 = lax.ppermute(packed, PLANES, TO_PLANE)
-    (packed_kv,) = call(pack_keys, [shape((8, 4, 32, HD), BF16)], keys, values, gains)
+    (q0,) = call(turn, [shape((256, 512), BF16)], lax.ppermute(packed, PLANES, TO_PLANE), flops=HEAVY)
     got = exchange(packed_kv.reshape(32, 32, HD), ("y", "core", "x"))
-    got, q0 = lax.optimization_barrier((got, q0))
     (chosen,) = call(choose_tiles, [shape((2, 8, BLOCK, HD), BF16)], owner, got.reshape(8, 4, 32, HD), smem=1)
     mine = exchange(chosen.reshape(16, BLOCK, HD), ("zhi", "seq")).reshape(MID, HD)
     q1, q2, q3 = rotated(q0, 1), rotated(q0, 2), rotated(q0, 3)
@@ -355,8 +359,8 @@
     r1, r2, r3, placed = lax.optimization_barrier((r1, r2, r3, placed))
     (summed,) = call(sum_tokens, [shape((256, 512), BF16)], gate, r0, r1, r2, r3, smem=1)
     summed = lax.ppermute(summed, PLANES, FROM_PLANE)
-    d_keys, d_values = call(finish_keys, [shape(keys.shape, BF16), shape(values.shape, BF16)], keys, home, gains, flops=20_000_000_000)
-    attended, d_queries = call(finish_queries, [shape(queries.shape, BF16)] * 2, queries, summed, gains)
+    d_keys, d_values = call(finish_keys, [shape(keys.shape, BF16), shape(values.shape, BF16)], keys, home, k_gain, flops=HEAVY)
+    attended, d_queries = call(finish_queries, [shape(queries.shape, BF16)] * 2, queries, summed, q_gain)
     return (attended, d_queries, d_keys, d_values)
 
 

time: 146 us -> 147 us (level)
  starting transfers between devices: 85 us -> 87.6 us
    all_to_all x4, starting transfers between devices: 41.3 us -> 43 us  [exchange(): return lax.all_to_all(value, axes, split_axis=0, concat_axis=0, tiled=True)]
    pallas_call x9 -> x10, Pallas kernels: 15.9 us -> 15.8 us  [call(): pl.pallas_call(kernel, out_shape=outs, in_specs=specs, out_specs=[pl.Bloc...]
where the time goes in v6:
time: 147 us; the launch traced here: 146 us
  starting transfers between devices  87.6 us (60%)
  waiting for transfers between devices  29.3 us (20%)
  Pallas kernels  15.8 us (11%)
  blocking collectives  7.47 us (5%)
  local copies, waits for them, and re-layouts  3.19 us (2%)
  between operations  1.6 us (1%)
    all_to_all x4, starting transfers between devices, exchange(): return lax.all_to_all(value, axes, split_axis=0, concat_axis=0, tiled=True)  43 us
    ppermute x6, starting transfers between devices, rotated(): return lax.ppermute(value, 'y', [(i, (i + k) % Y) for i in range(Y)])  20 us
    pallas_call x10, Pallas kernels, call(): pl.pallas_call(kernel, out_shape=outs, in_specs=specs, out_specs=[pl.Bloc...  15.8 us
    all_to_all x4, waiting for transfers between devices, exchange(): return lax.all_to_all(value, axes, split_axis=0, concat_axis=0, tiled=True)  14.3 us
    ppermute x1, waiting for transfers between devices, shards(): summed = lax.ppermute(summed, PLANES, FROM_PLANE)  12.9 us
    ppermute x2, starting transfers between devices, swapped(): return lax.ppermute(value, 'core', [(0, 1), (1, 0)])  10.1 us
    ppermute x1, starting transfers between devices, shards(): lax.ppermute(packed, PLANES, TO_PLANE)  8.48 us
    all_to_all x1, blocking collectives, exchange(): return lax.all_to_all(value, axes, split_axis=0, concat_axis=0, tiled=True)  7.47 us
  transfers between devices with their start and end apart: 14, of which 7 were waited for; matrix products, arithmetic and copies ran while one was open for 1% of the time, Pallas kernels for 2%

profile of v6, /device:TPU:25, one launch (start us, length us, event | category | flops | bytes accessed | tf_op | source)
XLA Modules:
  0.0 145.8 jit_solution(450966284830522485)
XLA Ops:
  3.8 1.9 %shard_map.131 = bf16[256,512]{1,0:T(8,128)(2,1)} custom-call(f32[1]{0:T(128)S(6)} %copy.19.gate_ref, bf16[1,128,512]{2,1,0:T(8,128)(2,1)} %queries_ref.1, bf16[1,128,512]{2,1,0:T(8,128)(2,1)} %d_out_ref.1, f32[1,128]{1,0:T(1,128)} %bitcast.21), custom_call_target="tpu_custom_call" | custom-call | bytes 524804 | tf_op jit(solution)/shard_map/pallas_call | solution.py:40
  5.7 8.5 %collective-permute-start.1 = (bf16[256,512]{1,0:T(8,128)(2,1)}, bf16[256,512]{1,0:T(8,128)(2,1)S(1)}, u32[]{:S(2)}, u32[]{:S(2)}) collective-permute-start(bf16[256,512]{1,0:T(8,128)(2,1)} %shard_map.131), channel_id=1, source_target_pairs={{0,0},{136,8},{272,16},{408,24},{480,32},{360,40},{240,48},{120,56... | collective-permute-start | bytes 786440 | tf_op jit(solution)/shard_map/ppermute | solution.py:330
  14.2 10.5 %all-to-all-start = ((bf16[32,32,128]{2,1,0:T(8,128)(2,1)}), bf16[32,32,128]{2,1,0:T(8,128)(2,1)S(1)}, u32[]{:S(2)}, u32[]{:S(2)}) async-start(bf16[32,32,128]{2,1,0:T(8,128)(2,1)} %bitcast.5), calls=%async_computation | async-start | bytes 524288 | tf_op jit(solution)/shard_map/all_to_all | solution.py:297
  24.7 7.1 %all-to-all-done = bf16[32,32,128]{2,1,0:T(8,128)(2,1)S(1)} async-done(((bf16[32,32,128]{2,1,0:T(8,128)(2,1)}), bf16[32,32,128]{2,1,0:T(8,128)(2,1)S(1)}, u32[]{:S(2)}, u32[]{:S(2)}) %all-to-all-start) | async-done | bytes 262176 | tf_op jit(solution)/shard_map/all_to_all | solution.py:297
  31.8 1.3 shard_map.130
  33.1 10.2 %all-to-all-start.1 = ((bf16[16,56,128]{2,1,0:T(8,128)(2,1)}), bf16[16,56,128]{2,1,0:T(8,128)(2,1)S(1)}, u32[]{:S(2)}, u32[]{:S(2)}) async-start(bf16[16,56,128]{2,1,0:T(8,128)(2,1)} %bitcast.7), calls=%async_computation.1 | async-start | bytes 458752 | tf_op jit(solution)/shard_map/all_to_all | solution.py:297
  43.4 3.9 %collective-permute-start.4 = (bf16[256,512]{1,0:T(8,128)(2,1)S(1)}, bf16[256,512]{1,0:T(8,128)(2,1)S(1)}, u32[]{:S(2)}, u32[]{:S(2)}) collective-permute-start(bf16[256,512]{1,0:T(8,128)(2,1)S(1)} %shard_map.132.q0), channel_id=1, source_target_pairs={{0,384},{128,0},{256,128},{384,256},{1,385},{129,1},{257,129},{385... | collective-permute-start | bytes 786440 | tf_op jit(solution)/shard_map/ppermute | solution.py:301
  47.4 3.6 %collective-permute-start.3 = (bf16[256,512]{1,0:T(8,128)(2,1)S(1)}, bf16[256,512]{1,0:T(8,128)(2,1)S(1)}, u32[]{:S(2)}, u32[]{:S(2)}) collective-permute-start(bf16[256,512]{1,0:T(8,128)(2,1)S(1)} %shard_map.132.q0), channel_id=1, source_target_pairs={{0,256},{128,384},{256,0},{384,128},{1,257},{129,385},{257,1},{385... | collective-permute-start | bytes 786440 | tf_op jit(solution)/shard_map/ppermute | solution.py:301
  51.0 2.8 %collective-permute-start.2 = (bf16[256,512]{1,0:T(8,128)(2,1)S(1)}, bf16[256,512]{1,0:T(8,128)(2,1)S(1)}, u32[]{:S(2)}, u32[]{:S(2)}) collective-permute-start(bf16[256,512]{1,0:T(8,128)(2,1)S(1)} %shard_map.132.q0), channel_id=1, source_target_pairs={{0,128},{128,256},{256,384},{384,0},{1,129},{129,257},{257,385},{3... | collective-permute-start | bytes 786440 | tf_op jit(solution)/shard_map/ppermute | solution.py:301
  53.9 2.6 %all-to-all-done.1 = bf16[16,56,128]{2,1,0:T(8,128)(2,1)S(1)} async-done(((bf16[16,56,128]{2,1,0:T(8,128)(2,1)}), bf16[16,56,128]{2,1,0:T(8,128)(2,1)S(1)}, u32[]{:S(2)}, u32[]{:S(2)}) %all-to-all-start.1) | async-done | bytes 229408 | tf_op jit(solution)/shard_map/all_to_all | solution.py:297
  56.5 6.7 %collective-permute-start = (bf16[896,128]{1,0:T(8,128)(2,1)S(1)}, bf16[896,128]{1,0:T(8,128)(2,1)S(1)}, u32[]{:S(2)}, u32[]{:S(2)}) collective-permute-start(bf16[896,128]{1,0:T(8,128)(2,1)S(1)} %bitcast.18), channel_id=1, source_target_pairs={{0,64},{64,0},{1,65},{65,1},{2,66},{66,2},{3,67},{67,3},{4,68},{68... | collective-permute-start | bytes 688136 | tf_op jit(solution)/shard_map/ppermute | solution.py:305
  64.3 2.9 %shard_map.133 = (f32[4,128,512]{2,1,0:T(8,128)S(1)}, f32[4,4,2,512]{3,2,1,0:T(2,128)S(1)}) custom-call(s32[3]{0:T(128)S(1)} %pad_add_fusion.ids_ref, s32[8]{0:T(128)S(1)} %copy-done.4, s32[64,128]{1,0:T(8,128)S(1)} %reshape.42.visible_ref, bf16[896,128]{1,0:T(8,128)(2,1)S(1)} %bitcast.19, bf16[896,128]{1,0:T(8,128)(2,1)S(1)} %collective-permute-done.other_ref, ...), custom_call_target="tpu_custom_call" | custom-call | flops 939524096 | bytes 2654252 | tf_op jit(solution)/shard_map/pallas_call | solution.py:40
  67.2 7.5 %all_to_all.25.sums_ref = f32[4,4,2,512]{3,2,1,0:T(2,128)S(1)} all-to-all(f32[4,4,2,512]{3,2,1,0:T(2,128)S(1)} %get-tuple-element.24), channel_id=1, replica_groups=mesh['y'=4,'core'=2,'seq'=8,'zhi'=2,'x'=4] {'y'}, dimensions={0} | all-to-all | bytes 131072 | tf_op jit(solution)/shard_map/all_to_all | solution.py:297
  74.6 6.1 %shard_map.134 = (bf16[256,512]{1,0:T(8,128)(2,1)S(1)}, bf16[256,512]{1,0:T(8,128)(2,1)S(1)}, bf16[256,512]{1,0:T(8,128)(2,1)S(1)}, bf16[256,512]{1,0:T(8,128)(2...) custom-call(s32[3]{0:T(128)S(1)} %pad_add_fusion.ids_ref, s32[8]{0:T(128)S(1)} %copy-done.4, ...), custom_call_target="tpu_custom_call" | custom-call | flops 2348810240 | bytes 4390956 | tf_op jit(solution)/shard_map/pallas_call | solution.py:40
  80.7 3.4 %collective-permute-start.8 = (bf16[896,128]{1,0:T(8,128)(2,1)S(1)}, bf16[896,128]{1,0:T(8,128)(2,1)S(1)}, u32[]{:S(2)}, u32[]{:S(2)}) collective-permute-start(bf16[896,128]{1,0:T(8,128)(2,1)S(1)} %get-tuple-element.30), channel_id=1, source_target_pairs={{0,64},{64,0},{1,65},{65,1},{2,66},{66,2},{3,67},{67,3},{4,68},{68... | collective-permute-start | bytes 688136 | tf_op jit(solution)/shard_map/ppermute | solution.py:305
  86.0 11.2 %all-to-all-start.3 = ((bf16[16,56,128]{2,1,0:T(8,128)(2,1)}), bf16[16,56,128]{2,1,0:T(8,128)(2,1)S(1)}, u32[]{:S(2)}, u32[]{:S(2)}) async-start(bf16[16,56,128]{2,1,0:T(8,128)(2,1)} %bitcast.10), calls=%async_computation.3 | async-start | bytes 458752 | tf_op jit(solution)/shard_map/all_to_all | solution.py:297
  97.2 2.0 %collective-permute-start.5 = (bf16[256,512]{1,0:T(8,128)(2,1)S(1)}, bf16[256,512]{1,0:T(8,128)(2,1)S(1)}, u32[]{:S(2)}, u32[]{:S(2)}) collective-permute-start(bf16[256,512]{1,0:T(8,128)(2,1)S(1)} %get-tuple-element.26), channel_id=1, source_target_pairs={{0,384},{128,0},{256,128},{384,256},{1,385},{129,1},{257,129},{385... | collective-permute-start | bytes 786440 | tf_op jit(solution)/shard_map/ppermute | solution.py:301
  99.2 4.8 %collective-permute-start.6 = (bf16[256,512]{1,0:T(8,128)(2,1)S(1)}, bf16[256,512]{1,0:T(8,128)(2,1)S(1)}, u32[]{:S(2)}, u32[]{:S(2)}) collective-permute-start(bf16[256,512]{1,0:T(8,128)(2,1)S(1)} %get-tuple-element.27), channel_id=1, source_target_pairs={{0,256},{128,384},{256,0},{384,128},{1,257},{129,385},{257,1},{385... | collective-permute-start | bytes 786440 | tf_op jit(solution)/shard_map/ppermute | solution.py:301
  104.0 2.8 %collective-permute-start.7 = (bf16[256,512]{1,0:T(8,128)(2,1)S(1)}, bf16[256,512]{1,0:T(8,128)(2,1)S(1)}, u32[]{:S(2)}, u32[]{:S(2)}) collective-permute-start(bf16[256,512]{1,0:T(8,128)(2,1)S(1)} %get-tuple-element.28), channel_id=1, source_target_pairs={{0,128},{128,256},{256,384},{384,0},{1,129},{129,257},{257,385},{3... | collective-permute-start | bytes 786440 | tf_op jit(solution)/shard_map/ppermute | solution.py:301
  106.8 3.8 %all-to-all-done.3 = bf16[16,56,128]{2,1,0:T(8,128)(2,1)S(1)} async-done(((bf16[16,56,128]{2,1,0:T(8,128)(2,1)}), bf16[16,56,128]{2,1,0:T(8,128)(2,1)S(1)}, u32[]{:S(2)}, u32[]{:S(2)}) %all-to-all-start.3) | async-done | bytes 229408 | tf_op jit(solution)/shard_map/all_to_all | solution.py:297
  110.6 1.3 shard_map.135
  111.9 11.2 %all-to-all-start.4 = ((bf16[32,32,128]{2,1,0:T(8,128)(2,1)}), bf16[32,32,128]{2,1,0:T(8,128)(2,1)S(1)}, u32[]{:S(2)}, u32[]{:S(2)}) async-start(bf16[32,32,128]{2,1,0:T(8,128)(2,1)} %bitcast.12), calls=%async_computation.4 | async-start | bytes 524288 | tf_op jit(solution)/shard_map/all_to_all | solution.py:297
  123.4 6.0 %collective-permute-start.9 = (bf16[256,512]{1,0:T(8,128)(2,1)S(1)}, bf16[256,512]{1,0:T(8,128)(2,1)S(1)}, u32[]{:S(2)}, u32[]{:S(2)}) collective-permute-start(bf16[256,512]{1,0:T(8,128)(2,1)S(1)} %shard_map.136), channel_id=1, source_target_pairs={{0,0},{8,136},{16,272},{24,408},{32,480},{40,360},{48,240},{56,120... | collective-permute-start | bytes 786440 | tf_op jit(solution)/shard_map/ppermute | solution.py:361
  132.0 12.9 %collective-permute-done.9.got_ref = bf16[256,512]{1,0:T(8,128)(2,1)S(1)} collective-permute-done((bf16[256,512]{1,0:T(8,128)(2,1)S(1)}, bf16[256,512]{1,0:T(8,128)(2,1)S(1)}, u32[]{:S(2)}, u32[]{:S(2)}) %collective-permute-start.9) | collective-permute-done | bytes 262176 | tf_op jit(solution)/shard_map/ppermute | solution.py:361
  (37 shorter events, 9.2 us)
Async XLA Ops:
  0.6 24.1 %copy-start = (s32[8,2]{0,1:T(2,128)S(1)}, s32[8,2]{0,1:T(2,128)}, u32[]{:S(2)}) copy-start(s32[8,2]{0,1:T(2,128)} %param.17) | copy-start | bytes 196
  1.3 1.0 copy-start.5
  2.3 0.7 copy-start.3
  5.7 37.6 %collective-permute-start.1 = (bf16[256,512]{1,0:T(8,128)(2,1)}, bf16[256,512]{1,0:T(8,128)(2,1)S(1)}, u32[]{:S(2)}, u32[]{:S(2)}) collective-permute-start(bf16[256,512]{1,0:T(8,128)(2,1)} %shard_map.131), channel_id=1, source_target_pairs={{0,0},{136,8},{272,16},{408,24},{480,32},{360,40},{240,48},{120,56... | collective-permute-start | bytes 786440 | tf_op jit(solution)/shard_map/ppermute | solution.py:330
  14.2 17.6 %all-to-all-start = ((bf16[32,32,128]{2,1,0:T(8,128)(2,1)}), bf16[32,32,128]{2,1,0:T(8,128)(2,1)S(1)}, u32[]{:S(2)}, u32[]{:S(2)}) async-start(bf16[32,32,128]{2,1,0:T(8,128)(2,1)} %bitcast.5), calls=%async_computation | async-start | bytes 524288 | tf_op jit(solution)/shard_map/all_to_all | solution.py:297
  33.1 23.4 %all-to-all-start.1 = ((bf16[16,56,128]{2,1,0:T(8,128)(2,1)}), bf16[16,56,128]{2,1,0:T(8,128)(2,1)S(1)}, u32[]{:S(2)}, u32[]{:S(2)}) async-start(bf16[16,56,128]{2,1,0:T(8,128)(2,1)} %bitcast.7), calls=%async_computation.1 | async-start | bytes 458752 | tf_op jit(solution)/shard_map/all_to_all | solution.py:297
  43.3 19.9 %copy-start.6 = (s32[8,1024]{1,0:T(8,128)S(1)}, s32[8,1024]{1,0:T(8,128)}, u32[]{:S(2)}) copy-start(s32[8,1024]{1,0:T(8,128)} %param.18) | copy-start | bytes 98308
  43.4 19.9 %collective-permute-start.4 = (bf16[256,512]{1,0:T(8,128)(2,1)S(1)}, bf16[256,512]{1,0:T(8,128)(2,1)S(1)}, u32[]{:S(2)}, u32[]{:S(2)}) collective-permute-start(bf16[256,512]{1,0:T(8,128)(2,1)S(1)} %shard_map.132.q0), channel_id=1, source_target_pairs={{0,384},{128,0},{256,128},{384,256},{1,385},{129,1},{257,129},{385... | collective-permute-start | bytes 786440 | tf_op jit(solution)/shard_map/ppermute | solution.py:301
  47.4 15.9 %collective-permute-start.3 = (bf16[256,512]{1,0:T(8,128)(2,1)S(1)}, bf16[256,512]{1,0:T(8,128)(2,1)S(1)}, u32[]{:S(2)}, u32[]{:S(2)}) collective-permute-start(bf16[256,512]{1,0:T(8,128)(2,1)S(1)} %shard_map.132.q0), channel_id=1, source_target_pairs={{0,256},{128,384},{256,0},{384,128},{1,257},{129,385},{257,1},{385... | collective-permute-start | bytes 786440 | tf_op jit(solution)/shard_map/ppermute | solution.py:301
  51.0 12.3 %collective-permute-start.2 = (bf16[256,512]{1,0:T(8,128)(2,1)S(1)}, bf16[256,512]{1,0:T(8,128)(2,1)S(1)}, u32[]{:S(2)}, u32[]{:S(2)}) collective-permute-start(bf16[256,512]{1,0:T(8,128)(2,1)S(1)} %shard_map.132.q0), channel_id=1, source_target_pairs={{0,128},{128,256},{256,384},{384,0},{1,129},{129,257},{257,385},{3... | collective-permute-start | bytes 786440 | tf_op jit(solution)/shard_map/ppermute | solution.py:301
  56.5 7.8 %collective-permute-start = (bf16[896,128]{1,0:T(8,128)(2,1)S(1)}, bf16[896,128]{1,0:T(8,128)(2,1)S(1)}, u32[]{:S(2)}, u32[]{:S(2)}) collective-permute-start(bf16[896,128]{1,0:T(8,128)(2,1)S(1)} %bitcast.18), channel_id=1, source_target_pairs={{0,64},{64,0},{1,65},{65,1},{2,66},{66,2},{3,67},{67,3},{4,68},{68... | collective-permute-start | bytes 688136 | tf_op jit(solution)/shard_map/ppermute | solution.py:305
  63.2 1.1 copy-start.4
  80.7 4.5 %collective-permute-start.8 = (bf16[896,128]{1,0:T(8,128)(2,1)S(1)}, bf16[896,128]{1,0:T(8,128)(2,1)S(1)}, u32[]{:S(2)}, u32[]{:S(2)}) collective-permute-start(bf16[896,128]{1,0:T(8,128)(2,1)S(1)} %get-tuple-element.30), channel_id=1, source_target_pairs={{0,64},{64,0},{1,65},{65,1},{2,66},{66,2},{3,67},{67,3},{4,68},{68... | collective-permute-start | bytes 688136 | tf_op jit(solution)/shard_map/ppermute | solution.py:305
  86.0 24.5 %all-to-all-start.3 = ((bf16[16,56,128]{2,1,0:T(8,128)(2,1)}), bf16[16,56,128]{2,1,0:T(8,128)(2,1)S(1)}, u32[]{:S(2)}, u32[]{:S(2)}) async-start(bf16[16,56,128]{2,1,0:T(8,128)(2,1)} %bitcast.10), calls=%async_computation.3 | async-start | bytes 458752 | tf_op jit(solution)/shard_map/all_to_all | solution.py:297
  97.2 25.9 %collective-permute-start.5 = (bf16[256,512]{1,0:T(8,128)(2,1)S(1)}, bf16[256,512]{1,0:T(8,128)(2,1)S(1)}, u32[]{:S(2)}, u32[]{:S(2)}) collective-permute-start(bf16[256,512]{1,0:T(8,128)(2,1)S(1)} %get-tuple-element.26), channel_id=1, source_target_pairs={{0,384},{128,0},{256,128},{384,256},{1,385},{129,1},{257,129},{385... | collective-permute-start | bytes 786440 | tf_op jit(solution)/shard_map/ppermute | solution.py:301
  99.2 23.9 %collective-permute-start.6 = (bf16[256,512]{1,0:T(8,128)(2,1)S(1)}, bf16[256,512]{1,0:T(8,128)(2,1)S(1)}, u32[]{:S(2)}, u32[]{:S(2)}) collective-permute-start(bf16[256,512]{1,0:T(8,128)(2,1)S(1)} %get-tuple-element.27), channel_id=1, source_target_pairs={{0,256},{128,384},{256,0},{384,128},{1,257},{129,385},{257,1},{385... | collective-permute-start | bytes 786440 | tf_op jit(solution)/shard_map/ppermute | solution.py:301
  104.0 19.1 %collective-permute-start.7 = (bf16[256,512]{1,0:T(8,128)(2,1)S(1)}, bf16[256,512]{1,0:T(8,128)(2,1)S(1)}, u32[]{:S(2)}, u32[]{:S(2)}) collective-permute-start(bf16[256,512]{1,0:T(8,128)(2,1)S(1)} %get-tuple-element.28), channel_id=1, source_target_pairs={{0,128},{128,256},{256,384},{384,0},{1,129},{129,257},{257,385},{3... | collective-permute-start | bytes 786440 | tf_op jit(solution)/shard_map/ppermute | solution.py:301
  111.9 18.3 %all-to-all-start.4 = ((bf16[32,32,128]{2,1,0:T(8,128)(2,1)}), bf16[32,32,128]{2,1,0:T(8,128)(2,1)S(1)}, u32[]{:S(2)}, u32[]{:S(2)}) async-start(bf16[32,32,128]{2,1,0:T(8,128)(2,1)} %bitcast.12), calls=%async_computation.4 | async-start | bytes 524288 | tf_op jit(solution)/shard_map/all_to_all | solution.py:297
  123.4 21.6 %collective-permute-start.9 = (bf16[256,512]{1,0:T(8,128)(2,1)S(1)}, bf16[256,512]{1,0:T(8,128)(2,1)S(1)}, u32[]{:S(2)}, u32[]{:S(2)}) collective-permute-start(bf16[256,512]{1,0:T(8,128)(2,1)S(1)} %shard_map.136), channel_id=1, source_target_pairs={{0,0},{8,136},{16,272},{24,408},{32,480},{40,360},{48,240},{56,120... | collective-permute-start | bytes 786440 | tf_op jit(solution)/shard_map/ppermute | solution.py:361
  131.2 13.7 %copy-start.1 = (bf16[1,128,512]{2,1,0:T(8,128)(2,1)S(1)}, bf16[1,128,512]{2,1,0:T(8,128)(2,1)}, u32[]{:S(2)}) copy-start(bf16[1,128,512]{2,1,0:T(8,128)(2,1)} %queries_ref.1) | copy-start | bytes 393220
  131.2 13.7 %copy-start.2 = (f32[128]{0:T(128)S(1)}, f32[128]{0:T(128)}, u32[]{:S(2)}) copy-start(f32[128]{0:T(128)} %param.13) | copy-start | bytes 1540

commit v7 on v6

--- a/solution.py
+++ b/solution.py
@@ -84,6 +84,11 @@
             out_ref[rows, lanes] = packed_ref[rows, lanes].astype(F32).T.astype(BF16)
 
 
+def owners_of(ids_ref, table_ref, *rest):
+    for c in range(N_C):
+        rest[-1][c] = jnp.where(ids_ref[0] >= 2, table_ref[c, 1], table_ref[c, 0])
+
+
 def pack_keys(keys_ref, values_ref, gain_ref, out_ref):
     gain = gain_ref[...]
     for n in range(2):
@@ -315,7 +320,6 @@
     ids = jnp.stack([y, core, z]).astype(jnp.int32)
     q_gain = q_gain.reshape(1, HD)
     k_gain = k_gain.reshape(1, HD)
-    owner = lax.dynamic_index_in_dim(tile_owner, y // 2, 1, keepdims=False)
     seen = visible.reshape(64, 128)
 
     (packed_kv,) = call(pack_keys, [shape((8, 4, 32, HD), BF16)], keys, values, k_gain)
@@ -327,6 +331,14 @@
         gate, queries, d_out, q_gain,
         smem=1, hbm=3, scratch=buffers, limit=60 << 20,
     )
+    owner = pl.pallas_call(
+        owners_of,
+        out_shape=shape((N_C,), jnp.int32),
+        in_specs=[pl.BlockSpec(memory_space=pltpu.SMEM)] * 2,
+        out_specs=pl.BlockSpec(memory_space=pltpu.SMEM),
+        cost_estimate=pl.CostEstimate(flops=HEAVY, bytes_accessed=64, transcendentals=0),
+        compiler_params=pltpu.CompilerParams(vmem_limit_bytes=1 << 20),
+    )(ids, tile_owner)
     (q0,) = call(turn, [shape((256, 512), BF16)], lax.ppermute(packed, PLANES, TO_PLANE), flops=HEAVY)
     got = exchange(packed_kv.reshape(32, 32, HD), ("y", "core", "x"))
     (chosen,) = call(choose_tiles, [shape((2, 8, BLOCK, HD), BF16)], owner, got.reshape(8, 4, 32, HD), smem=1)

time: 147 us -> 148 us (level)
  waiting for transfers between devices: 29.3 us -> 27 us
  blocking collectives: 7.47 us -> 9.65 us
    all_to_all x4, starting transfers between devices: 43 us -> 47.8 us  [exchange(): return lax.all_to_all(value, axes, split_axis=0, concat_axis=0, tiled=True)]
    ppermute x2, starting transfers between devices: 10.1 us -> 5.58 us  [swapped(): return lax.ppermute(value, 'core', [(0, 1), (1, 0)])]
    all_to_all x4, waiting for transfers between devices: 14.3 us -> 11.9 us  [exchange(): return lax.all_to_all(value, axes, split_axis=0, concat_axis=0, tiled=True)]
    all_to_all x1, blocking collectives: 7.47 us -> 9.65 us  [exchange(): return lax.all_to_all(value, axes, split_axis=0, concat_axis=0, tiled=True)]
    ppermute x1, starting transfers between devices: 8.48 us -> 6.64 us  [shards(): lax.ppermute(packed, PLANES, TO_PLANE)]
    unnamed x18 -> x19, local copies, waits for them, and re-layouts: 3.17 us -> 3.91 us
  transfers between devices with their start and end apart: 14 -> 14, of which waited for: 7 -> 6; matrix products, arithmetic and copies ran while one was open for 1% -> 1% of each run, Pallas kernels for 2% -> 4%
where the time goes in v7:
time: 148 us; the launch traced here: 147 us
  starting transfers between devices  86.9 us (59%)
  waiting for transfers between devices  27 us (18%)
  Pallas kernels  17 us (11%)
  blocking collectives  9.65 us (7%)
  local copies, waits for them, and re-layouts  3.92 us (3%)
  between operations  1.58 us (1%)
    all_to_all x4, starting transfers between devices, exchange(): return lax.all_to_all(value, axes, split_axis=0, concat_axis=0, tiled=True)  47.8 us
    ppermute x6, starting transfers between devices, rotated(): return lax.ppermute(value, 'y', [(i, (i + k) % Y) for i in range(Y)])  20.8 us
    pallas_call x10, Pallas kernels, call(): pl.pallas_call(kernel, out_shape=outs, in_specs=specs, out_specs=[pl.Bloc...  15.8 us
    ppermute x1, waiting for transfers between devices, shards(): summed = lax.ppermute(summed, PLANES, FROM_PLANE)  12.9 us
    all_to_all x4, waiting for transfers between devices, exchange(): return lax.all_to_all(value, axes, split_axis=0, concat_axis=0, tiled=True)  11.9 us
    all_to_all x1, blocking collectives, exchange(): return lax.all_to_all(value, axes, split_axis=0, concat_axis=0, tiled=True)  9.65 us
    ppermute x1, starting transfers between devices, shards(): lax.ppermute(packed, PLANES, TO_PLANE)  6.64 us
    ppermute x1, starting transfers between devices, shards(): summed = lax.ppermute(summed, PLANES, FROM_PLANE)  6.04 us
  transfers between devices with their start and end apart: 14, of which 6 were waited for; matrix products, arithmetic and copies ran while one was open for 1% of the time, Pallas kernels for 4%

profile of v7, /device:TPU:25, one launch (start us, length us, event | category | flops | bytes accessed | tf_op | source)
XLA Modules:
  0.0 146.8 jit_solution(4588916487152678181)
XLA Ops:
  3.2 9.6 %all-to-all-start = ((bf16[32,32,128]{2,1,0:T(8,128)(2,1)}), bf16[32,32,128]{2,1,0:T(8,128)(2,1)S(1)}, u32[]{:S(2)}, u32[]{:S(2)}) async-start(bf16[32,32,128]{2,1,0:T(8,128)(2,1)} %bitcast.4), calls=%async_computation | async-start | bytes 524288 | tf_op jit(solution)/shard_map/all_to_all | solution.py:302
  13.4 1.9 %shard_map.132 = bf16[256,512]{1,0:T(8,128)(2,1)} custom-call(f32[1]{0:T(128)S(6)} %copy.20.gate_ref, bf16[1,128,512]{2,1,0:T(8,128)(2,1)} %queries_ref.1, bf16[1,128,512]{2,1,0:T(8,128)(2,1)} %d_out_ref.1, f32[1,128]{1,0:T(1,128)} %bitcast.19), custom_call_target="tpu_custom_call" | custom-call | bytes 524804 | tf_op jit(solution)/shard_map/pallas_call | solution.py:40
  15.3 6.6 %collective-permute-start.1 = (bf16[256,512]{1,0:T(8,128)(2,1)}, bf16[256,512]{1,0:T(8,128)(2,1)S(1)}, u32[]{:S(2)}, u32[]{:S(2)}) collective-permute-start(bf16[256,512]{1,0:T(8,128)(2,1)} %shard_map.132), channel_id=1, source_target_pairs={{0,0},{136,8},{272,16},{408,24},{480,32},{360,40},{240,48},{120,56... | collective-permute-start | bytes 786440 | tf_op jit(solution)/shard_map/ppermute | solution.py:342
  22.8 1.2 shard_map.130.owner_ref
  24.0 1.3 shard_map.131
  25.3 10.1 %all-to-all-start.1 = ((bf16[16,56,128]{2,1,0:T(8,128)(2,1)}), bf16[16,56,128]{2,1,0:T(8,128)(2,1)S(1)}, u32[]{:S(2)}, u32[]{:S(2)}) async-start(bf16[16,56,128]{2,1,0:T(8,128)(2,1)} %bitcast.6), calls=%async_computation.1 | async-start | bytes 458752 | tf_op jit(solution)/shard_map/all_to_all | solution.py:302
  35.6 3.1 %collective-permute-start.4 = (bf16[256,512]{1,0:T(8,128)(2,1)S(1)}, bf16[256,512]{1,0:T(8,128)(2,1)S(1)}, u32[]{:S(2)}, u32[]{:S(2)}) collective-permute-start(bf16[256,512]{1,0:T(8,128)(2,1)S(1)} %shard_map.133.q0), channel_id=1, source_target_pairs={{0,384},{128,0},{256,128},{384,256},{1,385},{129,1},{257,129},{385... | collective-permute-start | bytes 786440 | tf_op jit(solution)/shard_map/ppermute | solution.py:306
  38.7 5.5 %collective-permute-start.3 = (bf16[256,512]{1,0:T(8,128)(2,1)S(1)}, bf16[256,512]{1,0:T(8,128)(2,1)S(1)}, u32[]{:S(2)}, u32[]{:S(2)}) collective-permute-start(bf16[256,512]{1,0:T(8,128)(2,1)S(1)} %shard_map.133.q0), channel_id=1, source_target_pairs={{0,256},{128,384},{256,0},{384,128},{1,257},{129,385},{257,1},{385... | collective-permute-start | bytes 786440 | tf_op jit(solution)/shard_map/ppermute | solution.py:306
  44.2 2.6 %collective-permute-start.2 = (bf16[256,512]{1,0:T(8,128)(2,1)S(1)}, bf16[256,512]{1,0:T(8,128)(2,1)S(1)}, u32[]{:S(2)}, u32[]{:S(2)}) collective-permute-start(bf16[256,512]{1,0:T(8,128)(2,1)S(1)} %shard_map.133.q0), channel_id=1, source_target_pairs={{0,128},{128,256},{256,384},{384,0},{1,129},{129,257},{257,385},{3... | collective-permute-start | bytes 786440 | tf_op jit(solution)/shard_map/ppermute | solution.py:306
  46.8 7.3 %all-to-all-done.1 = bf16[16,56,128]{2,1,0:T(8,128)(2,1)S(1)} async-done(((bf16[16,56,128]{2,1,0:T(8,128)(2,1)}), bf16[16,56,128]{2,1,0:T(8,128)(2,1)S(1)}, u32[]{:S(2)}, u32[]{:S(2)}) %all-to-all-start.1) | async-done | bytes 229408 | tf_op jit(solution)/shard_map/all_to_all | solution.py:302
  54.1 2.4 %collective-permute-start = (bf16[896,128]{1,0:T(8,128)(2,1)S(1)}, bf16[896,128]{1,0:T(8,128)(2,1)S(1)}, u32[]{:S(2)}, u32[]{:S(2)}) collective-permute-start(bf16[896,128]{1,0:T(8,128)(2,1)S(1)} %bitcast.16), channel_id=1, source_target_pairs={{0,64},{64,0},{1,65},{65,1},{2,66},{66,2},{3,67},{67,3},{4,68},{68... | collective-permute-start | bytes 688136 | tf_op jit(solution)/shard_map/ppermute | solution.py:310
  57.6 2.9 %shard_map.134 = (f32[4,128,512]{2,1,0:T(8,128)S(1)}, f32[4,4,2,512]{3,2,1,0:T(2,128)S(1)}) custom-call(s32[3]{0:T(128)S(1)} %pad_add_fusion.ids_ref, s32[8]{0:T(128)S(1)} %copy-done.3, s32[64,128]{1,0:T(8,128)S(1)} %reshape.42.visible_ref, bf16[896,128]{1,0:T(8,128)(2,1)S(1)} %bitcast.17, bf16[896,128]{1,0:T(8,128)(2,1)S(1)} %collective-permute-done.other_ref, ...), custom_call_target="tpu_custom_call" | custom-call | flops 939524096 | bytes 2654252 | tf_op jit(solution)/shard_map/pallas_call | solution.py:40
  60.5 9.6 %all_to_all.25.sums_ref = f32[4,4,2,512]{3,2,1,0:T(2,128)S(1)} all-to-all(f32[4,4,2,512]{3,2,1,0:T(2,128)S(1)} %get-tuple-element.24), channel_id=1, replica_groups=mesh['y'=4,'core'=2,'seq'=8,'zhi'=2,'x'=4] {'y'}, dimensions={0} | all-to-all | bytes 131072 | tf_op jit(solution)/shard_map/all_to_all | solution.py:302
  70.2 6.1 %shard_map.135 = (bf16[256,512]{1,0:T(8,128)(2,1)S(1)}, bf16[256,512]{1,0:T(8,128)(2,1)S(1)}, bf16[256,512]{1,0:T(8,128)(2,1)S(1)}, bf16[256,512]{1,0:T(8,128)(2...) custom-call(s32[3]{0:T(128)S(1)} %pad_add_fusion.ids_ref, s32[8]{0:T(128)S(1)} %copy-done.3, ...), custom_call_target="tpu_custom_call" | custom-call | flops 2348810240 | bytes 4390956 | tf_op jit(solution)/shard_map/pallas_call | solution.py:40
  76.3 3.2 %collective-permute-start.8 = (bf16[896,128]{1,0:T(8,128)(2,1)S(1)}, bf16[896,128]{1,0:T(8,128)(2,1)S(1)}, u32[]{:S(2)}, u32[]{:S(2)}) collective-permute-start(bf16[896,128]{1,0:T(8,128)(2,1)S(1)} %get-tuple-element.30), channel_id=1, source_target_pairs={{0,64},{64,0},{1,65},{65,1},{2,66},{66,2},{3,67},{67,3},{4,68},{68... | collective-permute-start | bytes 688136 | tf_op jit(solution)/shard_map/ppermute | solution.py:310
  81.3 16.9 %all-to-all-start.3 = ((bf16[16,56,128]{2,1,0:T(8,128)(2,1)}), bf16[16,56,128]{2,1,0:T(8,128)(2,1)S(1)}, u32[]{:S(2)}, u32[]{:S(2)}) async-start(bf16[16,56,128]{2,1,0:T(8,128)(2,1)} %bitcast.9), calls=%async_computation.3 | async-start | bytes 458752 | tf_op jit(solution)/shard_map/all_to_all | solution.py:302
  98.2 2.0 %collective-permute-start.5 = (bf16[256,512]{1,0:T(8,128)(2,1)S(1)}, bf16[256,512]{1,0:T(8,128)(2,1)S(1)}, u32[]{:S(2)}, u32[]{:S(2)}) collective-permute-start(bf16[256,512]{1,0:T(8,128)(2,1)S(1)} %get-tuple-element.26), channel_id=1, source_target_pairs={{0,384},{128,0},{256,128},{384,256},{1,385},{129,1},{257,129},{385... | collective-permute-start | bytes 786440 | tf_op jit(solution)/shard_map/ppermute | solution.py:306
  100.2 4.8 %collective-permute-start.6 = (bf16[256,512]{1,0:T(8,128)(2,1)S(1)}, bf16[256,512]{1,0:T(8,128)(2,1)S(1)}, u32[]{:S(2)}, u32[]{:S(2)}) collective-permute-start(bf16[256,512]{1,0:T(8,128)(2,1)S(1)} %get-tuple-element.27), channel_id=1, source_target_pairs={{0,256},{128,384},{256,0},{384,128},{1,257},{129,385},{257,1},{385... | collective-permute-start | bytes 786440 | tf_op jit(solution)/shard_map/ppermute | solution.py:306
  105.0 2.8 %collective-permute-start.7 = (bf16[256,512]{1,0:T(8,128)(2,1)S(1)}, bf16[256,512]{1,0:T(8,128)(2,1)S(1)}, u32[]{:S(2)}, u32[]{:S(2)}) collective-permute-start(bf16[256,512]{1,0:T(8,128)(2,1)S(1)} %get-tuple-element.28), channel_id=1, source_target_pairs={{0,128},{128,256},{256,384},{384,0},{1,129},{129,257},{257,385},{3... | collective-permute-start | bytes 786440 | tf_op jit(solution)/shard_map/ppermute | solution.py:306
  107.8 3.7 %all-to-all-done.3 = bf16[16,56,128]{2,1,0:T(8,128)(2,1)S(1)} async-done(((bf16[16,56,128]{2,1,0:T(8,128)(2,1)}), bf16[16,56,128]{2,1,0:T(8,128)(2,1)S(1)}, u32[]{:S(2)}, u32[]{:S(2)}) %all-to-all-start.3) | async-done | bytes 229408 | tf_op jit(solution)/shard_map/all_to_all | solution.py:302
  111.6 1.3 shard_map.136
  112.9 11.2 %all-to-all-start.4 = ((bf16[32,32,128]{2,1,0:T(8,128)(2,1)}), bf16[32,32,128]{2,1,0:T(8,128)(2,1)S(1)}, u32[]{:S(2)}, u32[]{:S(2)}) async-start(bf16[32,32,128]{2,1,0:T(8,128)(2,1)} %bitcast.11), calls=%async_computation.4 | async-start | bytes 524288 | tf_op jit(solution)/shard_map/all_to_all | solution.py:302
  124.4 6.0 %collective-permute-start.9 = (bf16[256,512]{1,0:T(8,128)(2,1)S(1)}, bf16[256,512]{1,0:T(8,128)(2,1)S(1)}, u32[]{:S(2)}, u32[]{:S(2)}) collective-permute-start(bf16[256,512]{1,0:T(8,128)(2,1)S(1)} %shard_map.137), channel_id=1, source_target_pairs={{0,0},{8,136},{16,272},{24,408},{32,480},{40,360},{48,240},{56,120... | collective-permute-start | bytes 786440 | tf_op jit(solution)/shard_map/ppermute | solution.py:373
  133.0 12.9 %collective-permute-done.9.got_ref = bf16[256,512]{1,0:T(8,128)(2,1)S(1)} collective-permute-done((bf16[256,512]{1,0:T(8,128)(2,1)S(1)}, bf16[256,512]{1,0:T(8,128)(2,1)S(1)}, u32[]{:S(2)}, u32[]{:S(2)}) %collective-permute-start.9) | collective-permute-done | bytes 262176 | tf_op jit(solution)/shard_map/ppermute | solution.py:373
  (38 shorter events, 10.1 us)
Async XLA Ops:
  0.6 1.0 copy-start.4
  1.6 0.7 copy-start.2
  3.2 20.8 %all-to-all-start = ((bf16[32,32,128]{2,1,0:T(8,128)(2,1)}), bf16[32,32,128]{2,1,0:T(8,128)(2,1)S(1)}, u32[]{:S(2)}, u32[]{:S(2)}) async-start(bf16[32,32,128]{2,1,0:T(8,128)(2,1)} %bitcast.4), calls=%async_computation | async-start | bytes 524288 | tf_op jit(solution)/shard_map/all_to_all | solution.py:302
  15.3 20.1 %collective-permute-start.1 = (bf16[256,512]{1,0:T(8,128)(2,1)}, bf16[256,512]{1,0:T(8,128)(2,1)S(1)}, u32[]{:S(2)}, u32[]{:S(2)}) collective-permute-start(bf16[256,512]{1,0:T(8,128)(2,1)} %shard_map.132), channel_id=1, source_target_pairs={{0,0},{136,8},{272,16},{408,24},{480,32},{360,40},{240,48},{120,56... | collective-permute-start | bytes 786440 | tf_op jit(solution)/shard_map/ppermute | solution.py:342
  22.0 0.7 copy-start.6
  25.3 28.8 %all-to-all-start.1 = ((bf16[16,56,128]{2,1,0:T(8,128)(2,1)}), bf16[16,56,128]{2,1,0:T(8,128)(2,1)S(1)}, u32[]{:S(2)}, u32[]{:S(2)}) async-start(bf16[16,56,128]{2,1,0:T(8,128)(2,1)} %bitcast.6), calls=%async_computation.1 | async-start | bytes 458752 | tf_op jit(solution)/shard_map/all_to_all | solution.py:302
  35.4 21.1 %copy-start.5 = (s32[8,1024]{1,0:T(8,128)S(1)}, s32[8,1024]{1,0:T(8,128)}, u32[]{:S(2)}) copy-start(s32[8,1024]{1,0:T(8,128)} %param.18) | copy-start | bytes 98308
  35.6 20.9 %collective-permute-start.4 = (bf16[256,512]{1,0:T(8,128)(2,1)S(1)}, bf16[256,512]{1,0:T(8,128)(2,1)S(1)}, u32[]{:S(2)}, u32[]{:S(2)}) collective-permute-start(bf16[256,512]{1,0:T(8,128)(2,1)S(1)} %shard_map.133.q0), channel_id=1, source_target_pairs={{0,384},{128,0},{256,128},{384,256},{1,385},{129,1},{257,129},{385... | collective-permute-start | bytes 786440 | tf_op jit(solution)/shard_map/ppermute | solution.py:306
  38.7 17.8 %collective-permute-start.3 = (bf16[256,512]{1,0:T(8,128)(2,1)S(1)}, bf16[256,512]{1,0:T(8,128)(2,1)S(1)}, u32[]{:S(2)}, u32[]{:S(2)}) collective-permute-start(bf16[256,512]{1,0:T(8,128)(2,1)S(1)} %shard_map.133.q0), channel_id=1, source_target_pairs={{0,256},{128,384},{256,0},{384,128},{1,257},{129,385},{257,1},{385... | collective-permute-start | bytes 786440 | tf_op jit(solution)/shard_map/ppermute | solution.py:306
  44.2 12.3 %collective-permute-start.2 = (bf16[256,512]{1,0:T(8,128)(2,1)S(1)}, bf16[256,512]{1,0:T(8,128)(2,1)S(1)}, u32[]{:S(2)}, u32[]{:S(2)}) collective-permute-start(bf16[256,512]{1,0:T(8,128)(2,1)S(1)} %shard_map.133.q0), channel_id=1, source_target_pairs={{0,128},{128,256},{256,384},{384,0},{1,129},{129,257},{257,385},{3... | collective-permute-start | bytes 786440 | tf_op jit(solution)/shard_map/ppermute | solution.py:306
  54.1 3.5 %copy-start.3 = (s32[8]{0:T(128)S(1)}, s32[8]{0:T(128)}, u32[]{:S(2)}) copy-start(s32[8]{0:T(128)} %count_ref.3) | copy-start | bytes 100
  54.1 3.5 %collective-permute-start = (bf16[896,128]{1,0:T(8,128)(2,1)S(1)}, bf16[896,128]{1,0:T(8,128)(2,1)S(1)}, u32[]{:S(2)}, u32[]{:S(2)}) collective-permute-start(bf16[896,128]{1,0:T(8,128)(2,1)S(1)} %bitcast.16), channel_id=1, source_target_pairs={{0,64},{64,0},{1,65},{65,1},{2,66},{66,2},{3,67},{67,3},{4,68},{68... | collective-permute-start | bytes 688136 | tf_op jit(solution)/shard_map/ppermute | solution.py:310
  76.3 4.3 %collective-permute-start.8 = (bf16[896,128]{1,0:T(8,128)(2,1)S(1)}, bf16[896,128]{1,0:T(8,128)(2,1)S(1)}, u32[]{:S(2)}, u32[]{:S(2)}) collective-permute-start(bf16[896,128]{1,0:T(8,128)(2,1)S(1)} %get-tuple-element.30), channel_id=1, source_target_pairs={{0,64},{64,0},{1,65},{65,1},{2,66},{66,2},{3,67},{67,3},{4,68},{68... | collective-permute-start | bytes 688136 | tf_op jit(solution)/shard_map/ppermute | solution.py:310
  81.3 30.3 %all-to-all-start.3 = ((bf16[16,56,128]{2,1,0:T(8,128)(2,1)}), bf16[16,56,128]{2,1,0:T(8,128)(2,1)S(1)}, u32[]{:S(2)}, u32[]{:S(2)}) async-start(bf16[16,56,128]{2,1,0:T(8,128)(2,1)} %bitcast.9), calls=%async_computation.3 | async-start | bytes 458752 | tf_op jit(solution)/shard_map/all_to_all | solution.py:302
  98.2 25.9 %collective-permute-start.5 = (bf16[256,512]{1,0:T(8,128)(2,1)S(1)}, bf16[256,512]{1,0:T(8,128)(2,1)S(1)}, u32[]{:S(2)}, u32[]{:S(2)}) collective-permute-start(bf16[256,512]{1,0:T(8,128)(2,1)S(1)} %get-tuple-element.26), channel_id=1, source_target_pairs={{0,384},{128,0},{256,128},{384,256},{1,385},{129,1},{257,129},{385... | collective-permute-start | bytes 786440 | tf_op jit(solution)/shard_map/ppermute | solution.py:306
  100.2 23.9 %collective-permute-start.6 = (bf16[256,512]{1,0:T(8,128)(2,1)S(1)}, bf16[256,512]{1,0:T(8,128)(2,1)S(1)}, u32[]{:S(2)}, u32[]{:S(2)}) collective-permute-start(bf16[256,512]{1,0:T(8,128)(2,1)S(1)} %get-tuple-element.27), channel_id=1, source_target_pairs={{0,256},{128,384},{256,0},{384,128},{1,257},{129,385},{257,1},{385... | collective-permute-start | bytes 786440 | tf_op jit(solution)/shard_map/ppermute | solution.py:306
  105.0 19.1 %collective-permute-start.7 = (bf16[256,512]{1,0:T(8,128)(2,1)S(1)}, bf16[256,512]{1,0:T(8,128)(2,1)S(1)}, u32[]{:S(2)}, u32[]{:S(2)}) collective-permute-start(bf16[256,512]{1,0:T(8,128)(2,1)S(1)} %get-tuple-element.28), channel_id=1, source_target_pairs={{0,128},{128,256},{256,384},{384,0},{1,129},{129,257},{257,385},{3... | collective-permute-start | bytes 786440 | tf_op jit(solution)/shard_map/ppermute | solution.py:306
  112.9 18.3 %all-to-all-start.4 = ((bf16[32,32,128]{2,1,0:T(8,128)(2,1)}), bf16[32,32,128]{2,1,0:T(8,128)(2,1)S(1)}, u32[]{:S(2)}, u32[]{:S(2)}) async-start(bf16[32,32,128]{2,1,0:T(8,128)(2,1)} %bitcast.11), calls=%async_computation.4 | async-start | bytes 524288 | tf_op jit(solution)/shard_map/all_to_all | solution.py:302
  124.4 21.6 %collective-permute-start.9 = (bf16[256,512]{1,0:T(8,128)(2,1)S(1)}, bf16[256,512]{1,0:T(8,128)(2,1)S(1)}, u32[]{:S(2)}, u32[]{:S(2)}) collective-permute-start(bf16[256,512]{1,0:T(8,128)(2,1)S(1)} %shard_map.137), channel_id=1, source_target_pairs={{0,0},{8,136},{16,272},{24,408},{32,480},{40,360},{48,240},{56,120... | collective-permute-start | bytes 786440 | tf_op jit(solution)/shard_map/ppermute | solution.py:373
  132.2 13.7 %copy-start = (bf16[1,128,512]{2,1,0:T(8,128)(2,1)S(1)}, bf16[1,128,512]{2,1,0:T(8,128)(2,1)}, u32[]{:S(2)}) copy-start(bf16[1,128,512]{2,1,0:T(8,128)(2,1)} %queries_ref.1) | copy-start | bytes 393220
  132.2 13.7 %copy-start.1 = (f32[128]{0:T(128)S(1)}, f32[128]{0:T(128)}, u32[]{:S(2)}) copy-start(f32[128]{0:T(128)} %param.13) | copy-start | bytes 1540

commit v8 on v7

--- a/solution.py
+++ b/solution.py
@@ -26,6 +26,8 @@
 SHIFT = (0, 4, 1, 3, 2, 6, 5, 7)
 BLOCK = 4 * STEP
 MID = 2 * Z * BLOCK
+ALL = 2 * MID
+BLOCKS = 2
 
 
 def dot(a, b):
@@ -149,7 +151,7 @@
 def seen_row(ids_ref, count_ref, visible_ref, j):
     y, core, z = ids_ref[0], ids_ref[1], ids_ref[2]
     conv = jnp.where(z < 4, 2 * z, 15 - 2 * z)
-    source = ((y - j) & 3) * 2 + core
+    source = ((y - 2 * j) & 3) * 2 + core
     shift = jnp.int32(0)
     for i in range(1, 8):
         shift = jnp.where(source == i, SHIFT[i], shift)
@@ -163,73 +165,68 @@
     return jnp.exp2(dot(keys_s[...], q_t) * SCALE_LOG2)
 
 
-def load_pair(ids_ref, mine_ref, other_ref, keys_s, values_s):
+def load_pair(ids_ref, mine, other, keys_s, values_s):
     core = ids_ref[1]
-
-    @pl.when(core == 0)
-    def _():
-        keys_s[...] = mine_ref[...]
-        values_s[...] = other_ref[...]
-
-    @pl.when(core != 0)
-    def _():
-        keys_s[...] = other_ref[...]
-        values_s[...] = mine_ref[...]
-
-    return row_mask(ids_ref[0] & 1, (MID, HD), 0)
-
-
-def forward(ids_ref, count_ref, visible_ref, mine_ref, other_ref, q0, q1, q2, q3, acc_ref, sums_ref, keys_s, values_s, turned_s, q_s):
-    ok = load_pair(ids_ref, mine_ref, other_ref, keys_s, values_s)
+    for i in range(2):
+        rows = slice(i * MID, (i + 1) * MID)
+
+        @pl.when(core == 0)
+        def _():
+            keys_s[rows, :] = mine[i][...]
+            values_s[rows, :] = other[i][...]
+
+        @pl.when(core != 0)
+        def _():
+            keys_s[rows, :] = other[i][...]
+            values_s[rows, :] = mine[i][...]
+
+    return all_rows(ids_ref, HD, 0)
+
+
+def all_rows(ids_ref, size, axis):
+    half = ids_ref[0] & 1
+    dims = (MID, size) if axis == 0 else (size, MID)
+    return jnp.concatenate([row_mask(half, dims, axis), row_mask(1 - half, dims, axis)], axis=axis)
+
+
+def forward(ids_ref, count_ref, visible_ref, mine0, mine1, other0, other1, q0, q1, acc_ref, sums_ref, keys_s, values_s, turned_s):
+    ok = load_pair(ids_ref, (mine0, mine1), (other0, other1), keys_s, values_s)
     keys_s[...] = (keys_s[...].astype(F32) * ok).astype(BF16)
     turned_s[0:HD, :] = (values_s[...].astype(F32) * ok).T.astype(BF16)
-    turned_s[HD:, :] = row_mask(ids_ref[0] & 1, (16, MID), 1).astype(BF16)
-    for j, q in enumerate((q0, q1, q2, q3)):
-        q_s[j] = q[...]
-
-    def block(j, carry):
-        q_t = q_s[j, 0:128, :]
-        o_t = q_s[j, 128:256, :].astype(F32)
+    turned_s[HD:, :] = all_rows(ids_ref, 16, 1).astype(BF16)
+    for j, q in enumerate((q0, q1)):
+        q_t = q[0:128, :]
+        o_t = q[128:256, :].astype(F32)
         acc = dot(turned_s[...], weights_of(keys_s, q_t).astype(BF16))
         acc = acc * seen_row(ids_ref, count_ref, visible_ref, j)
         both = jnp.concatenate([acc[HD : HD + 1], jnp.sum(acc[:HD] * o_t, axis=0, keepdims=True)], axis=0)
-        for to in range(Y):
-            sums_ref[to, j] = both
+        sums_ref[j] = both
         acc_ref[j] = acc[:HD]
-        return carry
-
-    lax.fori_loop(0, Y, block, 0, unroll=True)
-
-
-def all_sums(ids_ref, sums_ref, j):
-    y = ids_ref[0]
-    both = sums_ref[y, j]
-    for k in range(1, Y):
-        both = both + sums_ref[(y - k) & 3, (j - k) & 3]
+
+
+def all_sums(mine_ref, other_ref, j):
+    both = mine_ref[j] + other_ref[1 - j]
     total = both[0:1]
     safe = jnp.where(total > 0, total, 1.0)
     return 1.0 / safe, both[1:2] / safe
 
 
 def backward(
-    ids_ref, count_ref, visible_ref, mine_ref, other_ref, q0, q1, q2, q3, acc_ref, sums_ref,
-    r0, r1, r2, r3, keep_ref, send_ref, keys_s, values_s, turned_s, q_s, dk_s, dv_s,
+    ids_ref, count_ref, visible_ref, mine0, mine1, other0, other1, q0, q1, acc_ref, s0, s1,
+    r0, r1, keep_ref, send_ref, keys_s, values_s, turned_s, dk_s, dv_s,
 ):
-    ok = load_pair(ids_ref, mine_ref, other_ref, keys_s, values_s)
+    ok = load_pair(ids_ref, (mine0, mine1), (other0, other1), keys_s, values_s)
     masked = keys_s[...].astype(F32) * ok
     keys_s[...] = masked.astype(BF16)
     turned_s[...] = masked.T.astype(BF16)
-    dk_s[...] = jnp.zeros((MID, HD), F32)
-    dv_s[...] = jnp.zeros((MID, HD), F32)
-    for j, q in enumerate((q0, q1, q2, q3)):
-        q_s[j] = q[...]
-
-    def block(j, carry):
-        q_t = q_s[j, 0:128, :]
-        o_t = q_s[j, 128:256, :]
+    dk_s[...] = jnp.zeros((ALL, HD), F32)
+    dv_s[...] = jnp.zeros((ALL, HD), F32)
+    for j, (q, r) in enumerate(((q0, r0), (q1, r1))):
+        q_t = q[0:128, :]
+        o_t = q[128:256, :]
         q_rows = stacked(q_t)
         o_rows = stacked(o_t)
-        inverse, delta = all_sums(ids_ref, sums_ref, j)
+        inverse, delta = all_sums(s0, s1, j)
         acc = (acc_ref[j] * inverse).astype(BF16)
         inverse = inverse * seen_row(ids_ref, count_ref, visible_ref, j)
         prob = weights_of(keys_s, q_t) * inverse
@@ -237,12 +234,7 @@
         dk_s[...] += dot(d_score, q_rows)
         dv_s[...] += dot(prob.astype(BF16), o_rows)
         dq = dot(turned_s[...], d_score)
-        q_s[j] = jnp.concatenate([acc, (dq * SCALE).astype(BF16)], axis=0)
-        return carry
-
-    lax.fori_loop(0, Y, block, 0, unroll=2)
-    for j, r in enumerate((r0, r1, r2, r3)):
-        r[...] = q_s[j]
+        r[...] = jnp.concatenate([acc, (dq * SCALE).astype(BF16)], axis=0)
     core = ids_ref[1]
 
     @pl.when(core == 0)
@@ -256,9 +248,9 @@
         send_ref[...] = (dk_s[...] * (ok * SCALE)).astype(BF16)
 
 
-def sum_tokens(gate_ref, r0, r1, r2, r3, out_ref):
+def sum_tokens(gate_ref, r0, r1, out_ref):
     gate = gate_value(gate_ref)
-    both = r0[...].astype(F32) + r1[...].astype(F32) + r2[...].astype(F32) + r3[...].astype(F32)
+    both = r0[...].astype(F32) + r1[...].astype(F32)
     for g in range(4):
         lanes = slice(g * HD, (g + 1) * HD)
         out_ref[0:128, lanes] = (both[0:128, lanes].T * gate).astype(BF16)
@@ -304,6 +296,10 @@
 
 def rotated(value, k):
     return lax.ppermute(value, "y", [(i, (i + k) % Y) for i in range(Y)])
+
+
+def traded(value):
+    return lax.ppermute(value, "y", [(i, i ^ 1) for i in range(Y)])
 
 
 def swapped(value):
@@ -343,33 +339,33 @@
     got = exchange(packed_kv.reshape(32, 32, HD), ("y", "core", "x"))
     (chosen,) = call(choose_tiles, [shape((2, 8, BLOCK, HD), BF16)], owner, got.reshape(8, 4, 32, HD), smem=1)
     mine = exchange(chosen.reshape(16, BLOCK, HD), ("zhi", "seq")).reshape(MID, HD)
-    q1, q2, q3 = rotated(q0, 1), rotated(q0, 2), rotated(q0, 3)
-    other = swapped(mine)
-
-    pair = [pltpu.VMEM((MID, HD), BF16), pltpu.VMEM((MID, HD), BF16)]
-    tokens = pltpu.VMEM((Y, 256, 512), BF16)
-    gradients = [pltpu.VMEM((MID, HD), F32), pltpu.VMEM((MID, HD), F32)]
+    q1 = rotated(q0, 2)
+    mine, q1 = lax.optimization_barrier((mine, q1))
+    beside = traded(mine)
+    tiles = (mine, beside, swapped(mine), swapped(beside))
+
+    pair = [pltpu.VMEM((ALL, HD), BF16), pltpu.VMEM((ALL, HD), BF16)]
+    gradients = [pltpu.VMEM((ALL, HD), F32), pltpu.VMEM((ALL, HD), F32)]
     acc, sums = call(
         forward,
-        [shape((Y, HD, 512), F32), shape((Y, Y, 2, 512), F32)],
-        ids, tile_count, seen, mine, other, q0, q1, q2, q3,
-        smem=2, scratch=pair + [pltpu.VMEM((HD + 16, MID), BF16), tokens], flops=2 * 2 * 2048 * MID * HD, limit=32 << 20,
+        [shape((BLOCKS, HD, 512), F32), shape((BLOCKS, 2, 512), F32)],
+        ids, tile_count, seen, *tiles, q0, q1,
+        smem=2, scratch=pair + [pltpu.VMEM((HD + 16, ALL), BF16)], flops=2 * 2 * 1024 * ALL * HD, limit=32 << 20,
     )
-    sums = exchange(sums, "y")
-    r0, r1, r2, r3, keep, send = call(
+    r0, r1, keep, send = call(
         backward,
-        [shape((256, 512), BF16)] * 4 + [shape((MID, HD), F32), shape((MID, HD), BF16)],
-        ids, tile_count, seen, mine, other, q0, q1, q2, q3, acc, sums,
-        smem=2, scratch=pair + [pltpu.VMEM((HD, MID), BF16), tokens] + gradients, flops=5 * 2 * 2048 * MID * HD, limit=32 << 20,
+        [shape((256, 512), BF16)] * 2 + [shape((ALL, HD), F32), shape((ALL, HD), BF16)],
+        ids, tile_count, seen, *tiles, q0, q1, acc, sums, rotated(sums, 2),
+        smem=2, scratch=pair + [pltpu.VMEM((HD, ALL), BF16)] + gradients, flops=5 * 2 * 1024 * ALL * HD, limit=32 << 20,
     )
 
-    grads = (keep + swapped(send).astype(F32)).astype(BF16)
+    grads = keep + swapped(send).astype(F32)
+    grads = (grads[:MID] + traded(grads[MID:].astype(BF16)).astype(F32)).astype(BF16)
     back = exchange(grads.reshape(16, BLOCK, HD), ("zhi", "seq"))
-    r1, r2, r3 = rotated(r1, 3), rotated(r2, 2), rotated(r3, 1)
+    r1 = rotated(r1, 2)
     (placed,) = call(return_tiles, [shape((8, 4, 32, HD), BF16)], owner, back.reshape(2, 8, BLOCK, HD), smem=1)
     home = exchange(placed.reshape(32, 32, HD), ("y", "core", "x")).reshape(8, 4, 32, HD)
-    r1, r2, r3, placed = lax.optimization_barrier((r1, r2, r3, placed))
-    (summed,) = call(sum_tokens, [shape((256, 512), BF16)], gate, r0, r1, r2, r3, smem=1)
+    (summed,) = call(sum_tokens, [shape((256, 512), BF16)], gate, r0, r1, smem=1)
     summed = lax.ppermute(summed, PLANES, FROM_PLANE)
     d_keys, d_values = call(finish_keys, [shape(keys.shape, BF16), shape(values.shape, BF16)], keys, home, k_gain, flops=HEAVY)
     attended, d_queries = call(finish_queries, [shape(queries.shape, BF16)] * 2, queries, summed, q_gain)

time: 148 us -> 157 us (1.061)
  the two profiles are of different devices: /device:TPU:25 before, /device:TPU:1 now
where the time goes in v8:
time: 157 us; the launch traced here: 156 us
  starting transfers between devices  83.2 us (53%)
  waiting for transfers between devices  49.8 us (32%)
  Pallas kernels  17 us (11%)
  local copies, waits for them, and re-layouts  3.95 us (3%)
  between operations  1.59 us (1%)
    all_to_all x4, starting transfers between devices, exchange(): return lax.all_to_all(value, axes, split_axis=0, concat_axis=0, tiled=True)  42.2 us
    ppermute x3, waiting for transfers between devices, rotated(): return lax.ppermute(value, 'y', [(i, (i + k) % Y) for i in range(Y)])  17.9 us
    all_to_all x4, waiting for transfers between devices, exchange(): return lax.all_to_all(value, axes, split_axis=0, concat_axis=0, tiled=True)  17.6 us
    pallas_call x10, Pallas kernels, call(): pl.pallas_call(kernel, out_shape=outs, in_specs=specs, out_specs=[pl.Bloc...  15.8 us
    ppermute x1, starting transfers between devices, shards(): lax.ppermute(packed, PLANES, TO_PLANE)  12.4 us
    ppermute x2, waiting for transfers between devices, traded(): return lax.ppermute(value, 'y', [(i, i ^ 1) for i in range(Y)])  11.8 us
    ppermute x1, starting transfers between devices, shards(): summed = lax.ppermute(summed, PLANES, FROM_PLANE)  9.46 us
    ppermute x3, starting transfers between devices, swapped(): return lax.ppermute(value, 'core', [(0, 1), (1, 0)])  7.62 us
  transfers between devices with their start and end apart: 14, of which 9 were waited for; matrix products, arithmetic and copies ran while one was open for 0% of the time, Pallas kernels for 4%

profile of v8, /device:TPU:1, one launch (start us, length us, event | category | flops | bytes accessed | tf_op | source)
XLA Modules:
  0.0 156.5 jit_solution(13650138875115750616)
XLA Ops:
  3.2 10.4 %all-to-all-start = ((bf16[32,32,128]{2,1,0:T(8,128)(2,1)}), bf16[32,32,128]{2,1,0:T(8,128)(2,1)S(1)}, u32[]{:S(2)}, u32[]{:S(2)}) async-start(bf16[32,32,128]{2,1,0:T(8,128)(2,1)} %bitcast.4), calls=%async_computation | async-start | bytes 524288 | tf_op jit(solution)/shard_map/all_to_all | solution.py:294
  14.2 1.9 %shard_map.132 = bf16[256,512]{1,0:T(8,128)(2,1)} custom-call(f32[1]{0:T(128)S(6)} %copy.20.gate_ref, bf16[1,128,512]{2,1,0:T(8,128)(2,1)} %queries_ref.1, bf16[1,128,512]{2,1,0:T(8,128)(2,1)} %d_out_ref.1, f32[1,128]{1,0:T(1,128)} %bitcast.20), custom_call_target="tpu_custom_call" | custom-call | bytes 524804 | tf_op jit(solution)/shard_map/pallas_call | solution.py:42
  16.1 12.4 %collective-permute-start = (bf16[256,512]{1,0:T(8,128)(2,1)}, bf16[256,512]{1,0:T(8,128)(2,1)S(1)}, u32[]{:S(2)}, u32[]{:S(2)}) collective-permute-start(bf16[256,512]{1,0:T(8,128)(2,1)} %shard_map.132), channel_id=1, source_target_pairs={{0,0},{136,8},{272,16},{408,24},{480,32},{360,40},{240,48},{120,56... | collective-permute-start | bytes 786440 | tf_op jit(solution)/shard_map/ppermute | solution.py:338
  31.9 8.0 %all-to-all-start.1 = ((bf16[16,56,128]{2,1,0:T(8,128)(2,1)}), bf16[16,56,128]{2,1,0:T(8,128)(2,1)S(1)}, u32[]{:S(2)}, u32[]{:S(2)}) async-start(bf16[16,56,128]{2,1,0:T(8,128)(2,1)} %bitcast.6), calls=%async_computation.1 | async-start | bytes 458752 | tf_op jit(solution)/shard_map/all_to_all | solution.py:294
  40.1 1.9 %collective-permute-start.1 = (bf16[256,512]{1,0:T(8,128)(2,1)S(1)}, bf16[256,512]{1,0:T(8,128)(2,1)S(1)}, u32[]{:S(2)}, u32[]{:S(2)}) collective-permute-start(bf16[256,512]{1,0:T(8,128)(2,1)S(1)} %shard_map.133.q0), channel_id=1, source_target_pairs={{0,256},{128,384},{256,0},{384,128},{1,257},{129,385},{257,1},{385... | collective-permute-start | bytes 786440 | tf_op jit(solution)/shard_map/ppermute | solution.py:298
  42.0 7.9 %collective-permute-done.1.q1 = bf16[256,512]{1,0:T(8,128)(2,1)S(1)} collective-permute-done((bf16[256,512]{1,0:T(8,128)(2,1)S(1)}, bf16[256,512]{1,0:T(8,128)(2,1)S(1)}, u32[]{:S(2)}, u32[]{:S(2)}) %collective-permute-start.1) | collective-permute-done | bytes 262176 | tf_op jit(solution)/shard_map/ppermute | solution.py:298
  50.0 9.6 %all-to-all-done.1 = bf16[16,56,128]{2,1,0:T(8,128)(2,1)S(1)} async-done(((bf16[16,56,128]{2,1,0:T(8,128)(2,1)}), bf16[16,56,128]{2,1,0:T(8,128)(2,1)S(1)}, u32[]{:S(2)}, u32[]{:S(2)}) %all-to-all-start.1) | async-done | bytes 229408 | tf_op jit(solution)/shard_map/all_to_all | solution.py:294
  59.6 2.0 %collective-permute-start.2 = (bf16[896,128]{1,0:T(8,128)(2,1)S(1)}, bf16[896,128]{1,0:T(8,128)(2,1)S(1)}, u32[]{:S(2)}, u32[]{:S(2)}) collective-permute-start(bf16[896,128]{1,0:T(8,128)(2,1)S(1)} %bitcast.16), channel_id=1, source_target_pairs={{0,128},{128,0},{256,384},{384,256},{1,129},{129,1},{257,385},{385... | collective-permute-start | bytes 688136 | tf_op jit(solution)/shard_map/ppermute | solution.py:302
  61.6 1.9 %collective-permute-start.3 = (bf16[896,128]{1,0:T(8,128)(2,1)S(1)}, bf16[896,128]{1,0:T(8,128)(2,1)S(1)}, u32[]{:S(2)}, u32[]{:S(2)}) collective-permute-start(bf16[896,128]{1,0:T(8,128)(2,1)S(1)} %bitcast.17), channel_id=1, source_target_pairs={{0,64},{64,0},{1,65},{65,1},{2,66},{66,2},{3,67},{67,3},{4,68},{68... | collective-permute-start | bytes 688136 | tf_op jit(solution)/shard_map/ppermute | solution.py:306
  63.6 5.1 %collective-permute-done.2.mine1 = bf16[896,128]{1,0:T(8,128)(2,1)S(1)} collective-permute-done((bf16[896,128]{1,0:T(8,128)(2,1)S(1)}, bf16[896,128]{1,0:T(8,128)(2,1)S(1)}, u32[]{:S(2)}, u32[]{:S(2)}) %collective-permute-start.2) | collective-permute-done | bytes 229408 | tf_op jit(solution)/shard_map/ppermute | solution.py:302
  68.6 2.3 %collective-permute-start.4 = (bf16[896,128]{1,0:T(8,128)(2,1)S(1)}, bf16[896,128]{1,0:T(8,128)(2,1)S(1)}, u32[]{:S(2)}, u32[]{:S(2)}) collective-permute-start(bf16[896,128]{1,0:T(8,128)(2,1)S(1)} %collective-permute-done.2.mine1), channel_id=1, source_target_pairs={{0,64},{64,0},{1,65},{65,1},{2,66},{66,2},{3,67},{67,3},{4,68},{68... | collective-permute-start | bytes 688136 | tf_op jit(solution)/shard_map/ppermute | solution.py:306
  72.0 3.0 %shard_map.134 = (f32[2,128,512]{2,1,0:T(8,128)S(1)}, f32[2,2,512]{2,1,0:T(2,128)S(1)}) custom-call(s32[3]{0:T(128)S(1)} %pad_add_fusion.ids_ref, s32[8]{0:T(128)S(1)} %copy-done.3, s32[64,128]{1,0:T(8,128)S(1)} %reshape.42.visible_ref, bf16[896,128]{1,0:T(8,128)(2,1)S(1)} %bitcast.18, bf16[896,128]{1,0:T(8,128)(2,1)S(1)} %collective-permute-done.2.mine1, ...), custom_call_target="tpu_custom_call" | custom-call | flops 939524096 | bytes 2007084 | tf_op jit(solution)/shard_map/pallas_call | solution.py:42
  75.0 1.9 %collective-permute-start.5 = (f32[2,2,512]{2,1,0:T(2,128)S(1)}, f32[2,2,512]{2,1,0:T(2,128)S(1)}, u32[]{:S(2)}, u32[]{:S(2)}) collective-permute-start(f32[2,2,512]{2,1,0:T(2,128)S(1)} %get-tuple-element.23.s0), channel_id=1, source_target_pairs={{0,256},{128,384},{256,0},{384,128},{1,257},{129,385},{257,1},{385... | collective-permute-start | bytes 24584 | tf_op jit(solution)/shard_map/ppermute | solution.py:298
  76.9 4.0 %collective-permute-done.5.s1 = f32[2,2,512]{2,1,0:T(2,128)S(1)} collective-permute-done((f32[2,2,512]{2,1,0:T(2,128)S(1)}, f32[2,2,512]{2,1,0:T(2,128)S(1)}, u32[]{:S(2)}, u32[]{:S(2)}) %collective-permute-start.5) | collective-permute-done | bytes 8224 | tf_op jit(solution)/shard_map/ppermute | solution.py:298
  80.9 6.0 %shard_map.135 = (bf16[256,512]{1,0:T(8,128)(2,1)S(1)}, bf16[256,512]{1,0:T(8,128)(2,1)S(1)}, f32[1792,128]{1,0:T(8,128)S(1)}, bf16[1792,128]{1,0:T(8,128)(2,1)S(1)}) custom-call(s32[3]{0:T(128)S(1)} %pad_add_fusion.ids_ref, s32[8]{0:T(128)S(1)} %copy-done.3, s32[64,128]{1,0:T(8,128)S(1)} %reshape.42.visible_ref, bf16[896,128]{1,0:T(8,128)(2,1)S(1)} %bitcast.19, ...), custom_call_target="tpu_custom_call" | custom-call | flops 2348810240 | bytes 3915820 | tf_op jit(solution)/shard_map/pallas_call | solution.py:42
  86.9 3.4 %collective-permute-start.8 = (bf16[1792,128]{1,0:T(8,128)(2,1)S(1)}, bf16[1792,128]{1,0:T(8,128)(2,1)S(1)}, u32[]{:S(2)}, u32[]{:S(2)}) collective-permute-start(bf16[1792,128]{1,0:T(8,128)(2,1)S(1)} %get-tuple-element.29), channel_id=1, source_target_pairs={{0,64},{64,0},{1,65},{65,1},{2,66},{66,2},{3,67},{67,3},{4,68},{68... | collective-permute-start | bytes 1376264 | tf_op jit(solution)/shard_map/ppermute | solution.py:306
  91.9 1.9 %collective-permute-start.9 = (bf16[896,128]{1,0:T(8,128)(2,1)S(1)}, bf16[896,128]{1,0:T(8,128)(2,1)S(1)}, u32[]{:S(2)}, u32[]{:S(2)}) collective-permute-start(bf16[896,128]{1,0:T(8,128)(2,1)S(1)} %slice.15), channel_id=1, source_target_pairs={{0,128},{128,0},{256,384},{384,256},{1,129},{129,1},{257,385},{385... | collective-permute-start | bytes 688136 | tf_op jit(solution)/shard_map/ppermute | solution.py:302
  93.8 6.8 %collective-permute-done.9 = bf16[896,128]{1,0:T(8,128)(2,1)S(1)} collective-permute-done((bf16[896,128]{1,0:T(8,128)(2,1)S(1)}, bf16[896,128]{1,0:T(8,128)(2,1)S(1)}, u32[]{:S(2)}, u32[]{:S(2)}) %collective-permute-start.9) | collective-permute-done | bytes 229408 | tf_op jit(solution)/shard_map/ppermute | solution.py:302
  101.3 14.2 %all-to-all-start.2 = ((bf16[16,56,128]{2,1,0:T(8,128)(2,1)}), bf16[16,56,128]{2,1,0:T(8,128)(2,1)S(1)}, u32[]{:S(2)}, u32[]{:S(2)}) async-start(bf16[16,56,128]{2,1,0:T(8,128)(2,1)} %bitcast.9), calls=%async_computation.2 | async-start | bytes 458752 | tf_op jit(solution)/shard_map/all_to_all | solution.py:294
  115.5 3.7 %collective-permute-start.6 = (bf16[256,512]{1,0:T(8,128)(2,1)S(1)}, bf16[256,512]{1,0:T(8,128)(2,1)S(1)}, u32[]{:S(2)}, u32[]{:S(2)}) collective-permute-start(bf16[256,512]{1,0:T(8,128)(2,1)S(1)} %get-tuple-element.25), channel_id=1, source_target_pairs={{0,256},{128,384},{256,0},{384,128},{1,257},{129,385},{257,1},{385... | collective-permute-start | bytes 786440 | tf_op jit(solution)/shard_map/ppermute | solution.py:298
  119.3 6.0 %collective-permute-done.6.r1 = bf16[256,512]{1,0:T(8,128)(2,1)S(1)} collective-permute-done((bf16[256,512]{1,0:T(8,128)(2,1)S(1)}, bf16[256,512]{1,0:T(8,128)(2,1)S(1)}, u32[]{:S(2)}, u32[]{:S(2)}) %collective-permute-start.6) | collective-permute-done | bytes 262176 | tf_op jit(solution)/shard_map/ppermute | solution.py:298
  125.4 9.5 %collective-permute-start.7 = (bf16[256,512]{1,0:T(8,128)(2,1)S(1)}, bf16[256,512]{1,0:T(8,128)(2,1)S(1)}, u32[]{:S(2)}, u32[]{:S(2)}) collective-permute-start(bf16[256,512]{1,0:T(8,128)(2,1)S(1)} %shard_map.136), channel_id=1, source_target_pairs={{0,0},{8,136},{16,272},{24,408},{32,480},{40,360},{48,240},{56,120... | collective-permute-start | bytes 786440 | tf_op jit(solution)/shard_map/ppermute | solution.py:369
  136.3 9.6 %all-to-all-start.3 = ((bf16[32,32,128]{2,1,0:T(8,128)(2,1)}), bf16[32,32,128]{2,1,0:T(8,128)(2,1)S(1)}, u32[]{:S(2)}, u32[]{:S(2)}) async-start(bf16[32,32,128]{2,1,0:T(8,128)(2,1)} %bitcast.11), calls=%async_computation.3 | async-start | bytes 524288 | tf_op jit(solution)/shard_map/all_to_all | solution.py:294
  146.8 8.0 %all-to-all-done.3 = bf16[32,32,128]{2,1,0:T(8,128)(2,1)S(1)} async-done(((bf16[32,32,128]{2,1,0:T(8,128)(2,1)}), bf16[32,32,128]{2,1,0:T(8,128)(2,1)S(1)}, u32[]{:S(2)}, u32[]{:S(2)}) %all-to-all-start.3) | async-done | bytes 262176 | tf_op jit(solution)/shard_map/all_to_all | solution.py:294
  (39 shorter events, 13.4 us)
Async XLA Ops:
  0.6 1.0 copy-start.4
  1.6 0.7 copy-start.2
  3.2 27.4 %all-to-all-start = ((bf16[32,32,128]{2,1,0:T(8,128)(2,1)}), bf16[32,32,128]{2,1,0:T(8,128)(2,1)S(1)}, u32[]{:S(2)}, u32[]{:S(2)}) async-start(bf16[32,32,128]{2,1,0:T(8,128)(2,1)} %bitcast.4), calls=%async_computation | async-start | bytes 524288 | tf_op jit(solution)/shard_map/all_to_all | solution.py:294
  16.1 23.8 %collective-permute-start = (bf16[256,512]{1,0:T(8,128)(2,1)}, bf16[256,512]{1,0:T(8,128)(2,1)S(1)}, u32[]{:S(2)}, u32[]{:S(2)}) collective-permute-start(bf16[256,512]{1,0:T(8,128)(2,1)} %shard_map.132), channel_id=1, source_target_pairs={{0,0},{136,8},{272,16},{408,24},{480,32},{360,40},{240,48},{120,56... | collective-permute-start | bytes 786440 | tf_op jit(solution)/shard_map/ppermute | solution.py:338
  28.5 0.7 copy-start.6
  31.9 27.7 %all-to-all-start.1 = ((bf16[16,56,128]{2,1,0:T(8,128)(2,1)}), bf16[16,56,128]{2,1,0:T(8,128)(2,1)S(1)}, u32[]{:S(2)}, u32[]{:S(2)}) async-start(bf16[16,56,128]{2,1,0:T(8,128)(2,1)} %bitcast.6), calls=%async_computation.1 | async-start | bytes 458752 | tf_op jit(solution)/shard_map/all_to_all | solution.py:294
  39.9 31.0 %copy-start.5 = (s32[8,1024]{1,0:T(8,128)S(1)}, s32[8,1024]{1,0:T(8,128)}, u32[]{:S(2)}) copy-start(s32[8,1024]{1,0:T(8,128)} %param.18) | copy-start | bytes 98308
  40.1 9.9 %collective-permute-start.1 = (bf16[256,512]{1,0:T(8,128)(2,1)S(1)}, bf16[256,512]{1,0:T(8,128)(2,1)S(1)}, u32[]{:S(2)}, u32[]{:S(2)}) collective-permute-start(bf16[256,512]{1,0:T(8,128)(2,1)S(1)} %shard_map.133.q0), channel_id=1, source_target_pairs={{0,256},{128,384},{256,0},{384,128},{1,257},{129,385},{257,1},{385... | collective-permute-start | bytes 786440 | tf_op jit(solution)/shard_map/ppermute | solution.py:298
  59.6 12.4 %copy-start.3 = (s32[8]{0:T(128)S(1)}, s32[8]{0:T(128)}, u32[]{:S(2)}) copy-start(s32[8]{0:T(128)} %count_ref.3) | copy-start | bytes 100
  59.6 9.0 %collective-permute-start.2 = (bf16[896,128]{1,0:T(8,128)(2,1)S(1)}, bf16[896,128]{1,0:T(8,128)(2,1)S(1)}, u32[]{:S(2)}, u32[]{:S(2)}) collective-permute-start(bf16[896,128]{1,0:T(8,128)(2,1)S(1)} %bitcast.16), channel_id=1, source_target_pairs={{0,128},{128,0},{256,384},{384,256},{1,129},{129,1},{257,385},{385... | collective-permute-start | bytes 688136 | tf_op jit(solution)/shard_map/ppermute | solution.py:302
  61.6 9.3 %collective-permute-start.3 = (bf16[896,128]{1,0:T(8,128)(2,1)S(1)}, bf16[896,128]{1,0:T(8,128)(2,1)S(1)}, u32[]{:S(2)}, u32[]{:S(2)}) collective-permute-start(bf16[896,128]{1,0:T(8,128)(2,1)S(1)} %bitcast.17), channel_id=1, source_target_pairs={{0,64},{64,0},{1,65},{65,1},{2,66},{66,2},{3,67},{67,3},{4,68},{68... | collective-permute-start | bytes 688136 | tf_op jit(solution)/shard_map/ppermute | solution.py:306
  68.6 3.4 %collective-permute-start.4 = (bf16[896,128]{1,0:T(8,128)(2,1)S(1)}, bf16[896,128]{1,0:T(8,128)(2,1)S(1)}, u32[]{:S(2)}, u32[]{:S(2)}) collective-permute-start(bf16[896,128]{1,0:T(8,128)(2,1)S(1)} %collective-permute-done.2.mine1), channel_id=1, source_target_pairs={{0,64},{64,0},{1,65},{65,1},{2,66},{66,2},{3,67},{67,3},{4,68},{68... | collective-permute-start | bytes 688136 | tf_op jit(solution)/shard_map/ppermute | solution.py:306
  75.0 5.9 %collective-permute-start.5 = (f32[2,2,512]{2,1,0:T(2,128)S(1)}, f32[2,2,512]{2,1,0:T(2,128)S(1)}, u32[]{:S(2)}, u32[]{:S(2)}) collective-permute-start(f32[2,2,512]{2,1,0:T(2,128)S(1)} %get-tuple-element.23.s0), channel_id=1, source_target_pairs={{0,256},{128,384},{256,0},{384,128},{1,257},{129,385},{257,1},{385... | collective-permute-start | bytes 24584 | tf_op jit(solution)/shard_map/ppermute | solution.py:298
  86.9 4.8 %collective-permute-start.8 = (bf16[1792,128]{1,0:T(8,128)(2,1)S(1)}, bf16[1792,128]{1,0:T(8,128)(2,1)S(1)}, u32[]{:S(2)}, u32[]{:S(2)}) collective-permute-start(bf16[1792,128]{1,0:T(8,128)(2,1)S(1)} %get-tuple-element.29), channel_id=1, source_target_pairs={{0,64},{64,0},{1,65},{65,1},{2,66},{66,2},{3,67},{67,3},{4,68},{68... | collective-permute-start | bytes 1376264 | tf_op jit(solution)/shard_map/ppermute | solution.py:306
  91.9 8.7 %collective-permute-start.9 = (bf16[896,128]{1,0:T(8,128)(2,1)S(1)}, bf16[896,128]{1,0:T(8,128)(2,1)S(1)}, u32[]{:S(2)}, u32[]{:S(2)}) collective-permute-start(bf16[896,128]{1,0:T(8,128)(2,1)S(1)} %slice.15), channel_id=1, source_target_pairs={{0,128},{128,0},{256,384},{384,256},{1,129},{129,1},{257,385},{385... | collective-permute-start | bytes 688136 | tf_op jit(solution)/shard_map/ppermute | solution.py:302
  101.3 33.6 %all-to-all-start.2 = ((bf16[16,56,128]{2,1,0:T(8,128)(2,1)}), bf16[16,56,128]{2,1,0:T(8,128)(2,1)S(1)}, u32[]{:S(2)}, u32[]{:S(2)}) async-start(bf16[16,56,128]{2,1,0:T(8,128)(2,1)} %bitcast.9), calls=%async_computation.2 | async-start | bytes 458752 | tf_op jit(solution)/shard_map/all_to_all | solution.py:294
  115.5 9.7 %collective-permute-start.6 = (bf16[256,512]{1,0:T(8,128)(2,1)S(1)}, bf16[256,512]{1,0:T(8,128)(2,1)S(1)}, u32[]{:S(2)}, u32[]{:S(2)}) collective-permute-start(bf16[256,512]{1,0:T(8,128)(2,1)S(1)} %get-tuple-element.25), channel_id=1, source_target_pairs={{0,256},{128,384},{256,0},{384,128},{1,257},{129,385},{257,1},{385... | collective-permute-start | bytes 786440 | tf_op jit(solution)/shard_map/ppermute | solution.py:298
  125.4 20.4 %collective-permute-start.7 = (bf16[256,512]{1,0:T(8,128)(2,1)S(1)}, bf16[256,512]{1,0:T(8,128)(2,1)S(1)}, u32[]{:S(2)}, u32[]{:S(2)}) collective-permute-start(bf16[256,512]{1,0:T(8,128)(2,1)S(1)} %shard_map.136), channel_id=1, source_target_pairs={{0,0},{8,136},{16,272},{24,408},{32,480},{40,360},{48,240},{56,120... | collective-permute-start | bytes 786440 | tf_op jit(solution)/shard_map/ppermute | solution.py:369
  136.3 9.6 %copy-start = (bf16[1,128,512]{2,1,0:T(8,128)(2,1)S(1)}, bf16[1,128,512]{2,1,0:T(8,128)(2,1)}, u32[]{:S(2)}) copy-start(bf16[1,128,512]{2,1,0:T(8,128)(2,1)} %queries_ref.1) | copy-start | bytes 393220
  136.3 9.6 %copy-start.1 = (f32[128]{0:T(128)S(1)}, f32[128]{0:T(128)}, u32[]{:S(2)}) copy-start(f32[128]{0:T(128)} %param.13) | copy-start | bytes 1540
  136.3 18.5 %all-to-all-start.3 = ((bf16[32,32,128]{2,1,0:T(8,128)(2,1)}), bf16[32,32,128]{2,1,0:T(8,128)(2,1)S(1)}, u32[]{:S(2)}, u32[]{:S(2)}) async-start(bf16[32,32,128]{2,1,0:T(8,128)(2,1)} %bitcast.11), calls=%async_computation.3 | async-start | bytes 524288 | tf_op jit(solution)/shard_map/all_to_all | solution.py:294

commit v9 on v6

--- a/solution.py
+++ b/solution.py
@@ -318,8 +318,6 @@
     owner = lax.dynamic_index_in_dim(tile_owner, y // 2, 1, keepdims=False)
     seen = visible.reshape(64, 128)
 
-    (packed_kv,) = call(pack_keys, [shape((8, 4, 32, HD), BF16)], keys, values, k_gain)
-    packed_kv, queries = lax.optimization_barrier((packed_kv, queries))
     buffers = [pltpu.VMEM((128, 512), BF16), pltpu.VMEM((128, 512), BF16), pltpu.VMEM((1, HD), F32), pltpu.SemaphoreType.DMA((3,))]
     (packed,) = call(
         pack_queries,
@@ -327,7 +325,9 @@
         gate, queries, d_out, q_gain,
         smem=1, hbm=3, scratch=buffers, limit=60 << 20,
     )
+    packed, k_gain = lax.optimization_barrier((packed, k_gain))
     (q0,) = call(turn, [shape((256, 512), BF16)], lax.ppermute(packed, PLANES, TO_PLANE), flops=HEAVY)
+    (packed_kv,) = call(pack_keys, [shape((8, 4, 32, HD), BF16)], keys, values, k_gain)
     got = exchange(packed_kv.reshape(32, 32, HD), ("y", "core", "x"))
     (chosen,) = call(choose_tiles, [shape((2, 8, BLOCK, HD), BF16)], owner, got.reshape(8, 4, 32, HD), smem=1)
     mine = exchange(chosen.reshape(16, BLOCK, HD), ("zhi", "seq")).reshape(MID, HD)

time: 147 us -> 146 us (level)
    unnamed x18 -> x20, local copies, waits for them, and re-layouts: 3.17 us -> 2.21 us
  transfers between devices with their start and end apart: 14 -> 14, of which waited for: 7 -> 7; matrix products, arithmetic and copies ran while one was open for 1% -> 1% of each run, Pallas kernels for 2% -> 3%
where the time goes in v9:
time: 146 us; the launch traced here: 145 us
  starting transfers between devices  88.1 us (60%)
  waiting for transfers between devices  28.6 us (20%)
  Pallas kernels  15.8 us (11%)
  blocking collectives  7.71 us (5%)
  local copies, waits for them, and re-layouts  2.23 us (2%)
  between operations  1.62 us (1%)
    all_to_all x4, starting transfers between devices, exchange(): return lax.all_to_all(value, axes, split_axis=0, concat_axis=0, tiled=True)  42.5 us
    ppermute x6, starting transfers between devices, rotated(): return lax.ppermute(value, 'y', [(i, (i + k) % Y) for i in range(Y)])  20.7 us
    pallas_call x10, Pallas kernels, call(): pl.pallas_call(kernel, out_shape=outs, in_specs=specs, out_specs=[pl.Bloc...  15.8 us
    all_to_all x4, waiting for transfers between devices, exchange(): return lax.all_to_all(value, axes, split_axis=0, concat_axis=0, tiled=True)  13.6 us
    ppermute x1, waiting for transfers between devices, shards(): summed = lax.ppermute(summed, PLANES, FROM_PLANE)  12.9 us
    ppermute x2, starting transfers between devices, swapped(): return lax.ppermute(value, 'core', [(0, 1), (1, 0)])  10.2 us
    ppermute x1, starting transfers between devices, shards(): lax.ppermute(packed, PLANES, TO_PLANE)  8.61 us
    all_to_all x1, blocking collectives, exchange(): return lax.all_to_all(value, axes, split_axis=0, concat_axis=0, tiled=True)  7.71 us
  transfers between devices with their start and end apart: 14, of which 7 were waited for; matrix products, arithmetic and copies ran while one was open for 1% of the time, Pallas kernels for 3%

profile of v9, /device:TPU:25, one launch (start us, length us, event | category | flops | bytes accessed | tf_op | source)
XLA Modules:
  0.0 144.9 jit_solution(14954689172796027252)
XLA Ops:
  1.3 1.9 %shard_map.129 = bf16[256,512]{1,0:T(8,128)(2,1)} custom-call(f32[1]{0:T(128)S(6)} %copy.19.gate_ref, bf16[1,128,512]{2,1,0:T(8,128)(2,1)} %queries_ref.3, bf16[1,128,512]{2,1,0:T(8,128)(2,1)} %d_out_ref.1, f32[1,128]{1,0:T(1,128)} %bitcast.21), custom_call_target="tpu_custom_call" | custom-call | bytes 524804 | tf_op jit(solution)/shard_map/pallas_call | solution.py:40
  3.2 8.6 %collective-permute-start.1 = (bf16[256,512]{1,0:T(8,128)(2,1)}, bf16[256,512]{1,0:T(8,128)(2,1)S(1)}, u32[]{:S(2)}, u32[]{:S(2)}) collective-permute-start(bf16[256,512]{1,0:T(8,128)(2,1)} %shard_map.129), channel_id=1, source_target_pairs={{0,0},{136,8},{272,16},{408,24},{480,32},{360,40},{240,48},{120,56... | collective-permute-start | bytes 786440 | tf_op jit(solution)/shard_map/ppermute | solution.py:329
  13.4 10.5 %all-to-all-start = ((bf16[32,32,128]{2,1,0:T(8,128)(2,1)}), bf16[32,32,128]{2,1,0:T(8,128)(2,1)S(1)}, u32[]{:S(2)}, u32[]{:S(2)}) async-start(bf16[32,32,128]{2,1,0:T(8,128)(2,1)} %bitcast.6), calls=%async_computation | async-start | bytes 524288 | tf_op jit(solution)/shard_map/all_to_all | solution.py:297
  23.9 7.1 %all-to-all-done = bf16[32,32,128]{2,1,0:T(8,128)(2,1)S(1)} async-done(((bf16[32,32,128]{2,1,0:T(8,128)(2,1)}), bf16[32,32,128]{2,1,0:T(8,128)(2,1)S(1)}, u32[]{:S(2)}, u32[]{:S(2)}) %all-to-all-start) | async-done | bytes 262176 | tf_op jit(solution)/shard_map/all_to_all | solution.py:297
  31.0 1.3 shard_map.131
  32.3 9.3 %all-to-all-start.1 = ((bf16[16,56,128]{2,1,0:T(8,128)(2,1)}), bf16[16,56,128]{2,1,0:T(8,128)(2,1)S(1)}, u32[]{:S(2)}, u32[]{:S(2)}) async-start(bf16[16,56,128]{2,1,0:T(8,128)(2,1)} %bitcast.8), calls=%async_computation.1 | async-start | bytes 458752 | tf_op jit(solution)/shard_map/all_to_all | solution.py:297
  41.8 3.6 %collective-permute-start.4 = (bf16[256,512]{1,0:T(8,128)(2,1)S(1)}, bf16[256,512]{1,0:T(8,128)(2,1)S(1)}, u32[]{:S(2)}, u32[]{:S(2)}) collective-permute-start(bf16[256,512]{1,0:T(8,128)(2,1)S(1)} %shard_map.132.q0), channel_id=1, source_target_pairs={{0,384},{128,0},{256,128},{384,256},{1,385},{129,1},{257,129},{385... | collective-permute-start | bytes 786440 | tf_op jit(solution)/shard_map/ppermute | solution.py:301
  45.4 3.6 %collective-permute-start.3 = (bf16[256,512]{1,0:T(8,128)(2,1)S(1)}, bf16[256,512]{1,0:T(8,128)(2,1)S(1)}, u32[]{:S(2)}, u32[]{:S(2)}) collective-permute-start(bf16[256,512]{1,0:T(8,128)(2,1)S(1)} %shard_map.132.q0), channel_id=1, source_target_pairs={{0,256},{128,384},{256,0},{384,128},{1,257},{129,385},{257,1},{385... | collective-permute-start | bytes 786440 | tf_op jit(solution)/shard_map/ppermute | solution.py:301
  49.0 4.0 %collective-permute-start.2 = (bf16[256,512]{1,0:T(8,128)(2,1)S(1)}, bf16[256,512]{1,0:T(8,128)(2,1)S(1)}, u32[]{:S(2)}, u32[]{:S(2)}) collective-permute-start(bf16[256,512]{1,0:T(8,128)(2,1)S(1)} %shard_map.132.q0), channel_id=1, source_target_pairs={{0,128},{128,256},{256,384},{384,0},{1,129},{129,257},{257,385},{3... | collective-permute-start | bytes 786440 | tf_op jit(solution)/shard_map/ppermute | solution.py:301
  53.0 1.9 %all-to-all-done.1 = bf16[16,56,128]{2,1,0:T(8,128)(2,1)S(1)} async-done(((bf16[16,56,128]{2,1,0:T(8,128)(2,1)}), bf16[16,56,128]{2,1,0:T(8,128)(2,1)S(1)}, u32[]{:S(2)}, u32[]{:S(2)}) %all-to-all-start.1) | async-done | bytes 229408 | tf_op jit(solution)/shard_map/all_to_all | solution.py:297
  54.9 6.5 %collective-permute-start = (bf16[896,128]{1,0:T(8,128)(2,1)S(1)}, bf16[896,128]{1,0:T(8,128)(2,1)S(1)}, u32[]{:S(2)}, u32[]{:S(2)}) collective-permute-start(bf16[896,128]{1,0:T(8,128)(2,1)S(1)} %bitcast.18), channel_id=1, source_target_pairs={{0,64},{64,0},{1,65},{65,1},{2,66},{66,2},{3,67},{67,3},{4,68},{68... | collective-permute-start | bytes 688136 | tf_op jit(solution)/shard_map/ppermute | solution.py:305
  62.5 2.9 %shard_map.133 = (f32[4,128,512]{2,1,0:T(8,128)S(1)}, f32[4,4,2,512]{3,2,1,0:T(2,128)S(1)}) custom-call(s32[3]{0:T(128)S(1)} %pad_add_fusion.ids_ref, s32[8]{0:T(128)S(1)} %copy-done.4, s32[64,128]{1,0:T(8,128)S(1)} %reshape.41.visible_ref, bf16[896,128]{1,0:T(8,128)(2,1)S(1)} %bitcast.19, bf16[896,128]{1,0:T(8,128)(2,1)S(1)} %collective-permute-done.other_ref, ...), custom_call_target="tpu_custom_call" | custom-call | flops 939524096 | bytes 2654252 | tf_op jit(solution)/shard_map/pallas_call | solution.py:40
  65.4 7.7 %all_to_all.25.sums_ref = f32[4,4,2,512]{3,2,1,0:T(2,128)S(1)} all-to-all(f32[4,4,2,512]{3,2,1,0:T(2,128)S(1)} %get-tuple-element.24), channel_id=1, replica_groups=mesh['y'=4,'core'=2,'seq'=8,'zhi'=2,'x'=4] {'y'}, dimensions={0} | all-to-all | bytes 131072 | tf_op jit(solution)/shard_map/all_to_all | solution.py:297
  73.1 6.1 %shard_map.134 = (bf16[256,512]{1,0:T(8,128)(2,1)S(1)}, bf16[256,512]{1,0:T(8,128)(2,1)S(1)}, bf16[256,512]{1,0:T(8,128)(2,1)S(1)}, bf16[256,512]{1,0:T(8,128)(2...) custom-call(s32[3]{0:T(128)S(1)} %pad_add_fusion.ids_ref, s32[8]{0:T(128)S(1)} %copy-done.4, ...), custom_call_target="tpu_custom_call" | custom-call | flops 2348810240 | bytes 4390956 | tf_op jit(solution)/shard_map/pallas_call | solution.py:40
  79.2 3.7 %collective-permute-start.8 = (bf16[896,128]{1,0:T(8,128)(2,1)S(1)}, bf16[896,128]{1,0:T(8,128)(2,1)S(1)}, u32[]{:S(2)}, u32[]{:S(2)}) collective-permute-start(bf16[896,128]{1,0:T(8,128)(2,1)S(1)} %get-tuple-element.30), channel_id=1, source_target_pairs={{0,64},{64,0},{1,65},{65,1},{2,66},{66,2},{3,67},{67,3},{4,68},{68... | collective-permute-start | bytes 688136 | tf_op jit(solution)/shard_map/ppermute | solution.py:305
  84.8 11.5 %all-to-all-start.3 = ((bf16[16,56,128]{2,1,0:T(8,128)(2,1)}), bf16[16,56,128]{2,1,0:T(8,128)(2,1)S(1)}, u32[]{:S(2)}, u32[]{:S(2)}) async-start(bf16[16,56,128]{2,1,0:T(8,128)(2,1)} %bitcast.10), calls=%async_computation.3 | async-start | bytes 458752 | tf_op jit(solution)/shard_map/all_to_all | solution.py:297
  96.2 2.0 %collective-permute-start.5 = (bf16[256,512]{1,0:T(8,128)(2,1)S(1)}, bf16[256,512]{1,0:T(8,128)(2,1)S(1)}, u32[]{:S(2)}, u32[]{:S(2)}) collective-permute-start(bf16[256,512]{1,0:T(8,128)(2,1)S(1)} %get-tuple-element.26), channel_id=1, source_target_pairs={{0,384},{128,0},{256,128},{384,256},{1,385},{129,1},{257,129},{385... | collective-permute-start | bytes 786440 | tf_op jit(solution)/shard_map/ppermute | solution.py:301
  98.3 4.8 %collective-permute-start.6 = (bf16[256,512]{1,0:T(8,128)(2,1)S(1)}, bf16[256,512]{1,0:T(8,128)(2,1)S(1)}, u32[]{:S(2)}, u32[]{:S(2)}) collective-permute-start(bf16[256,512]{1,0:T(8,128)(2,1)S(1)} %get-tuple-element.27), channel_id=1, source_target_pairs={{0,256},{128,384},{256,0},{384,128},{1,257},{129,385},{257,1},{385... | collective-permute-start | bytes 786440 | tf_op jit(solution)/shard_map/ppermute | solution.py:301
  103.0 2.8 %collective-permute-start.7 = (bf16[256,512]{1,0:T(8,128)(2,1)S(1)}, bf16[256,512]{1,0:T(8,128)(2,1)S(1)}, u32[]{:S(2)}, u32[]{:S(2)}) collective-permute-start(bf16[256,512]{1,0:T(8,128)(2,1)S(1)} %get-tuple-element.28), channel_id=1, source_target_pairs={{0,128},{128,256},{256,384},{384,0},{1,129},{129,257},{257,385},{3... | collective-permute-start | bytes 786440 | tf_op jit(solution)/shard_map/ppermute | solution.py:301
  105.8 3.8 %all-to-all-done.3 = bf16[16,56,128]{2,1,0:T(8,128)(2,1)S(1)} async-done(((bf16[16,56,128]{2,1,0:T(8,128)(2,1)}), bf16[16,56,128]{2,1,0:T(8,128)(2,1)S(1)}, u32[]{:S(2)}, u32[]{:S(2)}) %all-to-all-start.3) | async-done | bytes 229408 | tf_op jit(solution)/shard_map/all_to_all | solution.py:297
  109.6 1.3 shard_map.135
  110.9 11.2 %all-to-all-start.4 = ((bf16[32,32,128]{2,1,0:T(8,128)(2,1)}), bf16[32,32,128]{2,1,0:T(8,128)(2,1)S(1)}, u32[]{:S(2)}, u32[]{:S(2)}) async-start(bf16[32,32,128]{2,1,0:T(8,128)(2,1)} %bitcast.12), calls=%async_computation.4 | async-start | bytes 524288 | tf_op jit(solution)/shard_map/all_to_all | solution.py:297
  122.4 6.0 %collective-permute-start.9 = (bf16[256,512]{1,0:T(8,128)(2,1)S(1)}, bf16[256,512]{1,0:T(8,128)(2,1)S(1)}, u32[]{:S(2)}, u32[]{:S(2)}) collective-permute-start(bf16[256,512]{1,0:T(8,128)(2,1)S(1)} %shard_map.136), channel_id=1, source_target_pairs={{0,0},{8,136},{16,272},{24,408},{32,480},{40,360},{48,240},{56,120... | collective-permute-start | bytes 786440 | tf_op jit(solution)/shard_map/ppermute | solution.py:361
  131.0 12.9 %collective-permute-done.9.got_ref = bf16[256,512]{1,0:T(8,128)(2,1)S(1)} collective-permute-done((bf16[256,512]{1,0:T(8,128)(2,1)S(1)}, bf16[256,512]{1,0:T(8,128)(2,1)S(1)}, u32[]{:S(2)}, u32[]{:S(2)}) %collective-permute-start.9) | collective-permute-done | bytes 262176 | tf_op jit(solution)/shard_map/ppermute | solution.py:361
  (39 shorter events, 8.3 us)
Async XLA Ops:
  0.6 23.3 %copy-start = (s32[8,2]{0,1:T(2,128)S(1)}, s32[8,2]{0,1:T(2,128)}, u32[]{:S(2)}) copy-start(s32[8,2]{0,1:T(2,128)} %param.17) | copy-start | bytes 196
  1.3 10.5 %copy-start.5 = (bf16[2,26,1024]{2,0,1:T(2,128)(2,1)S(1)}, bf16[2,26,1024]{2,0,1:T(2,128)(2,1)}, u32[]{:S(2)}) copy-start(bf16[2,26,1024]{2,0,1:T(2,128)(2,1)} %param.11) | copy-start | bytes 319492
  3.2 8.7 %copy-start.6 = (bf16[2,26,1024]{2,0,1:T(2,128)(2,1)S(1)}, bf16[2,26,1024]{2,0,1:T(2,128)(2,1)}, u32[]{:S(2)}) copy-start(bf16[2,26,1024]{2,0,1:T(2,128)(2,1)} %param.12) | copy-start | bytes 319492
  3.2 38.4 %collective-permute-start.1 = (bf16[256,512]{1,0:T(8,128)(2,1)}, bf16[256,512]{1,0:T(8,128)(2,1)S(1)}, u32[]{:S(2)}, u32[]{:S(2)}) collective-permute-start(bf16[256,512]{1,0:T(8,128)(2,1)} %shard_map.129), channel_id=1, source_target_pairs={{0,0},{136,8},{272,16},{408,24},{480,32},{360,40},{240,48},{120,56... | collective-permute-start | bytes 786440 | tf_op jit(solution)/shard_map/ppermute | solution.py:329
  11.9 0.7 copy-start.3
  13.4 17.6 %all-to-all-start = ((bf16[32,32,128]{2,1,0:T(8,128)(2,1)}), bf16[32,32,128]{2,1,0:T(8,128)(2,1)S(1)}, u32[]{:S(2)}, u32[]{:S(2)}) async-start(bf16[32,32,128]{2,1,0:T(8,128)(2,1)} %bitcast.6), calls=%async_computation | async-start | bytes 524288 | tf_op jit(solution)/shard_map/all_to_all | solution.py:297
  32.3 22.6 %all-to-all-start.1 = ((bf16[16,56,128]{2,1,0:T(8,128)(2,1)}), bf16[16,56,128]{2,1,0:T(8,128)(2,1)S(1)}, u32[]{:S(2)}, u32[]{:S(2)}) async-start(bf16[16,56,128]{2,1,0:T(8,128)(2,1)} %bitcast.8), calls=%async_computation.1 | async-start | bytes 458752 | tf_op jit(solution)/shard_map/all_to_all | solution.py:297
  41.7 19.8 %copy-start.7 = (s32[8,1024]{1,0:T(8,128)S(1)}, s32[8,1024]{1,0:T(8,128)}, u32[]{:S(2)}) copy-start(s32[8,1024]{1,0:T(8,128)} %param.18) | copy-start | bytes 98308
  41.8 19.7 %collective-permute-start.4 = (bf16[256,512]{1,0:T(8,128)(2,1)S(1)}, bf16[256,512]{1,0:T(8,128)(2,1)S(1)}, u32[]{:S(2)}, u32[]{:S(2)}) collective-permute-start(bf16[256,512]{1,0:T(8,128)(2,1)S(1)} %shard_map.132.q0), channel_id=1, source_target_pairs={{0,384},{128,0},{256,128},{384,256},{1,385},{129,1},{257,129},{385... | collective-permute-start | bytes 786440 | tf_op jit(solution)/shard_map/ppermute | solution.py:301
  45.4 16.2 %collective-permute-start.3 = (bf16[256,512]{1,0:T(8,128)(2,1)S(1)}, bf16[256,512]{1,0:T(8,128)(2,1)S(1)}, u32[]{:S(2)}, u32[]{:S(2)}) collective-permute-start(bf16[256,512]{1,0:T(8,128)(2,1)S(1)} %shard_map.132.q0), channel_id=1, source_target_pairs={{0,256},{128,384},{256,0},{384,128},{1,257},{129,385},{257,1},{385... | collective-permute-start | bytes 786440 | tf_op jit(solution)/shard_map/ppermute | solution.py:301
  49.0 12.6 %collective-permute-start.2 = (bf16[256,512]{1,0:T(8,128)(2,1)S(1)}, bf16[256,512]{1,0:T(8,128)(2,1)S(1)}, u32[]{:S(2)}, u32[]{:S(2)}) collective-permute-start(bf16[256,512]{1,0:T(8,128)(2,1)S(1)} %shard_map.132.q0), channel_id=1, source_target_pairs={{0,128},{128,256},{256,384},{384,0},{1,129},{129,257},{257,385},{3... | collective-permute-start | bytes 786440 | tf_op jit(solution)/shard_map/ppermute | solution.py:301
  54.9 7.6 %collective-permute-start = (bf16[896,128]{1,0:T(8,128)(2,1)S(1)}, bf16[896,128]{1,0:T(8,128)(2,1)S(1)}, u32[]{:S(2)}, u32[]{:S(2)}) collective-permute-start(bf16[896,128]{1,0:T(8,128)(2,1)S(1)} %bitcast.18), channel_id=1, source_target_pairs={{0,64},{64,0},{1,65},{65,1},{2,66},{66,2},{3,67},{67,3},{4,68},{68... | collective-permute-start | bytes 688136 | tf_op jit(solution)/shard_map/ppermute | solution.py:305
  61.4 1.1 copy-start.4
  79.2 4.8 %collective-permute-start.8 = (bf16[896,128]{1,0:T(8,128)(2,1)S(1)}, bf16[896,128]{1,0:T(8,128)(2,1)S(1)}, u32[]{:S(2)}, u32[]{:S(2)}) collective-permute-start(bf16[896,128]{1,0:T(8,128)(2,1)S(1)} %get-tuple-element.30), channel_id=1, source_target_pairs={{0,64},{64,0},{1,65},{65,1},{2,66},{66,2},{3,67},{67,3},{4,68},{68... | collective-permute-start | bytes 688136 | tf_op jit(solution)/shard_map/ppermute | solution.py:305
  84.8 24.8 %all-to-all-start.3 = ((bf16[16,56,128]{2,1,0:T(8,128)(2,1)}), bf16[16,56,128]{2,1,0:T(8,128)(2,1)S(1)}, u32[]{:S(2)}, u32[]{:S(2)}) async-start(bf16[16,56,128]{2,1,0:T(8,128)(2,1)} %bitcast.10), calls=%async_computation.3 | async-start | bytes 458752 | tf_op jit(solution)/shard_map/all_to_all | solution.py:297
  96.2 25.9 %collective-permute-start.5 = (bf16[256,512]{1,0:T(8,128)(2,1)S(1)}, bf16[256,512]{1,0:T(8,128)(2,1)S(1)}, u32[]{:S(2)}, u32[]{:S(2)}) collective-permute-start(bf16[256,512]{1,0:T(8,128)(2,1)S(1)} %get-tuple-element.26), channel_id=1, source_target_pairs={{0,384},{128,0},{256,128},{384,256},{1,385},{129,1},{257,129},{385... | collective-permute-start | bytes 786440 | tf_op jit(solution)/shard_map/ppermute | solution.py:301
  98.3 23.9 %collective-permute-start.6 = (bf16[256,512]{1,0:T(8,128)(2,1)S(1)}, bf16[256,512]{1,0:T(8,128)(2,1)S(1)}, u32[]{:S(2)}, u32[]{:S(2)}) collective-permute-start(bf16[256,512]{1,0:T(8,128)(2,1)S(1)} %get-tuple-element.27), channel_id=1, source_target_pairs={{0,256},{128,384},{256,0},{384,128},{1,257},{129,385},{257,1},{385... | collective-permute-start | bytes 786440 | tf_op jit(solution)/shard_map/ppermute | solution.py:301
  103.0 19.2 %collective-permute-start.7 = (bf16[256,512]{1,0:T(8,128)(2,1)S(1)}, bf16[256,512]{1,0:T(8,128)(2,1)S(1)}, u32[]{:S(2)}, u32[]{:S(2)}) collective-permute-start(bf16[256,512]{1,0:T(8,128)(2,1)S(1)} %get-tuple-element.28), channel_id=1, source_target_pairs={{0,128},{128,256},{256,384},{384,0},{1,129},{129,257},{257,385},{3... | collective-permute-start | bytes 786440 | tf_op jit(solution)/shard_map/ppermute | solution.py:301
  110.9 18.4 %all-to-all-start.4 = ((bf16[32,32,128]{2,1,0:T(8,128)(2,1)}), bf16[32,32,128]{2,1,0:T(8,128)(2,1)S(1)}, u32[]{:S(2)}, u32[]{:S(2)}) async-start(bf16[32,32,128]{2,1,0:T(8,128)(2,1)} %bitcast.12), calls=%async_computation.4 | async-start | bytes 524288 | tf_op jit(solution)/shard_map/all_to_all | solution.py:297
  122.4 21.6 %collective-permute-start.9 = (bf16[256,512]{1,0:T(8,128)(2,1)S(1)}, bf16[256,512]{1,0:T(8,128)(2,1)S(1)}, u32[]{:S(2)}, u32[]{:S(2)}) collective-permute-start(bf16[256,512]{1,0:T(8,128)(2,1)S(1)} %shard_map.136), channel_id=1, source_target_pairs={{0,0},{8,136},{16,272},{24,408},{32,480},{40,360},{48,240},{56,120... | collective-permute-start | bytes 786440 | tf_op jit(solution)/shard_map/ppermute | solution.py:361
  130.3 13.7 %copy-start.1 = (bf16[1,128,512]{2,1,0:T(8,128)(2,1)S(1)}, bf16[1,128,512]{2,1,0:T(8,128)(2,1)}, u32[]{:S(2)}) copy-start(bf16[1,128,512]{2,1,0:T(8,128)(2,1)} %queries_ref.3) | copy-start | bytes 393220
  130.3 13.7 %copy-start.2 = (f32[128]{0:T(128)S(1)}, f32[128]{0:T(128)}, u32[]{:S(2)}) copy-start(f32[128]{0:T(128)} %param.13) | copy-start | bytes 1540
